TPU v7x, 32 devices: a whole 2x2x4 slice. The times are simulated.
32 devices in a mesh: dp: 4 (over y, core), mp: 8 (over z, x).
Axes of the slice: x: 2, y: 2, z: 4, core: 2. Of those that a mesh axis runs over, the one named last changes fastest.
Arguments:
- tokens_in: bfloat16 [80, 256, 1024], P('dp', 'mp'), may hold values from -6 to 6
- segment_ids: int32 [80, 256], P('dp'), may hold values from 0 to 64, as said below
- attn_gain: float32 [1024], replicated, may hold values from 0.1 to 1.9
- attn_shift: float32 [1024], replicated, may hold values from -4 to 4
- qkv_weight: bfloat16 [1024, 3072], P(None, 'mp'), may hold values from -0.1875 to 0.1875
- qkv_bias: float32 [2, 1024], P(None, 'mp'), may hold values from -4 to 4
- out_weight: bfloat16 [1024, 1024], P('mp'), may hold values from -0.5 to 0.5
- out_bias: float32 [1024], replicated, may hold values from -4 to 4
- mlp_gain: float32 [1024], replicated, may hold values from 0.1 to 1.9
- mlp_shift: float32 [1024], replicated, may hold values from -4 to 4
- up_weight: bfloat16 [1024, 4096], P(None, 'mp'), may hold values from -0.1875 to 0.1875
- up_bias: float32 [4096], P('mp'), may hold values from -4 to 4
- down_weight: bfloat16 [4096, 1024], P('mp'), may hold values from -0.125 to 0.125
- down_bias: float32 [1024], replicated, may hold values from -4 to 4
- cotangent: bfloat16 [80, 256, 1024], P('dp', 'mp'), may hold values from -6 to 6
Outputs:
- block_out: bfloat16 [80, 256, 1024], P('dp', 'mp')
- tokens_grad: float32 [80, 256, 1024], P('dp', 'mp')
- attn_gain_grad: float32 [1024], replicated
- attn_shift_grad: float32 [1024], replicated
- qkv_weight_grad: float32 [1024, 3072], P(None, 'mp')
- qkv_bias_grad: float32 [2, 1024], P(None, 'mp')
- out_weight_grad: float32 [1024, 1024], P('mp')
- out_bias_grad: float32 [1024], replicated
- mlp_gain_grad: float32 [1024], replicated
- mlp_shift_grad: float32 [1024], replicated
- up_weight_grad: float32 [1024, 4096], P(None, 'mp')
- up_bias_grad: float32 [4096], P('mp')
- down_weight_grad: float32 [4096, 1024], P('mp')
- down_bias_grad: float32 [1024], replicated
Inputs may be any that keep to these rules, and one draw needn't show every extreme that they name: `segment_ids`: in each row, images occupy runs of positions with one nonzero id, the ids rising by one from 1 along the row; every row but the first ends in 1 to 32 padding positions with id 0. A token attends only to tokens with its own id.
All inputs are finite; a program needn't handle non-finite values.
Results may differ from a plain program's by a relative error of at most 0.012.
The roundings to bfloat16 on the way count: a program that leaves them out, or rounds other values in their place, can miss the bound.
Values may be sent and summed in bfloat16 or wider, within the bound.
A program may use at most 192 MiB of HBM per device.

v0:
```python
import math

import jax
import jax.numpy as jnp
from jax import lax
from jax.sharding import PartitionSpec as P

HEAD_DIM = 64


EPS = 1e-06
MASKED = -1000000000.0


def layer_norm(values, gain_vec, shift_vec):
    row_mean = jnp.mean(values, axis=-1, keepdims=True)
    centred = values - row_mean
    row_var = jnp.mean(centred * centred, axis=-1, keepdims=True)
    return centred * lax.rsqrt(row_var + EPS) * gain_vec + shift_vec


def gelu_exact(values):
    return jax.nn.gelu(values, approximate=False)


def attend_forward(blocks):
    query_vecs, key_vecs, value_vecs, labels = blocks
    raw_scores = jnp.einsum(
        "pqhe,pkhe->phqk", query_vecs, key_vecs, preferred_element_type=jnp.float32
    )
    allowed = (labels[:, :, None] == labels[:, None, :])[:, None]
    scores = jnp.where(allowed, raw_scores * HEAD_DIM ** (-0.5), MASKED)
    row_top = jnp.max(scores, axis=-1, keepdims=True)
    raised = jnp.exp(scores - row_top)
    row_total = jnp.sum(raised, axis=-1, keepdims=True)
    attn_probs = (raised / row_total).astype(jnp.bfloat16)
    mixed = jnp.einsum(
        "phqk,pkhe->pqhe", attn_probs, value_vecs, preferred_element_type=jnp.float32
    )
    return (mixed.astype(jnp.bfloat16), (row_top + jnp.log(row_total))[..., 0])


def attend_backward(blocks):
    query_vecs, key_vecs, value_vecs, labels, log_total, head_grad = blocks
    raw_scores = jnp.einsum(
        "pqhe,pkhe->phqk", query_vecs, key_vecs, preferred_element_type=jnp.float32
    )
    allowed = (labels[:, :, None] == labels[:, None, :])[:, None]
    scores = jnp.where(allowed, raw_scores * HEAD_DIM ** (-0.5), MASKED)
    probs_full = jnp.exp(scores - log_total[..., None])
    attn_probs = probs_full.astype(jnp.bfloat16)
    value_grad = jnp.einsum(
        "phqk,pqhe->pkhe", attn_probs, head_grad, preferred_element_type=jnp.float32
    )
    probs_grad = jnp.einsum(
        "pqhe,pkhe->phqk", head_grad, value_vecs, preferred_element_type=jnp.float32
    )
    row_delta = jnp.sum(probs_grad * probs_full, axis=-1, keepdims=True)
    score_grad = jnp.where(allowed, probs_full * (probs_grad - row_delta), 0.0) * HEAD_DIM ** (-0.5)
    score_low = score_grad.astype(jnp.bfloat16)
    query_grad = jnp.einsum(
        "phqk,pkhe->pqhe", score_low, key_vecs, preferred_element_type=jnp.float32
    )
    key_grad = jnp.einsum(
        "phqk,pqhe->pkhe", score_low, query_vecs, preferred_element_type=jnp.float32
    )
    return jnp.stack([query_grad, key_grad, value_grad], axis=3).astype(jnp.bfloat16)


def per_device(
    tokens_in,
    segment_ids,
    attn_gain,
    attn_shift,
    qkv_weight,
    qkv_bias,
    out_weight,
    out_bias,
    mlp_gain,
    mlp_shift,
    up_weight,
    up_bias,
    down_weight,
    down_bias,
    cotangent,
):
    rows_dev, tok_local, model_width = tokens_in.shape
    seq_len = segment_ids.shape[1]
    width_local = qkv_bias.shape[1]
    heads_local = width_local // HEAD_DIM
    tokens_all = rows_dev * seq_len
    per_block = math.gcd(rows_dev, max(1, 512 // seq_len))
    count_blocks = rows_dev // per_block
    tokens_f = tokens_in.astype(jnp.float32)
    normed_one = layer_norm(tokens_f, attn_gain, attn_shift).astype(jnp.bfloat16)
    gathered_one = lax.all_gather(normed_one, "mp", axis=1, tiled=True)
    flat_one = gathered_one.reshape(tokens_all, model_width)
    bias_parts = qkv_bias.reshape(2, heads_local, HEAD_DIM)
    zeros_bias = jnp.zeros((heads_local, HEAD_DIM), jnp.float32)
    full_bias = jnp.stack([bias_parts[0], zeros_bias, bias_parts[1]], axis=1).reshape(
        3 * width_local
    )
    projected = (
        jnp.dot(flat_one, qkv_weight, preferred_element_type=jnp.float32) + full_bias
    ).astype(jnp.bfloat16)
    head_split = projected.reshape(count_blocks, per_block, seq_len, heads_local, 3, HEAD_DIM)
    query_all = head_split[..., 0, :]
    key_all = head_split[..., 1, :]
    value_all = head_split[..., 2, :]
    label_blocks = segment_ids.reshape(count_blocks, per_block, seq_len)
    attn_out, log_total = lax.map(attend_forward, (query_all, key_all, value_all, label_blocks))
    attn_heads = attn_out.reshape(rows_dev, seq_len, width_local)
    attn_flat = attn_heads.reshape(tokens_all, width_local)
    partial_out = jnp.dot(attn_flat, out_weight, preferred_element_type=jnp.float32).reshape(
        rows_dev, seq_len, model_width
    )
    branch_one = lax.psum_scatter(partial_out, "mp", scatter_dimension=1, tiled=True)
    hidden = tokens_f + branch_one + out_bias
    normed_two = layer_norm(hidden, mlp_gain, mlp_shift).astype(jnp.bfloat16)
    gathered_two = lax.all_gather(normed_two, "mp", axis=1, tiled=True)
    flat_two = gathered_two.reshape(tokens_all, model_width)
    pre_act = jnp.dot(flat_two, up_weight, preferred_element_type=jnp.float32) + up_bias
    act_low = gelu_exact(pre_act).astype(jnp.bfloat16)
    partial_two = jnp.dot(act_low, down_weight, preferred_element_type=jnp.float32).reshape(
        rows_dev, seq_len, model_width
    )
    branch_two = lax.psum_scatter(
        partial_two.astype(jnp.bfloat16), "mp", scatter_dimension=1, tiled=True
    ).astype(jnp.float32)
    block_out = (hidden + branch_two + down_bias).astype(jnp.bfloat16)
    cot_f = cotangent.astype(jnp.float32)
    down_bias_part = jnp.sum(cot_f, axis=(0, 1))
    cot_all = lax.all_gather(cotangent, "mp", axis=1, tiled=True)
    cot_flat = cot_all.reshape(tokens_all, model_width)
    act_grad = jnp.einsum("td,fd->tf", cot_flat, down_weight, preferred_element_type=jnp.float32)
    down_weight_grad = jnp.einsum(
        "tf,td->fd", act_low, cot_flat, preferred_element_type=jnp.float32
    )
    gelu_pair = jax.vjp(gelu_exact, pre_act)
    pre_grad = gelu_pair[1](act_grad)[0].astype(jnp.bfloat16)
    up_bias_grad = jnp.sum(pre_grad, axis=0, dtype=jnp.float32)
    up_weight_grad = jnp.einsum("td,tf->df", flat_two, pre_grad, preferred_element_type=jnp.float32)
    normed_two_part = jnp.einsum(
        "tf,df->td", pre_grad, up_weight, preferred_element_type=jnp.float32
    ).reshape(rows_dev, seq_len, model_width)
    normed_two_grad = lax.psum_scatter(normed_two_part, "mp", scatter_dimension=1, tiled=True)
    norm_second = jax.vjp(layer_norm, hidden, mlp_gain, mlp_shift)
    hidden_part, mlp_gain_part, mlp_shift_part = norm_second[1](normed_two_grad)
    hidden_grad = cot_f + hidden_part
    out_bias_part = jnp.sum(hidden_grad, axis=(0, 1))
    branch_grad = hidden_grad.astype(jnp.bfloat16)
    branch_all = lax.all_gather(branch_grad, "mp", axis=1, tiled=True).reshape(
        tokens_all, model_width
    )
    head_grad_flat = jnp.einsum(
        "td,hd->th", branch_all, out_weight, preferred_element_type=jnp.float32
    ).astype(jnp.bfloat16)
    attn_grad_heads = head_grad_flat.reshape(rows_dev, seq_len, width_local)
    out_weight_grad = jnp.einsum(
        "th,td->hd", attn_flat, branch_all, preferred_element_type=jnp.float32
    )
    grad_blocks = attn_grad_heads.reshape(count_blocks, per_block, seq_len, heads_local, HEAD_DIM)
    qkv_grads = lax.map(
        attend_backward, (query_all, key_all, value_all, label_blocks, log_total, grad_blocks)
    )
    qkv_flat = qkv_grads.reshape(tokens_all, 3 * width_local)
    qkv_weight_grad = jnp.einsum(
        "td,tf->df", flat_one, qkv_flat, preferred_element_type=jnp.float32
    )
    bias_sums = jnp.sum(qkv_flat, axis=0, dtype=jnp.float32).reshape(heads_local, 3, HEAD_DIM)
    qkv_bias_grad = jnp.stack([bias_sums[:, 0], bias_sums[:, 2]], axis=0).reshape(2, width_local)
    normed_one_part = jnp.einsum(
        "tf,df->td", qkv_flat, qkv_weight, preferred_element_type=jnp.float32
    ).reshape(rows_dev, seq_len, model_width)
    normed_one_grad = lax.psum_scatter(normed_one_part, "mp", scatter_dimension=1, tiled=True)
    norm_first = jax.vjp(layer_norm, tokens_f, attn_gain, attn_shift)
    token_part, attn_gain_part, attn_shift_part = norm_first[1](normed_one_grad)
    tokens_grad = hidden_grad + token_part
    weight_grads = lax.psum(
        (
            qkv_weight_grad,
            qkv_bias_grad,
            out_weight_grad,
            up_weight_grad,
            up_bias_grad,
            down_weight_grad,
        ),
        "dp",
    )
    vector_grads = lax.psum(
        (
            attn_gain_part,
            attn_shift_part,
            out_bias_part,
            mlp_gain_part,
            mlp_shift_part,
            down_bias_part,
        ),
        ("dp", "mp"),
    )
    return (
        block_out,
        tokens_grad,
        vector_grads[0],
        vector_grads[1],
        weight_grads[0],
        weight_grads[1],
        weight_grads[2],
        vector_grads[2],
        vector_grads[3],
        vector_grads[4],
        weight_grads[3],
        weight_grads[4],
        weight_grads[5],
        vector_grads[5],
    )


def solution(mesh):
    in_specs = (
        P("dp", "mp", None),
        P("dp", None),
        P(),
        P(),
        P(None, "mp"),
        P(None, "mp"),
        P("mp", None),
        P(),
        P(),
        P(),
        P(None, "mp"),
        P("mp"),
        P("mp", None),
        P(),
        P("dp", "mp", None),
    )
    out_specs = (
        P("dp", "mp", None),
        P("dp", "mp", None),
        P(),
        P(),
        P(None, "mp"),
        P(None, "mp"),
        P("mp", None),
        P(),
        P(),
        P(),
        P(None, "mp"),
        P("mp"),
        P("mp", None),
        P(),
    )
    return jax.shard_map(
        per_device, mesh=mesh, in_specs=in_specs, out_specs=out_specs, check_vma=False
    )
```

profile of v0, /device:TPU:11, one launch (start us, length us, event | category | flops | bytes accessed | tf_op | source)
XLA Modules:
  0.0 2246.6 jit_solution(4501569503423795171)
XLA Ops:
  14.9 148.0 %all-gather.5.cloned.1.call-done = bf16[20,256,1024]{2,1,0:T(8,128)(2,1)} async-done(((bf16[20,32,1024]{2,1,0:T(8,128)(2,1)}), bf16[20,256,1024]{2,1,0:T(8,128)(2,1)}) %all-gather.5.cloned.1.call-update) | async-done | bytes 10485776 | tf_op jit(solution)/shard_map/all_gather | solution.py:96
  162.9 10.9 add_convert_fusion.1
  198.2 48.1 %while.22 = (s32[]{:T(128)}, bf16[10,2,256,2,64]{2,4,3,1,0:T(8,128)(2,1)}, f32[10,2,2,256]{3,2,1,0:T(2,128)}, bf16[10,2,256,2,64]{2,4,3,1,0:T(8,128)(2,1)}, s32[...) while((s32[]{:T(128)}, ...), condition=%wide.region_5.6_spmd, body=%wide.region_2.5_spmd.sunk | while | flops 69401600 | bytes 3973221 | solution.py:111
  246.3 9.9 fusion.85
  256.5 344.3 %reduce-scatter.5.cloned.1.call-done = f32[20,32,1024]{2,1,0:T(8,128)} async-done(((f32[20,256,1024]{2,1,0:T(8,128)}), f32[20,32,1024]{2,1,0:T(8,128)}) %reduce-scatter.5.cloned.1.call-update) | async-done | bytes 2621456 | tf_op jit(solution)/shard_map/reduce_scatter | solution.py:117
  606.7 148.1 %all-gather.7.cloned.1.call-done = bf16[20,256,1024]{2,1,0:T(8,128)(2,1)} async-done(((bf16[20,32,1024]{2,1,0:T(8,128)(2,1)}), bf16[20,256,1024]{2,1,0:T(8,128)(2,1)}) %all-gather.7.cloned.1.call-update) | async-done | bytes 10485776 | tf_op jit(solution)/shard_map/all_gather | solution.py:120
  754.8 12.3 fusion.96
  767.1 138.8 %all-gather.9.cloned.1.call-done = bf16[20,256,1024]{2,1,0:T(8,128)(2,1)} async-done(((bf16[20,32,1024]{2,1,0:T(8,128)(2,1)}), bf16[20,256,1024]{2,1,0:T(8,128)(2,1)}) %all-gather.9.cloned.1.call-update) | async-done | bytes 10485776 | tf_op jit(solution)/shard_map/all_gather | solution.py:133
  905.9 33.5 %convert_reduce_fusion = (f32[512]{0:T(512)}, bf16[5120,512]{1,0:T(8,128)(2,1)S(1)}, f32[5120,512]{1,0:T(8,128)}) fusion(f32[5120,512]{1,0:T(8,128)} %fusion.96, f32[512]{0:T(512)S(1)} %copy-done.34, bf16[5120,1024]{1,0:T(8,128)(2,1)} %bitcast.156, bf16[512,1024]{1,0:T(8,128)(2,1)S(1)} %copy-done), kind=kOutput, calls=%fused_computation.76 | convolution fusion | flops 5565316608 | bytes 37752832 | tf_op jit(solution)/shard_map/td,fd->tf/dot_general | solution.py:135
  939.4 10.0 fusion.97
  949.9 12.1 multiply_convert_fusion
  962.0 10.7 convolution_convert_fusion.4
  972.9 321.1 %reduce-scatter.9.cloned.1.call-done = f32[20,32,1024]{2,1,0:T(8,128)} async-done(((f32[20,256,1024]{2,1,0:T(8,128)}), f32[20,32,1024]{2,1,0:T(8,128)}) %reduce-scatter.9.cloned.1.call-update) | async-done | bytes 2621456 | tf_op jit(solution)/shard_map/reduce_scatter | solution.py:146
  1298.1 176.9 %reduce-scatter.7.cloned.1.call-done = bf16[20,32,1024]{2,1,0:T(8,128)(2,1)} async-done(((bf16[20,256,1024]{2,1,0:T(8,128)(2,1)}), bf16[20,32,1024]{2,1,0:T(8,128)(2,1)}) %reduce-scatter.7.cloned.1.call-update) | async-done | bytes 1310736 | tf_op jit(solution)/shard_map/reduce_scatter | solution.py:127
  1482.5 148.5 %all-gather.11.cloned.1.call-done = bf16[20,256,1024]{2,1,0:T(8,128)(2,1)} async-done(((bf16[20,32,1024]{2,1,0:T(8,128)(2,1)}), bf16[20,256,1024]{2,1,0:T(8,128)(2,1)}) %all-gather.11.cloned.1.call-update) | async-done | bytes 10485776 | tf_op jit(solution)/shard_map/all_gather | solution.py:152
  1646.1 104.9 %while.23 = (s32[]{:T(128)}, bf16[10,2,256,2,3,64]{2,5,3,1,4,0:T(8,128)(2,1)}, bf16[10,2,256,2,64]{2,4,3,1,0:T(8,128)(2,1)}, s32[10,2,256]{2,1,0:T(2,128)}, bf16...) while((s32[]{:T(128)}, ...), condition=%wide.region_15.16_spmd, body=%wide.region_13.15_spmd.sunk | while | flops 173476352 | bytes 14176381 | solution.py:163
  1753.5 10.0 fusion.81
  1770.8 11.7 fusion.100
  1782.6 11.0 fusion.101
  1799.5 9.8 reshape.232
  1816.1 9.9 fusion.98
  1835.5 272.0 %reduce-scatter.11.cloned.1.call-done = f32[20,32,1024]{2,1,0:T(8,128)} async-done(((f32[20,256,1024]{2,1,0:T(8,128)}), f32[20,32,1024]{2,1,0:T(8,128)}) %reduce-scatter.11.cloned.1.call-update) | async-done | bytes 2621456 | tf_op jit(solution)/shard_map/reduce_scatter | solution.py:175
  2114.7 41.9 %all-reduce = (f32[1024]{0:T(1024)}, f32[1024]{0:T(1024)}, f32[1024]{0:T(1024)}, f32[1024]{0:T(1024)}, f32[1024]{0:T(1024)}, /*index=5*/f32[1024]{0:T(1024)}) all-reduce(f32[1024]{0:T(1024)S(1)} %get-tuple-element.122, f32[1024]{0:T(1024)S(1)} %get-tuple-element.125, ...), channel_id=1, replica_groups=mesh['dp'=4,'mp'=8] {'dp','mp'}, use_global_device_ids=true, to_apply=%region_20.21 | all-reduce | flops 6144 | bytes 49152 | tf_op jit(solution)/shard_map/psum | solution.py:190
  2156.6 76.8 %all-reduce.5.cloned.1.call-done = (f32[1024,384]{1,0:T(8,128)}, f32[128,1024]{1,0:T(8,128)}, f32[1024,512]{1,0:T(8,128)}, f32[512,1024]{1,0:T(8,128)}) async-done(((f32[1024,384]{1,0:T(8,128)}, f32[128,1024]{1,0:T(8,128)}, f32[1024,512]{1,0:T(8,128)}, f32[512,1024]{1,0:T(8,128)}), (f32[1024,384]{1,0:T(8,128)}, f32[128,1024]{1,0:T(8,128)}, f32[1024,512]{1,0:T(8,128)}, ...) | async-done | bytes 6291472 | tf_op jit(solution)/shard_map/psum | solution.py:179
  (299 shorter events, 263.2 us)
Async XLA Ops:
  7.2 898.7 %copy-start = (bf16[512,1024]{1,0:T(8,128)(2,1)S(1)}, bf16[512,1024]{1,0:T(8,128)(2,1)}, u32[]{:S(2)}) copy-start(bf16[512,1024]{1,0:T(8,128)(2,1)} %param.31) | copy-start | bytes 3145732
  7.2 155.6 %all-gather.5.cloned.1.call-start = ((), (), s32[]{:S(2)}) async-start(), calls=%async_computation.4 | async-start | bytes 11796480 | tf_op jit(solution)/shard_map/all_gather | solution.py:96
  9.0 153.8 %copy-start.14 = (bf16[1024,384]{1,0:T(8,128)(2,1)S(1)}, bf16[1024,384]{1,0:T(8,128)(2,1)}, u32[]{:S(2)}) copy-start(bf16[1024,384]{1,0:T(8,128)(2,1)} %param.23) | copy-start | bytes 2359300
  13.8 587.1 %reduce-scatter.5.cloned.1.call-start = ((), (), s32[]{:S(2)}) async-start(), calls=%async_computation.5 | async-start | bytes 23592960 | tf_op jit(solution)/shard_map/reduce_scatter | solution.py:117
  198.2 48.1 %copy-start.19 = (bf16[128,1024]{1,0:T(8,128)(2,1)S(1)}, bf16[128,1024]{1,0:T(8,128)(2,1)}, u32[]{:S(2)}) copy-start(bf16[128,1024]{1,0:T(8,128)(2,1)} %param.25) | copy-start | bytes 786436
  256.2 344.6 %copy-start.30 = (f32[1024]{0:T(1024)S(1)}, f32[1024]{0:T(1024)}, u32[]{:S(2)}) copy-start(f32[1024]{0:T(1024)} %param.26) | copy-start | bytes 12292
  256.3 498.5 %all-gather.7.cloned.1.call-start = ((), (), s32[]{:S(2)}) async-start(), calls=%async_computation.6 | async-start | bytes 11796480 | tf_op jit(solution)/shard_map/all_gather | solution.py:120
  604.5 150.3 %copy-start.36 = (bf16[1024,512]{1,0:T(8,128)(2,1)S(1)}, bf16[1024,512]{1,0:T(8,128)(2,1)}, u32[]{:S(2)}) copy-start(bf16[1024,512]{1,0:T(8,128)(2,1)} %param.29) | copy-start | bytes 3145732
  606.1 299.8 %all-gather.9.cloned.1.call-start = ((), (), s32[]{:S(2)}) async-start(), calls=%async_computation.8 | async-start | bytes 11796480 | tf_op jit(solution)/shard_map/all_gather | solution.py:133
  606.7 687.3 %reduce-scatter.9.cloned.1.call-start = ((), (), s32[]{:S(2)}) async-start(), calls=%async_computation.9 | async-start | bytes 23592960 | tf_op jit(solution)/shard_map/reduce_scatter | solution.py:146
  754.8 151.1 %copy-start.34 = (f32[512]{0:T(512)S(1)}, f32[512]{0:T(512)}, u32[]{:S(2)}) copy-start(f32[512]{0:T(512)} %param.30) | copy-start | bytes 6148
  939.4 10.0 copy-start.37
  949.4 525.6 %reduce-scatter.7.cloned.1.call-start = ((), (), s32[]{:S(2)}) async-start(), calls=%async_computation.7 | async-start | bytes 11796480 | tf_op jit(solution)/shard_map/reduce_scatter | solution.py:127
  972.8 502.2 %copy-start.31 = (f32[1024]{0:T(1024)S(1)}, f32[1024]{0:T(1024)}, u32[]{:S(2)}) copy-start(f32[1024]{0:T(1024)} %param.32) | copy-start | bytes 12292
  972.8 658.2 %all-gather.11.cloned.1.call-start = ((), (), s32[]{:S(2)}) async-start(), calls=%async_computation.10 | async-start | bytes 11796480 | tf_op jit(solution)/shard_map/all_gather | solution.py:152
  1298.1 182.7 %copy-start.8 = (bf16[20,32,1024]{2,1,0:T(8,128)(2,1)S(1)}, bf16[20,32,1024]{2,1,0:T(8,128)(2,1)}, u32[]{:S(2)}) copy-start(bf16[20,32,1024]{2,1,0:T(8,128)(2,1)} %param.33) | copy-start | bytes 3932164
  1482.3 625.3 %reduce-scatter.11.cloned.1.call-start = ((), (), s32[]{:S(2)}) async-start(), calls=%async_computation.11 | async-start | bytes 23592960 | tf_op jit(solution)/shard_map/reduce_scatter | solution.py:175
  1763.6 469.9 %all-reduce.5.cloned.1.call-start = ((), (), s32[]{:S(2)}) async-start(), calls=%async_computation.12 | async-start | bytes 12582912 | tf_op jit(solution)/shard_map/psum | solution.py:179
  1782.6 11.0 copy-start.4
  1826.0 281.6 %copy-start.3 = (bf16[20,32,1024]{2,1,0:T(8,128)(2,1)S(1)}, bf16[20,32,1024]{2,1,0:T(8,128)(2,1)}, u32[]{:S(2)}) copy-start(bf16[20,32,1024]{2,1,0:T(8,128)(2,1)} %param.19) | copy-start | bytes 3932164
  1826.0 281.5 %copy-start.18 = (f32[20,32]{1,0:T(8,128)S(1)}, f32[20,32]{1,0:T(8,128)}, u32[]{:S(2)}) copy-start(f32[20,32]{1,0:T(8,128)} %copy-done.17) | copy-start | bytes 7684
  1826.0 281.5 %copy-start.25 = (f32[1024]{0:T(1024)S(1)}, f32[1024]{0:T(1024)}, u32[]{:S(2)}) copy-start(f32[1024]{0:T(1024)} %param.21) | copy-start | bytes 12292
  1828.9 281.3 %copy-start.23 = (f32[20,32]{1,0:T(8,128)S(1)}, f32[20,32]{1,0:T(8,128)}, u32[]{:S(2)}) copy-start(f32[20,32]{1,0:T(8,128)} %copy-done.22) | copy-start | bytes 7684
  1828.9 281.3 %copy-start.21 = (f32[20,32]{1,0:T(8,128)S(1)}, f32[20,32]{1,0:T(8,128)}, u32[]{:S(2)}) copy-start(f32[20,32]{1,0:T(8,128)} %copy-done.20) | copy-start | bytes 7684
  (23 other events, 65.7 us)
Sparse Core Ops, SparseCore 0:
  13.9 148.9 all-gather.4
  256.4 344.4 reduce-scatter.4
  606.2 148.5 all-gather.6
  756.8 149.0 all-gather.8
  949.6 344.3 reduce-scatter.8
  1297.4 177.5 reduce-scatter.6
  1482.4 148.5 all-gather.10
  1763.7 343.8 reduce-scatter.10
  2111.3 122.0 all-reduce.4
where the time goes:
time: 2260 us; the launch traced here: 2250 us
  waiting for transfers between devices  1780 us (79%)
  matrix products  248 us (11%)
  local copies, waits for them, and re-layouts  90.3 us (4%)
  other arithmetic  68 us (3%)
  blocking collectives  48.4 us (2%)
    reduce_scatter x1, waiting for transfers between devices, per_device(): lax.psum_scatter(partial_out, 'mp', scatter_dimension=1, tiled=True)  344 us
    reduce_scatter x1, waiting for transfers between devices, per_device(): lax.psum_scatter(normed_two_part, 'mp', scatter_dimension=1, tiled=True)  321 us
    reduce_scatter x1, waiting for transfers between devices, per_device(): lax.psum_scatter(normed_one_part, 'mp', scatter_dimension=1, tiled=True)  272 us
    reduce_scatter x1, waiting for transfers between devices, per_device(): lax.psum_scatter(partial_two.astype(jnp.bfloat16), 'mp', scatter_dimensio...  177 us
    all_gather x1, waiting for transfers between devices, per_device(): lax.all_gather(branch_grad, 'mp', axis=1, tiled=True)  148 us
    all_gather x1, waiting for transfers between devices, per_device(): gathered_two = lax.all_gather(normed_two, 'mp', axis=1, tiled=True)  148 us
    all_gather x1, waiting for transfers between devices, per_device(): gathered_one = lax.all_gather(normed_one, 'mp', axis=1, tiled=True)  148 us
    all_gather x1, waiting for transfers between devices, per_device(): cot_all = lax.all_gather(cotangent, 'mp', axis=1, tiled=True)  139 us
  transfers between devices with their start and end apart: 9, of which 9 were waited for; matrix products, arithmetic and copies ran while one was open for 5% of the time, Pallas kernels for 0%

commit v1 on v0

v1 whole, which is shorter than its diff:
```python
import functools
import math

import jax
import jax.numpy as jnp
from jax import lax
from jax.experimental import pallas as pl
from jax.experimental.pallas import tpu as pltpu
from jax.sharding import PartitionSpec as P

HEAD_DIM = 64
EPS = 1e-06
MASKED = -1000000000.0
MESH = pl.DeviceIdType.MESH
BF = jnp.bfloat16
F32 = jnp.float32


class Plan:
    def __init__(self, dp, mp, rows_dev, tok_local, seq_len):
        self.dp, self.mp, self.rows_dev, self.tok, self.seq = dp, mp, rows_dev, tok_local, seq_len
        self.share = mp // math.gcd(rows_dev, mp)
        self.group_rows = rows_dev * self.share // mp
        self.own = self.group_rows // self.share
        if self.share % 2 or dp % self.share or self.group_rows != self.own * self.share + 1:
            raise ValueError("unsupported sizes")
        self.groups = mp // self.share
        self.part = seq_len // self.share
        self.rows = self.own + 1

    def ring_at(self, p):
        p = lax.rem(p, self.mp)
        back = lax.div(p, self.mp // 2)
        return 2 * p * (1 - back) + (2 * self.mp - 1 - 2 * p) * back

    def place(self):
        d, m = lax.axis_index("dp"), lax.axis_index("mp")
        odd = lax.rem(m, 2)
        p = lax.div(m, 2) * (1 - odd) + (self.mp - 1 - lax.div(m, 2)) * odd
        return d, m, p


def greet(plan, d, m, others):
    barrier = pltpu.get_barrier_semaphore()
    base = lax.div(d, plan.share) * plan.share

    def one(i, carry):
        e, q = base + lax.div(i, plan.mp), lax.rem(i, plan.mp)

        @pl.when(jnp.logical_or(e != d, q != m))
        def _():
            pl.semaphore_signal(barrier, inc=1, device_id={"dp": e, "mp": q}, device_id_type=MESH)

        return carry

    lax.fori_loop(0, plan.share * plan.mp, one, 0)
    for e in others:
        pl.semaphore_signal(barrier, inc=1, device_id={"dp": e, "mp": m}, device_id_type=MESH)
    pl.semaphore_wait(barrier, plan.share * plan.mp - 1 + len(others))


def gather_kernel(
    plan, tok, cot, seg, w0, w1, w2, w3, tok3, cot3, seg3, g0, g1, g2, g3,
    tok_send, tok_recv, cot_send, cot_recv, seg_send, seg_recv, own_sem, ring_send, ring_recv, sib_send, sib_recv,
):
    n, share, own = plan.mp, plan.share, plan.own
    d, m, p = plan.place()
    core = lax.rem(d, 2)
    sib = d + 1 - 2 * core
    k = lax.rem(d, share)
    base = d - k
    shards, full = (w0, w1, w2, w3), (g0, g1, g2, g3)
    greet(plan, d, m, ())

    def quarter(w, c, way):
        rows = shards[w].shape[0] // 4
        return pl.ds(pl.multiple_of((2 * c + way) * rows, rows), rows)

    def ring(w, way, s, first=False):
        origin = m if first else plan.ring_at(p + n - s if way == 0 else p + s)
        rows = quarter(w, core, way)
        to = plan.ring_at(p + 1 if way == 0 else p + n - 1)
        return pltpu.make_async_remote_copy(
            shards[w].at[rows] if first else full[w].at[origin, rows],
            full[w].at[origin, rows],
            ring_send.at[w, way],
            ring_recv.at[w, way, s],
            device_id={"mp": to},
            device_id_type=MESH,
        )

    def sibling(w, way, s):
        origin = plan.ring_at(p + n - 1 - s if way == 0 else p + 1 + s)
        block = full[w].at[origin, quarter(w, core, way)]
        return pltpu.make_async_remote_copy(
            block, block, sib_send.at[w], sib_recv.at[w], device_id={"dp": sib}, device_id_type=MESH
        )

    for j in range(plan.groups):
        q = k * plan.groups + j
        for e in range(share):
            first = j * plan.group_rows
            at = lax.rem(m * plan.tok + plan.seq - e * plan.part, plan.seq)
            at = pl.multiple_of(at, plan.tok)
            mine = pl.ds(pl.multiple_of(m * plan.tok, plan.tok), plan.tok)
            pairs = (
                (tok.at[pl.ds(first + own * e, own)], tok3.at[pl.ds(0, own), mine], tok_send, tok_recv, 0),
                (tok.at[pl.ds(first + own * share, 1)], tok3.at[pl.ds(own, 1), pl.ds(at, plan.tok)], tok_send, tok_recv, 1),
                (cot.at[pl.ds(first + own * e, own)], cot3.at[pl.ds(0, own), mine], cot_send, cot_recv, 0),
                (cot.at[pl.ds(first + own * share, 1)], cot3.at[pl.ds(own, 1), pl.ds(at, plan.tok)], cot_send, cot_recv, 1),
            )
            here = jnp.logical_and(k == e, m == q)
            holds = lax.div(m * plan.tok, plan.part) == e
            for i, (src, dst, send, recv, what) in enumerate(pairs):
                wanted = holds if i == 3 else True

                @pl.when(jnp.logical_and(here, wanted))
                def _():
                    pltpu.make_async_copy(src, dst, recv.at[what]).start()

                @pl.when(jnp.logical_and(jnp.logical_not(here), wanted))
                def _():
                    pltpu.make_async_remote_copy(
                        src, dst, send.at[j, e, what], recv.at[what],
                        device_id={"dp": base + e, "mp": q}, device_id_type=MESH,
                    ).start()

    for e in range(share):

        @pl.when(k == e)
        def _():
            pltpu.make_async_copy(seg, seg3.at[e], seg_recv.at[e]).start()

        for f in range(share):

            @pl.when(jnp.logical_and(k == e, k != f))
            def _():
                pltpu.make_async_remote_copy(
                    seg, seg3.at[e], seg_send.at[f], seg_recv.at[e],
                    device_id={"dp": base + f}, device_id_type=MESH,
                ).start()

    for w in range(4):
        for way in range(2):
            ring(w, way, 0, True).start()
        pltpu.make_async_copy(shards[w], full[w].at[m], own_sem.at[w]).start()

    def step(s, carry):
        for w in range(4):
            for way in range(2):
                ring(w, way, s).wait_recv()

                @pl.when(s < n - 2)
                def _():
                    ring(w, way, s + 1).start()

                sibling(w, way, s).start()
        return carry

    lax.fori_loop(0, n - 1, step, 0)

    for w in range(4):
        rows = shards[w].shape[0]
        some = full[w].at[pl.ds(0, n - 1), pl.ds(0, rows // 2)]
        pltpu.make_async_copy(some, some, sib_recv.at[w]).wait()
        pltpu.make_async_copy(some, some, sib_send.at[w]).wait()
        some = full[w].at[pl.ds(0, n - 1), pl.ds(0, rows // 4)]
        for way in range(2):
            pltpu.make_async_copy(some, some, ring_send.at[w, way]).wait()
        pltpu.make_async_copy(shards[w], full[w].at[m], own_sem.at[w]).wait()
    for e in range(share):
        pltpu.make_async_copy(seg, seg3.at[e], seg_recv.at[e]).wait()

        @pl.when(k != e)
        def _():
            pltpu.make_async_copy(seg, seg3.at[e], seg_send.at[e]).wait()

    for ref, recv, extent in ((tok3, tok_recv, plan.seq), (cot3, cot_recv, plan.part)):
        some = ref.at[pl.ds(0, own)]
        pltpu.make_async_copy(some, some, recv.at[0]).wait()
        some = ref.at[pl.ds(own, 1), pl.ds(0, extent)]
        pltpu.make_async_copy(some, some, recv.at[1]).wait()
    for j in range(plan.groups):
        q = k * plan.groups + j
        for e in range(share):
            away = jnp.logical_not(jnp.logical_and(k == e, m == q))
            holds = lax.div(m * plan.tok, plan.part) == e
            for i, (ref, sem, rows) in enumerate(
                ((tok, tok_send, own), (tok, tok_send, 1), (cot, cot_send, own), (cot, cot_send, 1))
            ):
                some = ref.at[pl.ds(0, rows)]

                @pl.when(jnp.logical_and(away, holds if i == 3 else True))
                def _():
                    pltpu.make_async_copy(some, some, sem.at[j, e, i % 2]).wait()


def gather(plan, tokens_in, cotangent, segment_ids, weights):
    n, share = plan.mp, plan.share
    width = tokens_in.shape[2]
    any_space = pl.BlockSpec(memory_space=pl.ANY)
    dma = pltpu.SemaphoreType.DMA
    rows = jax.ShapeDtypeStruct((plan.rows, plan.seq, width), BF)
    return pl.pallas_call(
        functools.partial(gather_kernel, plan),
        out_shape=(
            rows,
            rows,
            jax.ShapeDtypeStruct((share,) + segment_ids.shape, jnp.int32),
            *[jax.ShapeDtypeStruct((n,) + w.shape, BF) for w in weights],
        ),
        in_specs=[any_space] * 7,
        out_specs=[any_space] * 7,
        scratch_shapes=[
            dma((plan.groups, share, 2)), dma((2,)), dma((plan.groups, share, 2)), dma((2,)),
            dma((share,)), dma((share,)), dma((4,)), dma((4, 2)), dma((4, 2, n - 1)), dma((4,)), dma((4,)),
        ],
        compiler_params=pltpu.CompilerParams(collective_id=0, has_side_effects=True),
        name="gather",
    )(tokens_in, cotangent, segment_ids, *weights)


def reduce_kernel(
    plan, n_y, x0, x1, x2, x3, out3, tg3, o0, o1, o2, o3, blk, tg,
    l0, l1, l2, l3, s0, s1, s2, s3, r0, r1, r2, r3, y0, y1, y2, y3, f0, f1, f2, f3, tgs, tgo, tgl,
    loc_sem, sib_send, sib_recv, ring_send, ring_recv, y_send, y_recv, fin_loc, fin_send, fin_recv,
    blk_send, blk_recv, tg_send, tg_recv, tgs_send, tgs_recv, tgl_sem,
):
    n, share, own, part = plan.mp, plan.share, plan.own, plan.part
    d, m, p = plan.place()
    core, yi = lax.rem(d, 2), lax.div(d, 2)
    sib = d + 1 - 2 * core
    k = lax.rem(d, share)
    base = d - k
    grads, outs = (x0, x1, x2, x3), (o0, o1, o2, o3)
    loc, sbl, slot = (l0, l1, l2, l3), (s0, s1, s2, s3), (r0, r1, r2, r3)
    ysl, fin = (y0, y1, y2, y3), (f0, f1, f2, f3)
    per_block = plan.share // 2
    block = lax.div(d, share)
    others = [lax.rem(yi + i, n_y) * 2 + core for i in range(1, n_y)]
    greet_all(plan, n_y, d, m)

    def quarter(w):
        return grads[w].shape[1] // 4

    def target(way, s):
        return plan.ring_at(p + n - 1 - s if way == 0 else p + 1 + s)

    def half_rows(w, way):
        return pl.ds(way * quarter(w), quarter(w))

    def full_rows(w, c, way):
        return pl.ds(pl.multiple_of((2 * c + way) * quarter(w), quarter(w)), quarter(w))

    def load(w, way, s):
        t = target(way, s)
        return pltpu.make_async_copy(
            grads[w].at[t, full_rows(w, core, way)], loc[w].at[t, half_rows(w, way)], loc_sem.at[w, way, s]
        )

    def give(w, way, s):
        t = target(way, s)
        return pltpu.make_async_remote_copy(
            grads[w].at[t, full_rows(w, 1 - core, way)], sbl[w].at[t, half_rows(w, way)],
            sib_send.at[w], sib_recv.at[w, way, s], device_id={"dp": sib}, device_id_type=MESH,
        )

    def hop(w, way, s):
        return pltpu.make_async_remote_copy(
            loc[w].at[target(way, s), half_rows(w, way)], slot[w].at[way, s], ring_send.at[w, way],
            ring_recv.at[w, way, s],
            device_id={"mp": plan.ring_at(p + 1 if way == 0 else p + n - 1)}, device_id_type=MESH,
        )

    for i in range(share):
        src = tg3.at[own, pl.ds(i * part, part)]
        if i == 0:
            pltpu.make_async_copy(src, tgs.at[0], tgl_sem.at[0]).start()
        else:
            pltpu.make_async_remote_copy(
                src, tgs.at[share - i], tgs_send.at[i], tgs_recv.at[share - i],
                device_id={"dp": base + lax.rem(k + i, share)}, device_id_type=MESH,
            ).start()

    j = lax.rem(m, plan.groups)
    home = base + lax.div(m, plan.groups)

    def send_rows(src3, shared, dst, send, recv, start):
        for q in range(n):
            toks = pl.ds(q * plan.tok, plan.tok)
            at = lax.rem(q * plan.tok, part)
            here = jnp.logical_and(home == d, m == q)
            first = j * plan.group_rows
            holds = (q * plan.tok) // part == k
            for what, (src, to, wanted) in enumerate(
                (
                    (src3.at[pl.ds(0, own), toks], dst.at[pl.ds(first + own * k, own)], True),
                    (shared.at[pl.ds(at, plan.tok)], dst.at[first + own * share], holds),
                )
            ):
                if not start[what]:
                    continue

                @pl.when(jnp.logical_and(here, wanted))
                def _():
                    pltpu.make_async_copy(src, to, recv.at[0]).start()

                @pl.when(jnp.logical_and(jnp.logical_not(here), wanted))
                def _():
                    pltpu.make_async_remote_copy(
                        src, to, send.at[q, what], recv.at[0], device_id={"dp": home, "mp": q}, device_id_type=MESH
                    ).start()

    def wait_rows(dst, send, recv):
        pltpu.make_async_copy(dst, dst, recv.at[0]).wait()
        for q in range(n):
            away = jnp.logical_not(jnp.logical_and(home == d, m == q))
            holds = (q * plan.tok) // part == k
            for what, rows in enumerate((own, 1)):
                some = dst.at[pl.ds(0, rows)]

                @pl.when(jnp.logical_and(away, True if what == 0 else holds))
                def _():
                    pltpu.make_async_copy(some, some, send.at[q, what]).wait()

    def begin(s, carry):
        for w in range(4):
            for way in range(2):
                load(w, way, s).start()
                give(w, way, s).start()
        return carry

    lax.fori_loop(0, n, begin, 0)
    send_rows(out3, out3.at[own], blk, blk_send, blk_recv, (True, True))
    send_rows(tg3, tgo, tg, tg_send, tg_recv, (True, False))

    def add(w, way, s, more, dst):
        t = target(way, s)
        rows = quarter(w)
        size = 16 if rows % 32 else 32

        @pl.loop(0, rows // size)
        def _(i):
            inner = pl.ds(pl.multiple_of(i * size, size), size)
            at = pl.ds(pl.multiple_of(way * rows + i * size, size), size)
            total = loc[w][t, at].astype(F32) + sbl[w][t, at].astype(F32)
            if more is not None:
                total = total + slot[w][way, more, inner].astype(F32)
            dst(t, at, total.astype(BF))

    def to_loc(w):
        def put(t, at, value):
            loc[w][t, at] = value

        return put

    def to_y(w):
        def put(t, at, value):
            ysl[w][yi, at] = value

        return put

    for w in range(4):
        for way in range(2):
            load(w, way, 0).wait()
            give(w, way, 0).wait_recv()
            add(w, way, 0, None, to_loc(w))
            hop(w, way, 0).start()

    for i in range(1, share):
        pltpu.make_async_copy(tgs.at[i], tgs.at[i], tgs_recv.at[i]).wait()
    pltpu.make_async_copy(tgs.at[0], tgs.at[0], tgl_sem.at[0]).wait()
    tgo[...] = sum(tgs[i].astype(F32) for i in range(share)).astype(BF)
    send_rows(tg3, tgo, tg, tg_send, tg_recv, (False, True))

    def step(s, carry):
        for w in range(4):
            for way in range(2):
                load(w, way, s).wait()
                give(w, way, s).wait_recv()
                hop(w, way, s - 1).wait_recv()
                add(w, way, s, s - 1, to_loc(w))
                hop(w, way, s).start()
        return carry

    lax.fori_loop(1, n - 1, step, 0)

    def to_others(w, i):
        return pltpu.make_async_remote_copy(
            ysl[w].at[yi], ysl[w].at[yi], y_send.at[w, i], y_recv.at[w, n_y - 2 - i],
            device_id={"dp": others[i]}, device_id_type=MESH,
        )

    for w in range(4):
        for way in range(2):
            load(w, way, n - 1).wait()
            give(w, way, n - 1).wait_recv()
            hop(w, way, n - 2).wait_recv()
            add(w, way, n - 1, n - 2, to_y(w))
        for i in range(n_y - 1):
            to_others(w, i).start()
    for w in range(4):
        rows = 2 * quarter(w)
        for i in range(n_y - 1):
            pltpu.make_async_copy(ysl[w].at[0], ysl[w].at[0], y_recv.at[w, i]).wait()
        size = 32

        @pl.loop(0, rows // size)
        def _(i):
            at = pl.ds(pl.multiple_of(i * size, size), size)
            total = ysl[w][0, at].astype(F32)
            for y in range(1, n_y):
                total = total + ysl[w][y, at].astype(F32)
            fin[w][at] = total

        there = outs[w].at[pl.ds(pl.multiple_of(core * rows, rows), rows)]
        pltpu.make_async_copy(fin[w], there, fin_loc.at[w]).start()
        pltpu.make_async_remote_copy(
            fin[w], there, fin_send.at[w], fin_recv.at[w], device_id={"dp": sib}, device_id_type=MESH
        ).start()

    for w in range(4):
        pltpu.make_async_copy(fin[w], fin[w], fin_loc.at[w]).wait()
        pltpu.make_async_copy(fin[w], fin[w], fin_send.at[w]).wait()
        pltpu.make_async_copy(fin[w], fin[w], fin_recv.at[w]).wait()
        for i in range(n_y - 1):
            pltpu.make_async_copy(ysl[w].at[0], ysl[w].at[0], y_send.at[w, i]).wait()
        for way in range(2):
            some = slot[w].at[0]
            pltpu.make_async_copy(some, some, ring_send.at[w, way]).wait()
        pltpu.make_async_copy(sbl[w], sbl[w], sib_send.at[w]).wait()
    for i in range(1, share):
        pltpu.make_async_copy(tgs.at[0], tgs.at[0], tgs_send.at[i]).wait()
    wait_rows(blk, blk_send, blk_recv)
    wait_rows(tg, tg_send, tg_recv)


def greet_all(plan, n_y, d, m):
    barrier = pltpu.get_barrier_semaphore()
    base = lax.div(d, plan.share) * plan.share

    def one(i, carry):
        e, q = base + lax.div(i, plan.mp), lax.rem(i, plan.mp)

        @pl.when(jnp.logical_or(e != d, q != m))
        def _():
            pl.semaphore_signal(barrier, inc=1, device_id={"dp": e, "mp": q}, device_id_type=MESH)

        return carry

    lax.fori_loop(0, plan.share * plan.mp, one, 0)

    def two(i, carry):
        e = 2 * i + lax.rem(d, 2)

        @pl.when(lax.div(e, plan.share) != lax.div(d, plan.share))
        def _():
            pl.semaphore_signal(barrier, inc=1, device_id={"dp": e}, device_id_type=MESH)

        return carry

    lax.fori_loop(0, n_y, two, 0)
    pl.semaphore_wait(barrier, plan.share * plan.mp - 1 + n_y - plan.share // 2)


def reduce_out(plan, grads, out3, tg3):
    n, share = plan.mp, plan.share
    n_y = plan.dp // 2
    width = out3.shape[2]
    any_space = pl.BlockSpec(memory_space=pl.ANY)
    dma = pltpu.SemaphoreType.DMA
    rows = jax.ShapeDtypeStruct((plan.rows_dev, plan.tok, width), BF)
    halves = [pltpu.VMEM((n, g.shape[1] // 2, g.shape[2]), BF) for g in grads]
    return pl.pallas_call(
        functools.partial(reduce_kernel, plan, n_y),
        out_shape=(*[jax.ShapeDtypeStruct(g.shape[1:], F32) for g in grads], rows, rows),
        in_specs=[any_space] * 6,
        out_specs=[any_space] * 6,
        scratch_shapes=[
            *halves,
            *halves,
            *[pltpu.VMEM((2, n - 1, g.shape[1] // 4, g.shape[2]), BF) for g in grads],
            *[pltpu.VMEM((n_y, g.shape[1] // 2, g.shape[2]), BF) for g in grads],
            *[pltpu.VMEM((g.shape[1] // 2, g.shape[2]), F32) for g in grads],
            pltpu.VMEM((share, plan.part, width), BF),
            pltpu.VMEM((plan.part, width), BF),
            pltpu.VMEM((8, 128), BF),
            dma((4, 2, n)), dma((4,)), dma((4, 2, n)), dma((4, 2)), dma((4, 2, n - 1)),
            dma((4, n_y - 1)), dma((4, n_y - 1)), dma((4,)), dma((4,)), dma((4,)),
            dma((n, 2)), dma((1,)), dma((n, 2)), dma((1,)), dma((share,)), dma((share,)), dma((1,)),
        ],
        compiler_params=pltpu.CompilerParams(
            collective_id=1, has_side_effects=True, vmem_limit_bytes=58 << 20
        ),
        name="reduce",
    )(*grads, out3, tg3)


def scores_of(query, key, allowed):
    raw = lax.dot_general(query, key, (((1,), (1,)), ((), ())), preferred_element_type=F32)
    scores = jnp.where(allowed, raw * HEAD_DIM ** (-0.5), MASKED)
    raised = jnp.exp(scores - jnp.max(scores, axis=-1, keepdims=True))
    return raised / jnp.sum(raised, axis=-1, keepdims=True)


def attend_kernel(heads, proj, seg_col, seg_row, out):
    allowed = seg_col[0] == seg_row[0]
    for h in range(heads):
        at = h * 3 * HEAD_DIM
        query, key, value = (proj[0, :, at + i * HEAD_DIM : at + (i + 1) * HEAD_DIM] for i in range(3))
        probs = scores_of(query, key, allowed).astype(BF)
        mixed = jnp.dot(probs, value, preferred_element_type=F32)
        out[0, :, h * HEAD_DIM : (h + 1) * HEAD_DIM] = mixed.astype(BF)


def attend(proj, seg):
    rows, seq, width3 = proj.shape
    heads = width3 // (3 * HEAD_DIM)
    return pl.pallas_call(
        functools.partial(attend_kernel, heads),
        out_shape=jax.ShapeDtypeStruct((rows, seq, width3 // 3), BF),
        grid=(rows,),
        in_specs=[
            pl.BlockSpec((1, seq, width3), lambda r: (r, 0, 0)),
            pl.BlockSpec((1, seq, 1), lambda r: (r, 0, 0)),
            pl.BlockSpec((1, 1, seq), lambda r: (r, 0, 0)),
        ],
        out_specs=pl.BlockSpec((1, seq, width3 // 3), lambda r: (r, 0, 0)),
        name="attend",
    )(proj, seg[:, :, None], seg[:, None, :])


def attend_back_kernel(heads, proj, grad, seg_col, seg_row, out):
    allowed = seg_col[0] == seg_row[0]
    across = (((1,), (1,)), ((), ()))
    down = (((0,), (0,)), ((), ()))
    for h in range(heads):
        at = h * 3 * HEAD_DIM
        query, key, value = (proj[0, :, at + i * HEAD_DIM : at + (i + 1) * HEAD_DIM] for i in range(3))
        head_grad = grad[0, :, h * HEAD_DIM : (h + 1) * HEAD_DIM]
        full = scores_of(query, key, allowed)
        value_grad = lax.dot_general(full.astype(BF), head_grad, down, preferred_element_type=F32)
        probs_grad = lax.dot_general(head_grad, value, across, preferred_element_type=F32)
        delta = jnp.sum(probs_grad * full, axis=-1, keepdims=True)
        low = (jnp.where(allowed, full * (probs_grad - delta), 0.0) * HEAD_DIM ** (-0.5)).astype(BF)
        query_grad = jnp.dot(low, key, preferred_element_type=F32)
        key_grad = lax.dot_general(low, query, down, preferred_element_type=F32)
        for i, part in enumerate((query_grad, key_grad, value_grad)):
            out[0, :, at + i * HEAD_DIM : at + (i + 1) * HEAD_DIM] = part.astype(BF)


def attend_back(proj, grad, seg):
    rows, seq, width3 = proj.shape
    heads = width3 // (3 * HEAD_DIM)
    return pl.pallas_call(
        functools.partial(attend_back_kernel, heads),
        out_shape=jax.ShapeDtypeStruct((rows, seq, width3), BF),
        grid=(rows,),
        in_specs=[
            pl.BlockSpec((1, seq, width3), lambda r: (r, 0, 0)),
            pl.BlockSpec((1, seq, width3 // 3), lambda r: (r, 0, 0)),
            pl.BlockSpec((1, seq, 1), lambda r: (r, 0, 0)),
            pl.BlockSpec((1, 1, seq), lambda r: (r, 0, 0)),
        ],
        out_specs=pl.BlockSpec((1, seq, width3), lambda r: (r, 0, 0)),
        name="attend_back",
    )(proj, grad, seg[:, :, None], seg[:, None, :])


def norm(values, gain_vec, shift_vec):
    centred = values - jnp.mean(values, axis=-1, keepdims=True)
    scale = lax.rsqrt(jnp.mean(centred * centred, axis=-1, keepdims=True) + EPS)
    unit = centred * scale
    return unit, scale, unit * gain_vec + shift_vec


def norm_back(unit, scale, gain_vec, grad):
    pulled = grad * gain_vec
    inner = jnp.mean(pulled * unit, axis=-1, keepdims=True)
    return scale * (pulled - jnp.mean(pulled, axis=-1, keepdims=True) - unit * inner)


def per_device(
    plan, tokens_in, segment_ids, attn_gain, attn_shift, qkv_weight, qkv_bias, out_weight, out_bias, mlp_gain, mlp_shift,
    up_weight, up_bias, down_weight, down_bias, cotangent,
):
    n, own, seq, part = plan.mp, plan.own, plan.seq, plan.part
    width = tokens_in.shape[2]
    held = own * seq + part
    every = plan.rows * seq
    ff_local = up_weight.shape[1]
    tok3, cot3, seg_all, wq, wo, wu, wd = gather(
        plan, tokens_in, cotangent, segment_ids, (qkv_weight, out_weight, up_weight, down_weight)
    )
    d, m = lax.axis_index("dp"), lax.axis_index("mp")
    k = lax.rem(d, plan.share)
    seg_flat = seg_all.reshape(plan.share * plan.rows_dev, seq)
    seg_own = lax.dynamic_slice(seg_flat, (m * plan.group_rows + own * k, 0), (own, seq))
    seg_last = lax.dynamic_slice(seg_flat, (m * plan.group_rows + own * plan.share, 0), (1, seq))
    seg_last = lax.dynamic_slice(jnp.concatenate([seg_last, seg_last], axis=1), (0, k * part), (1, seq))
    seg = jnp.concatenate([seg_own, seg_last], axis=0)

    bias_q = lax.all_gather(qkv_bias, "mp", axis=0)
    heads_local = qkv_bias.shape[1] // HEAD_DIM
    bias_q = bias_q.reshape(n, 2, heads_local, HEAD_DIM)
    full_bias = jnp.stack([bias_q[:, 0], jnp.zeros_like(bias_q[:, 0]), bias_q[:, 1]], axis=2).reshape(n, -1)
    bias_up = lax.all_gather(up_bias, "mp", axis=0)

    tokens_f = tok3.reshape(every, width).astype(F32)
    unit_one, scale_one, normed = norm(tokens_f, attn_gain, attn_shift)
    normed_one = normed.astype(BF)
    projected = (
        (jnp.einsum("td,sdf->tsf", normed_one, wq, preferred_element_type=F32) + full_bias)
        .astype(BF)
        .reshape(plan.rows, seq, 3 * width)
    )
    attn_out = attend(projected, seg)
    attn_flat = attn_out.reshape(every, width)[:held]
    wo_full = wo.reshape(width, width)
    hidden = tokens_f[:held] + jnp.dot(attn_flat, wo_full, preferred_element_type=F32) + out_bias
    unit_two, scale_two, normed = norm(hidden, mlp_gain, mlp_shift)
    normed_two = normed.astype(BF)
    pre_act = jnp.einsum("td,sdf->tsf", normed_two, wu, preferred_element_type=F32) + bias_up
    act_low = jax.nn.gelu(pre_act, approximate=False).astype(BF)
    down_full = wd.reshape(n * ff_local, width)
    act_flat = act_low.reshape(held, n * ff_local)
    block = (hidden + jnp.dot(act_flat, down_full, preferred_element_type=F32) + down_bias).astype(BF)

    cot = cot3.reshape(every, width)[:held]
    cot_f = cot.astype(F32)
    act_grad = jnp.einsum("td,sfd->tsf", cot, wd, preferred_element_type=F32)
    down_grad = jnp.einsum("tsf,td->sfd", act_low, cot, preferred_element_type=F32).astype(BF)
    phi = 0.5 * (1.0 + lax.erf(pre_act * math.sqrt(0.5)))
    density = jnp.exp(-0.5 * pre_act * pre_act) * (1.0 / math.sqrt(2.0 * math.pi))
    pre_grad = (act_grad * (phi + pre_act * density)).astype(BF)
    up_bias_part = jnp.sum(pre_grad, axis=0, dtype=F32)
    up_grad = jnp.einsum("td,tsf->sdf", normed_two, pre_grad, preferred_element_type=F32).astype(BF)
    normed_two_grad = jnp.einsum("tsf,sdf->td", pre_grad, wu, preferred_element_type=F32)
    mlp_gain_part = jnp.sum(normed_two_grad * unit_two, axis=0)
    mlp_shift_part = jnp.sum(normed_two_grad, axis=0)
    hidden_grad = cot_f + norm_back(unit_two, scale_two, mlp_gain, normed_two_grad)
    branch_grad = hidden_grad.astype(BF)
    out_grad = jnp.einsum("th,td->hd", attn_flat, branch_grad, preferred_element_type=F32).astype(BF)
    out_grad = out_grad.reshape(n, width // n, width)
    attn_grad = jnp.einsum("td,hd->th", branch_grad, wo_full, preferred_element_type=F32).astype(BF)
    attn_grad = jnp.concatenate([attn_grad, jnp.zeros((every - held, width), BF)], axis=0)
    qkv_grads = attend_back(projected, attn_grad.reshape(plan.rows, seq, width), seg)
    qkv_flat = qkv_grads.reshape(every, n, -1)
    qkv_grad = jnp.einsum("td,tsf->sdf", normed_one, qkv_flat, preferred_element_type=F32).astype(BF)
    bias_sums = jnp.sum(qkv_flat, axis=0, dtype=F32).reshape(n, heads_local, 3, HEAD_DIM)
    qkv_bias_part = jnp.stack([bias_sums[:, :, 0], bias_sums[:, :, 2]], axis=1)
    normed_one_grad = jnp.einsum("tsf,sdf->td", qkv_flat, wq, preferred_element_type=F32)
    attn_gain_part = jnp.sum(normed_one_grad * unit_one, axis=0)
    attn_shift_part = jnp.sum(normed_one_grad, axis=0)
    token_part = norm_back(unit_one, scale_one, attn_gain, normed_one_grad)
    tokens_part = jnp.concatenate([token_part[:held] + hidden_grad, token_part[held:]], axis=0).astype(BF)

    block3 = jnp.concatenate([block, jnp.zeros((every - held, width), BF)], axis=0).reshape(plan.rows, seq, width)
    sums = jnp.concatenate(
        [
            attn_gain_part, attn_shift_part, jnp.sum(hidden_grad, axis=0), mlp_gain_part, mlp_shift_part,
            jnp.sum(cot_f, axis=0), up_bias_part.reshape(-1), qkv_bias_part.reshape(-1),
        ]
    )
    sums = lax.psum(sums, ("dp", "mp"))
    six = sums[: 6 * width].reshape(6, width)
    up_sums = sums[6 * width : 6 * width + n * ff_local].reshape(n, ff_local)
    qkv_sums = sums[6 * width + n * ff_local :].reshape(n, 2, width // n)
    up_bias_grad = lax.dynamic_index_in_dim(up_sums, m, 0, keepdims=False)
    qkv_bias_grad = lax.dynamic_index_in_dim(qkv_sums, m, 0, keepdims=False)

    dq, do, du, dd, block_out, tokens_low = reduce_out(
        plan, (qkv_grad, out_grad, up_grad, down_grad), block3, tokens_part.reshape(plan.rows, seq, width)
    )
    tokens_grad = tokens_low.astype(F32)
    return (
        block_out, tokens_grad, six[0], six[1], dq, qkv_bias_grad, do, six[2], six[3], six[4], du, up_bias_grad, dd, six[5],
    )


def solution(mesh):
    dp, mp = mesh.shape["dp"], mesh.shape["mp"]
    rows_spec = P("dp", "mp", None)
    in_specs = (
        rows_spec, P("dp", None), P(), P(), P(None, "mp"), P(None, "mp"), P("mp", None), P(), P(), P(),
        P(None, "mp"), P("mp"), P("mp", None), P(), rows_spec,
    )
    out_specs = (
        rows_spec, rows_spec, P(), P(), P(None, "mp"), P(None, "mp"), P("mp", None), P(), P(), P(),
        P(None, "mp"), P("mp"), P("mp", None), P(),
    )

    def run(tokens_in, segment_ids, *rest):
        rows_all, seq_len, _ = tokens_in.shape
        plan = Plan(dp, mp, rows_all // dp, seq_len // mp, seq_len)
        return jax.shard_map(
            functools.partial(per_device, plan), mesh=mesh, in_specs=in_specs, out_specs=out_specs, check_vma=False
        )(tokens_in, segment_ids, *rest)

    return run
```

time: 2260 us -> 723 us (0.32)
  waiting for transfers between devices: 1780 us -> 0 us
  Pallas kernels: 0 us -> 445 us
  matrix products: 248 us -> 94.3 us
  local copies, waits for them, and re-layouts: 90.3 us -> 39.7 us
  blocking collectives: 48.4 us -> 84.8 us
  other arithmetic: 68 us -> 44 us
    reduce_scatter x4 -> x0, waiting for transfers between devices: 1110 us -> none  [the longest x1 344 us: per_device(): lax.psum_scatter(partial_out, 'mp', scatter_dimension=1, tiled=True)]
    all_gather x4 -> x0, waiting for transfers between devices: 583 us -> none  [the longest x1 148 us: per_device(): lax.all_gather(branch_grad, 'mp', axis=1, tiled=True)]
    pallas_call x0 -> x4, Pallas kernels: none -> 445 us  [the longest x1 204 us: reduce_out(): pl.pallas_call(functools.partial(reduce_kernel, plan, n_y), out_shape=(*[...]
    dot_general x82 -> x12, matrix products: 248 us -> 94.3 us  [the longest x1 15.7 us: per_device(): act_grad = jnp.einsum('td,sfd->tsf', cot, wd, preferred_element_type=F32)]
    psum x1 -> x0, waiting for transfers between devices: 76.8 us -> none  [per_device(): lax.psum((qkv_weight_grad, qkv_bias_grad, out_weight_grad, up_weight_grad...]
    all_gather x0 -> x2, blocking collectives: none -> 33.1 us  [the longest x1 21.9 us: per_device(): bias_up = lax.all_gather(up_bias, 'mp', axis=0)]
    dynamic_update_slice x20 -> x0, other arithmetic: 22.9 us -> none  [the longest x10 16.9 us: per_device(): lax.map(attend_backward, (query_all, key_all, value_all, label_blocks, lo...]
    psum x2 -> x1, blocking collectives: 48.4 us -> 51.8 us  [per_device(): sums = lax.psum(sums, ('dp', 'mp'))]
  transfers between devices with their start and end apart: 9 -> 0, of which waited for: 9 -> 0; matrix products, arithmetic and copies ran while one was open for 5% -> 0% of each run, Pallas kernels for 0% -> 0%
where the time goes in v1:
time: 723 us; the launch traced here: 710 us
  Pallas kernels  445 us (62%)
  matrix products  94.3 us (13%)
  blocking collectives  84.8 us (12%)
  other arithmetic  44 us (6%)
  local copies, waits for them, and re-layouts  39.7 us (5%)
    pallas_call x1, Pallas kernels, reduce_out(): pl.pallas_call(functools.partial(reduce_kernel, plan, n_y), out_shape=(*[...  204 us
    pallas_call x1, Pallas kernels, gather(): pl.pallas_call(functools.partial(gather_kernel, plan), out_shape=(rows, r...  191 us
    psum x1, blocking collectives, per_device(): sums = lax.psum(sums, ('dp', 'mp'))  51.8 us
    pallas_call x1, Pallas kernels, attend_back(): pl.pallas_call(functools.partial(attend_back_kernel, heads), out_shape=ja...  32.1 us
    convert_element_type x1, other arithmetic, per_device(): act_low = jax.nn.gelu(pre_act, approximate=False).astype(BF)  25.5 us
    all_gather x1, blocking collectives, per_device(): bias_up = lax.all_gather(up_bias, 'mp', axis=0)  21.9 us
    pallas_call x1, Pallas kernels, attend(): pl.pallas_call(functools.partial(attend_kernel, heads), out_shape=jax.Sha...  18.3 us
    unnamed x111, local copies, waits for them, and re-layouts  15.7 us

profile of v1, /device:TPU:11, one launch (start us, length us, event | category | flops | bytes accessed | tf_op | source)
XLA Modules:
  0.0 709.6 jit_solution(7171177171439784758)
XLA Ops:
  0.7 191.2 %gather.1 = (bf16[3,256,1024]{2,1,0:T(8,128)(2,1)}, bf16[3,256,1024]{2,1,0:T(8,128)(2,1)}, s32[2,20,256]{2,1,0:T(8,128)}, bf16[8,1024,384]{2,1,0:T(8,128)(2,1)},...) custom-call(bf16[20,32,1024]{2,1,0:T(8,128)(2,1)} %tok.1, ...), custom_call_target="tpu_custom_call" | custom-call | tf_op jit(solution)/shard_map/gather/pallas_call | solution.py:204
  196.7 11.2 %all-gather.2 = f32[8,2,128]{2,1,0:T(2,128)S(1)} all-gather(f32[1,2,128]{2,1,0:T(2,128)S(1)} %bitcast.135), channel_id=2, replica_groups=mesh['dp'=4,'mp'=8] {'mp'}, dimensions={0}, use_global_device_ids=true | all-gather | bytes 9216 | tf_op jit(solution)/shard_map/all_gather | solution.py:603
  208.3 8.4 %add_convert_fusion = bf16[768,8,384]{2,0,1:T(8,128)(2,1)S(1)} fusion(f32[8,384]{1,0:T(8,128)S(1)} %add.130, bf16[8,1024,384]{2,1,0:T(8,128)(2,1)} %get-tuple-element.28, f32[1024]{0:T(1024)S(1)} %copy-done.28, f32[1024]{0:T(1024)S(1)} %copy-done.16, f32[768]{0:T(1024)S(1)} %rsqrt.21, f32[768]{0:T(1024)S(1)} %div.27, bf16[768,1024]{1,0:T(8,128)(2,1)S(1)} %bitcast.107), kind=kOutput, calls=%fused_computation.31 | convolution fusion | flops 4841275392 | bytes 12609536 | tf_op jit(solution)/shard_map/td,sdf->tsf/dot_general | solution.py:613
  216.7 5.0 copy.56
  221.7 8.3 %reshape.196.proj = bf16[3,256,3072]{2,1,0:T(8,128)(2,1)} reshape(bf16[768,8,384]{2,1,0:T(8,128)(2,1)} %copy.56) | data formatting | bytes 9437184 | tf_op jit(solution)/shard_map/reshape | solution.py:615
  230.0 18.3 %attend.1 = bf16[3,256,1024]{2,1,0:T(8,128)(2,1)} custom-call(bf16[3,256,3072]{2,1,0:T(8,128)(2,1)} %reshape.196.proj, s32[3,256,1]{2,1,0:T(8,128)} %copy.57.seg_col, s32[3,1,256]{2,1,0:T(1,128)} %broadcast_in_dim.5.seg_row), custom_call_target="tpu_custom_call" | custom-call | tf_op jit(solution)/shard_map/attend/pallas_call | solution.py:519
  252.6 21.9 %all-gather.3 = f32[8,1,512]{2,1,0:T(1,128)S(1)} all-gather(f32[1,1,512]{2,1,0:T(1,128)S(1)} %bitcast.133), channel_id=3, replica_groups=mesh['dp'=4,'mp'=8] {'mp'}, dimensions={0}, use_global_device_ids=true | all-gather | bytes 18432 | tf_op jit(solution)/shard_map/all_gather | solution.py:607
  274.5 8.6 %fusion.29 = (u8[640,512]{1,0:T(8,128)(4,1)S(1)}, u8[640,512]{1,0:T(8,128)(4,1)}, f32[640,8,512]{2,0,1:T(8,128)S(1)}) fusion(f32[8,512]{1,0:T(8,128)S(1)} %bitcast.123, bf16[8,1024,512]{2,1,0:T(8,128)(2,1)S(1)} %bitcast.139, f32[640,1024]{1,0:T(8,128)S(1)} %get-tuple-element.66, f32[1024]{0:T(1024)S(1)} %copy-done.38, f32[1024]{0:T(1024)S(1)} %copy-done.26, ...), kind=kOutput, calls=%fused_computation.67 | convolution fusion | flops 5408030720 | bytes 22180864 | tf_op jit(solution)/shard_map/td,sdf->tsf/dot_general | solution.py:623
  283.0 15.7 %convert_reduce_fusion = (f32[8,512]{1,0:T(8,128)}, bf16[640,8,512]{2,0,1:T(8,128)(2,1)}) fusion(f32[640,8,512]{2,0,1:T(8,128)S(1)} %get-tuple-element.68, f32[8,512]{1,0:T(8,128)S(1)} %bitcast.124, bf16[8,512,1024]{2,1,0:T(8,128)(2,1)} %get-tuple-element.32, bf16[768,1024]{1,0:T(8,128)(2,1)} %bitcast.120), kind=kOutput, calls=%fused_computation.16 | convolution fusion | flops 5402783744 | bytes 25460736 | tf_op jit(solution)/shard_map/td,sfd->tsf/dot_general | solution.py:631
  298.8 11.0 %fusion.27 = (f32[1024]{0:T(1024)}, f32[640]{0:T(1024)S(1)}, f32[640]{0:T(1024)S(1)}, f32[1024]{0:T(1024)}, f32[640,1024,1]{1,0,2:T(8,128)S(1)}) fusion(f32[640,1024]{1,0:T(8,128)S(1)} %get-tuple-element.66, f32[640]{0:T(1024)S(1)} %add_rsqrt_fusion, f32[640]{0:T(1024)S(1)} %broadcast_multiply_fusion.4, f32[1024]{0:T(1024)S(1)} %copy-done.26, ...), kind=kOutput, calls=%fused_computation.62 | convolution fusion | flops 5374604288 | bytes 18896896 | tf_op jit(solution)/shard_map/tsf,sdf->td/dot_general | solution.py:638
  314.7 32.1 %attend_back.1 = bf16[3,256,3072]{2,1,0:T(8,128)(2,1)} custom-call(bf16[3,256,3072]{2,1,0:T(8,128)(2,1)} %reshape.196.proj, bf16[3,256,1024]{2,1,0:T(8,128)(2,1)} %bitcast.111, s32[3,256,1]{2,1,0:T(8,128)} %copy.57.seg_col, s32[3,1,256]{2,1,0:T(1,128)} %broadcast_in_dim.5.seg_row), custom_call_target="tpu_custom_call" | custom-call | tf_op jit(solution)/shard_map/attend_back/pallas_call | solution.py:555
  346.8 3.2 convert_reduce_fusion.1
  350.2 3.5 copy.75
  353.8 12.3 %fusion.21 = (f32[1024]{0:T(1024)S(1)}, f32[768]{0:T(1024)}, f32[768]{0:T(1024)}, f32[1024]{0:T(1024)S(1)}, f32[768,1024,1]{1,0,2:T(8,128)}) fusion(f32[768]{0:T(1024)S(1)} %copy-done.18, f32[768]{0:T(1024)S(1)} %copy-done.20, bf16[3,256,1024]{2,1,0:T(8,128)(2,1)S(1)} %copy-done, f32[1024]{0:T(1024)S(1)} %copy-done.16, ...), kind=kOutput, calls=%fused_computation.44 | convolution fusion | flops 4839698432 | bytes 15753216 | tf_op jit(solution)/shard_map/tsf,sdf->td/dot_general | solution.py:652
  370.8 51.8 %psum.7 = f32[12288]{0:T(1024)S(1)} all-reduce(f32[12288]{0:T(1024)} %constant_dynamic-update-slice_fusion), channel_id=1, replica_groups=mesh['dp'=4,'mp'=8] {'dp','mp'}, use_global_device_ids=true, to_apply=%region_16.0 | all-reduce | flops 12288 | bytes 98304 | tf_op jit(solution)/shard_map/psum | solution.py:665
  428.4 2.9 subtract_multiply_fusion
  433.9 25.5 %fusion.8 = bf16[640,8,512]{2,0,1:T(8,128)(2,1)S(1)} fusion(f32[640,8,512]{2,0,1:T(8,128)} %copy-done.5, f32[8,512]{1,0:T(8,128)S(1)} %bitcast.125, u8[640,512]{1,0:T(8,128)(4,1)S(1)} %copy-done.15, u8[640,512]{1,0:T(8,128)(4,1)S(1)} %get-tuple-element.40), kind=kLoop, calls=%fused_computation.10 | loop fusion | flops 186122240 | bytes 16400384 | tf_op jit(solution)/shard_map/convert_element_type | solution.py:624
  459.5 5.6 fusion.26
  466.4 9.3 %convolution_convert_fusion.x3 = bf16[8,512,1024]{2,1,0:T(8,128)(2,1)} fusion(bf16[640,8,512]{2,0,1:T(8,128)(2,1)S(1)} %fusion.8, bf16[768,1024]{1,0:T(8,128)(2,1)S(1)} %bitcast.122), kind=kOutput, calls=%fused_computation.33 | convolution fusion | flops 5372903424 | bytes 14942208 | tf_op jit(solution)/shard_map/tsf,td->sfd/dot_general | solution.py:632
  475.7 10.0 %convert_bitcast_fusion.x2 = bf16[8,1024,512]{2,1,0:T(8,128)(2,1)} fusion(bf16[640,8,512]{2,0,1:T(8,128)(2,1)S(1)} %bitcast.143, f32[640,1024]{1,0:T(8,128)S(1)} %copy-done.4, f32[1024]{0:T(1024)S(1)} %copy-done.39, f32[1024]{0:T(1024)S(1)} %copy-done.27, f32[640]{0:T(1024)S(1)} %copy-done.22, f32[640]{0:T(1024)S(1)} %broadcast_multiply_fusion.4), kind=kOutput, calls=%fused_computation.32 | convolution fusion | flops 5376180224 | bytes 16266240 | tf_op jit(solution)/shard_map/td,tsf->sdf/dot_general | solution.py:637
  485.7 3.2 convolution_convert_fusion.1
  489.5 7.2 %convert_bitcast_fusion.1.x0 = bf16[8,1024,384]{2,1,0:T(8,128)(2,1)} fusion(bf16[768,1024,1]{1,0,2:T(8,128)(2,1)S(1)} %bitcast.117, bf16[768,8,384]{2,1,0:T(8,128)(2,1)S(1)} %bitcast.115), kind=kOutput, calls=%fused_computation.34 | convolution fusion | flops 4834983936 | bytes 12582912 | tf_op jit(solution)/shard_map/td,tsf->sdf/dot_general | solution.py:649
  496.7 203.5 %reduce.8 = (f32[1024,384]{1,0:T(8,128)}, f32[128,1024]{1,0:T(8,128)}, f32[1024,512]{1,0:T(8,128)}, f32[512,1024]{1,0:T(8,128)}, bf16[20,32,1024]{2,1,0:T(8,128)(2,1)}, /*index=5*/bf16[20,32,1024]{2,1,0:T(8,128)(2,1)}) custom-call(bf16[8,1024,384]{2,1,0:T(8,128)(2,1)} %convert_bitcast_fusion.1.x0, bf16[8,128,1024]{2,1,0:T(8,128)(2,1)} %bitcast.116, ...), custom_call_target="tpu_custom_call" | custom-call | tf_op jit(solution)/shard_map/reduce/pallas_call | solution.py:474
  700.3 3.3 convert_element_type.95
  (160 shorter events, 35.1 us)
Async XLA Ops:
  191.9 16.4 %copy-start.16 = (f32[1024]{0:T(1024)S(1)}, f32[1024]{0:T(1024)}, u32[]{:S(2)}) copy-start(f32[1024]{0:T(1024)} %param.17) | copy-start | bytes 12292
  191.9 16.4 %copy-start.28 = (f32[1024]{0:T(1024)S(1)}, f32[1024]{0:T(1024)}, u32[]{:S(2)}) copy-start(f32[1024]{0:T(1024)} %param.18) | copy-start | bytes 12292
  196.7 20.0 %copy-start.17 = (f32[768]{0:T(1024)}, f32[768]{0:T(1024)S(1)}, u32[]{:S(2)}) copy-start(f32[768]{0:T(1024)S(1)} %rsqrt.21) | copy-start | bytes 9220
  196.7 20.0 %copy-start.19 = (f32[768]{0:T(1024)}, f32[768]{0:T(1024)S(1)}, u32[]{:S(2)}) copy-start(f32[768]{0:T(1024)S(1)} %div.27) | copy-start | bytes 9220
  248.4 26.1 %slice-start.4 = ((s8[8388608]{0:T(1024)(128)(4,1)}), s8[4194304]{0:T(1024)(128)(4,1)S(1)}, s32[]{:S(2)}) async-start(s8[8388608]{0:T(1024)(128)(4,1)} %bitcast.138), calls=%async_computation.4 | async-start | bytes 8388608
  250.5 24.0 %copy-start.26 = (f32[1024]{0:T(1024)S(1)}, f32[1024]{0:T(1024)}, u32[]{:S(2)}) copy-start(f32[1024]{0:T(1024)} %param.23) | copy-start | bytes 12292
  250.5 24.0 %slice-start.5 = ((s8[8388608]{0:T(1024)(128)(4,1)}), s8[4194304]{0:T(1024)(128)(4,1)S(1)}, s32[]{:S(2)}) async-start(s8[8388608]{0:T(1024)(128)(4,1)} %bitcast.138), calls=%async_computation.5 | async-start | bytes 8388608
  250.5 24.0 %copy-start.38 = (f32[1024]{0:T(1024)S(1)}, f32[1024]{0:T(1024)}, u32[]{:S(2)}) copy-start(f32[1024]{0:T(1024)} %param.24) | copy-start | bytes 12292
  252.1 57.7 %copy-start.3 = (f32[640,1024]{1,0:T(8,128)}, f32[640,1024]{1,0:T(8,128)S(1)}, u32[]{:S(2)}) copy-start(f32[640,1024]{1,0:T(8,128)S(1)} %get-tuple-element.66) | copy-start | bytes 7864324
  252.5 57.3 %copy-start.21 = (f32[640]{0:T(1024)}, f32[640]{0:T(1024)S(1)}, u32[]{:S(2)}) copy-start(f32[640]{0:T(1024)S(1)} %add_rsqrt_fusion) | copy-start | bytes 7684
  283.0 15.7 %copy-start.5 = (f32[640,8,512]{2,0,1:T(8,128)}, f32[640,8,512]{2,0,1:T(8,128)S(1)}, u32[]{:S(2)}) copy-start(f32[640,8,512]{2,0,1:T(8,128)S(1)} %get-tuple-element.68) | copy-start | bytes 31457284
  298.8 11.0 %copy-start.13 = (bf16[3,256,1024]{2,1,0:T(8,128)(2,1)S(1)}, bf16[3,256,1024]{2,1,0:T(8,128)(2,1)}, u32[]{:S(2)}) copy-start(bf16[3,256,1024]{2,1,0:T(8,128)(2,1)} %get-tuple-element.29) | copy-start | bytes 4718596
  353.7 12.4 %copy-start.6 = (bf16[96,8,8,384]{3,2,1,0:T(8,128)(2,1)}, bf16[96,8,8,384]{3,2,1,0:T(8,128)(2,1)S(1)}, u32[]{:S(2)}) copy-start(bf16[96,8,8,384]{3,2,1,0:T(8,128)(2,1)S(1)} %copy.75) | copy-start | bytes 14155780
  353.7 13.5 %copy-start.24 = (f32[1024]{0:T(1024)S(1)}, f32[1024]{0:T(1024)}, u32[]{:S(2)}) copy-start(f32[1024]{0:T(1024)} %get-tuple-element.50) | copy-start | bytes 12292
  353.7 14.1 %copy-start.31 = (f32[1024]{0:T(1024)S(1)}, f32[1024]{0:T(1024)}, u32[]{:S(2)}) copy-start(f32[1024]{0:T(1024)} %get-tuple-element.42) | copy-start | bytes 12292
  353.7 14.7 %copy-start.30 = (f32[1024]{0:T(1024)S(1)}, f32[1024]{0:T(1024)}, u32[]{:S(2)}) copy-start(f32[1024]{0:T(1024)} %get-tuple-element.49) | copy-start | bytes 12292
  353.8 15.3 %copy-start.23 = (f32[1024]{0:T(1024)S(1)}, f32[1024]{0:T(1024)}, u32[]{:S(2)}) copy-start(f32[1024]{0:T(1024)} %get-tuple-element.52) | copy-start | bytes 12292
  353.8 15.9 %copy-start.25 = (f32[8,512]{1,0:T(8,128)S(1)}, f32[8,512]{1,0:T(8,128)}, u32[]{:S(2)}) copy-start(f32[8,512]{1,0:T(8,128)} %get-tuple-element.70) | copy-start | bytes 49156
  431.3 28.1 %slice-start.2 = ((s8[8388608]{0:T(1024)(128)(4,1)}), s8[4194304]{0:T(1024)(128)(4,1)S(1)}, s32[]{:S(2)}) async-start(s8[8388608]{0:T(1024)(128)(4,1)} %bitcast.136), calls=%async_computation.2 | async-start | bytes 8388608
  433.9 25.6 %copy-start.4 = (f32[640,1024]{1,0:T(8,128)S(1)}, f32[640,1024]{1,0:T(8,128)}, u32[]{:S(2)}) copy-start(f32[640,1024]{1,0:T(8,128)} %copy-done.3) | copy-start | bytes 7864324
  433.9 25.6 %slice-start.3 = ((s8[8388608]{0:T(1024)(128)(4,1)}), s8[4194304]{0:T(1024)(128)(4,1)S(1)}, s32[]{:S(2)}) async-start(s8[8388608]{0:T(1024)(128)(4,1)} %bitcast.136), calls=%async_computation.3 | async-start | bytes 8388608
  433.9 25.6 %copy-start.37 = (f32[1024]{0:T(1024)S(1)}, f32[1024]{0:T(1024)}, u32[]{:S(2)}) copy-start(f32[1024]{0:T(1024)} %param.28) | copy-start | bytes 12292
  466.4 23.1 %slice-start = ((s8[4718592]{0:T(1024)(128)(4,1)}), s8[524288]{0:T(1024)(128)(4,1)S(1)}, s32[]{:S(2)}) async-start(s8[4718592]{0:T(1024)(128)(4,1)} %bitcast.113), calls=%async_computation | async-start | bytes 1048576
  475.7 13.8 %slice-start.1 = ((s8[4718592]{0:T(1024)(128)(4,1)}), s8[4194304]{0:T(1024)(128)(4,1)S(1)}, s32[]{:S(2)}) async-start(s8[4718592]{0:T(1024)(128)(4,1)} %bitcast.113), calls=%async_computation.1 | async-start | bytes 8388608
  (24 other events, 108.2 us)

commit v2 on v1

v2 whole, which is shorter than its diff:
```python
import functools
import math

import jax
import jax.numpy as jnp
from jax import lax
from jax.experimental import pallas as pl
from jax.experimental.pallas import tpu as pltpu
from jax.sharding import PartitionSpec as P

HEAD_DIM = 64
EPS = 1e-06
MASKED = -1000000000.0
MESH = pl.DeviceIdType.MESH
BF = jnp.bfloat16
F32 = jnp.float32


class Plan:
    def __init__(self, dp, mp, rows_dev, tok_local, seq_len):
        self.dp, self.mp, self.rows_dev, self.tok, self.seq = dp, mp, rows_dev, tok_local, seq_len
        self.share = mp // math.gcd(rows_dev, mp)
        self.group_rows = rows_dev * self.share // mp
        self.own = self.group_rows // self.share
        if self.share % 2 or dp % self.share or dp % 4 or self.group_rows != self.own * self.share + 1:
            raise ValueError("unsupported sizes")
        self.groups = mp // self.share
        self.part = seq_len // self.share
        self.rows = self.own + 1
        self.hops = mp // 2
        self.all = dp * mp

    def ring_at(self, p):
        p = lax.rem(p, self.mp)
        back = lax.div(p, self.mp // 2)
        return 2 * p * (1 - back) + (2 * self.mp - 1 - 2 * p) * back


class Place:
    def __init__(self, plan):
        d, m = lax.axis_index("dp"), lax.axis_index("mp")
        odd = lax.rem(m, 2)
        self.d, self.m = d, m
        self.p = lax.div(m, 2) * (1 - odd) + (plan.mp - 1 - lax.div(m, 2)) * odd
        self.core = lax.rem(d, 2)
        self.sib = d + 1 - 2 * self.core
        self.y = lax.rem(lax.div(d, 2), 2)
        self.other = d + 2 - 4 * self.y
        self.k = lax.rem(d, plan.share)
        self.base = d - self.k
        self.quarter = 2 * self.y + self.core
        self.neighbour = (plan.ring_at(self.p + 1), plan.ring_at(self.p + plan.mp - 1))

    def away(self, plan, way, s):
        return plan.ring_at(self.p + plan.mp - s if way == 0 else self.p + s)


def greet(plan, at, everyone):
    barrier = pltpu.get_barrier_semaphore()
    span = plan.dp if everyone else max(plan.share, 4)
    base = lax.div(at.d, span) * span

    def one(i, carry):
        e, q = base + lax.div(i, plan.mp), lax.rem(i, plan.mp)

        @pl.when(jnp.logical_or(e != at.d, q != at.m))
        def _():
            pl.semaphore_signal(barrier, inc=1, device_id={"dp": e, "mp": q}, device_id_type=MESH)

        return carry

    lax.fori_loop(0, span * plan.mp, one, 0)
    pl.semaphore_wait(barrier, span * plan.mp - 1)


def remote(src, dst, send, recv, **to):
    return pltpu.make_async_remote_copy(src, dst, send, recv, device_id=to, device_id_type=MESH)


def settle(ref, sem):
    pltpu.make_async_copy(ref, ref, sem).wait()


def piece(ref, quarter, half=None):
    rows, cols = ref.shape[0] // 4, ref.shape[1]
    first = quarter * rows
    if half is None:
        return ref.at[pl.ds(pl.multiple_of(first, rows), rows)]
    if cols % 256 == 0:
        return ref.at[pl.ds(pl.multiple_of(first, rows), rows), pl.ds(half * (cols // 2), cols // 2)]
    return ref.at[pl.ds(pl.multiple_of(first + half * (rows // 2), rows // 2), rows // 2)]


def half_of(ref, half):
    rows, cols = ref.shape
    if cols % 256 == 0:
        return ref.at[:, pl.ds(half * (cols // 2), cols // 2)]
    return ref.at[pl.ds(half * (rows // 2), rows // 2)]


class Gatherer:
    def __init__(self, plan, at, shards, full, sems):
        self.plan, self.at, self.shards, self.full = plan, at, shards, full
        self.own_sem, self.ring_send, self.ring_recv, self.y_send, self.y_recv, self.sib_send, self.sib_recv = sems

    def _half(self, way, s):
        return way if s == self.plan.hops - 1 else None

    def ring(self, w, way, s):
        at, origin = self.at, self.at.away(self.plan, way, s)
        half = self._half(way, s)
        dst = piece(self.full[w].at[origin], at.quarter, half)
        src = piece(self.shards[w], at.quarter, half) if s == 0 else dst
        return remote(src, dst, self.ring_send.at[w, way], self.ring_recv.at[w, way, s], mp=at.neighbour[way])

    def cross(self, w, way, s):
        at, origin = self.at, self.at.away(self.plan, way, s + 1)
        block = piece(self.full[w].at[origin], at.quarter, self._half(way, s))
        return remote(block, block, self.y_send.at[w], self.y_recv.at[w, way, s], dp=at.other)

    def give(self, w, way, s, mine):
        at, origin = self.at, self.at.away(self.plan, way, s + 1)
        quarter = at.quarter if mine else 2 - 2 * at.y + at.core
        block = piece(self.full[w].at[origin], quarter, self._half(way, s))
        return remote(block, block, self.sib_send.at[w], self.sib_recv.at[w], dp=at.sib)

    def begin(self, w):
        for way in range(2):
            self.ring(w, way, 0).start()
        pltpu.make_async_copy(self.shards[w], self.full[w].at[self.at.m], self.own_sem.at[w]).start()

    def step(self, w, s):
        for way in range(2):
            self.ring(w, way, s).wait_recv()
            if s < self.plan.hops - 1:
                self.ring(w, way, s + 1).start()
            self.cross(w, way, s).start()
            self.give(w, way, s, True).start()

    def follow(self, w, s):
        for way in range(2):
            self.cross(w, way, s).wait_recv()
            self.give(w, way, s, False).start()

    def arrived(self, w):
        n, rows = self.plan.mp, self.shards[w].shape[0]
        settle(self.full[w].at[pl.ds(0, n - 1), pl.ds(0, rows // 2)], self.sib_recv.at[w])
        settle(self.shards[w], self.own_sem.at[w])

    def finish(self, w):
        n, rows = self.plan.mp, self.shards[w].shape[0]
        settle(self.full[w].at[pl.ds(0, n - 1), pl.ds(0, rows // 2)], self.sib_send.at[w])
        settle(self.full[w].at[pl.ds(0, n - 1), pl.ds(0, rows // 4)], self.y_send.at[w])
        for way in range(2):
            settle(self.full[w].at[pl.ds(0, self.plan.hops - 1), pl.ds(0, rows // 4)], self.ring_send.at[w, way])
            settle(piece(self.full[w].at[0], 0, way), self.ring_send.at[w, way])


def gatherer_sems(plan, count):
    dma = pltpu.SemaphoreType.DMA
    return [
        dma((count,)), dma((count, 2)), dma((count, 2, plan.hops)), dma((count,)), dma((count, 2, plan.hops)),
        dma((count,)), dma((count,)),
    ]


class RowsIn:
    def __init__(self, plan, at, src, dst, send, recv, whole_shared):
        self.plan, self.at, self.src, self.dst, self.send, self.recv = plan, at, src, dst, send, recv
        self.whole_shared = whole_shared

    def copies(self):
        plan, at = self.plan, self.at
        mine = pl.ds(pl.multiple_of(at.m * plan.tok, plan.tok), plan.tok)
        for j in range(plan.groups):
            q = at.k * plan.groups + j
            first = j * plan.group_rows
            for e in range(plan.share):
                here = jnp.logical_and(at.k == e, at.m == q)
                holds = True if self.whole_shared else lax.div(at.m * plan.tok, plan.part) == e
                to = lax.rem(at.m * plan.tok + plan.seq - e * plan.part, plan.seq)
                to = pl.ds(pl.multiple_of(to, plan.tok), plan.tok)
                yield here, True, q, e, j, 0, self.src.at[pl.ds(first + plan.own * e, plan.own)], self.dst.at[
                    pl.ds(0, plan.own), mine
                ]
                yield here, holds, q, e, j, 1, self.src.at[first + plan.own * plan.share], self.dst.at[plan.own, to]

    def start(self):
        for here, wanted, q, e, j, what, src, dst in self.copies():

            @pl.when(jnp.logical_and(here, wanted))
            def _():
                pltpu.make_async_copy(src, dst, self.recv.at[what]).start()

            @pl.when(jnp.logical_and(jnp.logical_not(here), wanted))
            def _():
                remote(src, dst, self.send.at[j, e, what], self.recv.at[what], dp=self.at.base + e, mp=q).start()

    def arrived(self):
        plan = self.plan
        settle(self.dst.at[pl.ds(0, plan.own)], self.recv.at[0])
        extent = plan.seq if self.whole_shared else plan.part
        settle(self.dst.at[plan.own, pl.ds(0, extent)], self.recv.at[1])

    def finish(self):
        for here, wanted, q, e, j, what, src, dst in self.copies():

            @pl.when(jnp.logical_and(jnp.logical_not(here), wanted))
            def _():
                settle(src, self.send.at[j, e, what])


def gather_kernel(
    plan, tok, cot, seg, bq, bu, w0, w1, w2, w3, tok3, cot3, seg3, gbq, gbu, g0, g1, g2, g3,
    tok_send, tok_recv, cot_send, cot_recv, seg_send, seg_recv, bias_send, bias_recv, *sems,
):
    n, share = plan.mp, plan.share
    at = Place(plan)
    gat = Gatherer(plan, at, (w0, w1, w2, w3), (g0, g1, g2, g3), sems)
    tokens = RowsIn(plan, at, tok, tok3, tok_send, tok_recv, True)
    cots = RowsIn(plan, at, cot, cot3, cot_send, cot_recv, False)
    greet(plan, at, False)

    gat.begin(0)
    tokens.start()
    biases = ((bq, gbq, 0), (bu, gbu, 1))
    for src, dst, i in biases:
        pltpu.make_async_copy(src, dst.at[at.m], bias_recv.at[i]).start()
        for s in range(1, n):
            remote(src, dst.at[at.m], bias_send.at[i], bias_recv.at[i], mp=lax.rem(at.m + s, n)).start()
    pltpu.make_async_copy(seg, seg3.at[at.k], seg_recv.at[0]).start()
    for e in range(1, share):
        remote(seg, seg3.at[at.k], seg_send.at[0], seg_recv.at[0], dp=at.base + lax.rem(at.k + e, share)).start()
    for w in (1, 2, 3):
        gat.begin(w)
    cots.start()
    for s in range(plan.hops):
        for w in range(4):
            gat.step(w, s)
            if s:
                gat.follow(w, s - 1)
    for w in range(4):
        gat.follow(w, plan.hops - 1)
    for w in range(4):
        gat.arrived(w)
        gat.finish(w)
    tokens.arrived()
    tokens.finish()
    cots.arrived()
    cots.finish()
    for src, dst, i in biases:
        settle(dst, bias_recv.at[i])
        settle(dst.at[pl.ds(0, n - 1)], bias_send.at[i])
    settle(seg3, seg_recv.at[0])
    settle(seg3.at[pl.ds(0, share - 1)], seg_send.at[0])


def gather(plan, tokens_in, cotangent, segment_ids, biases, weights):
    n, share = plan.mp, plan.share
    width = tokens_in.shape[2]
    any_space = pl.BlockSpec(memory_space=pl.ANY)
    dma = pltpu.SemaphoreType.DMA
    rows = jax.ShapeDtypeStruct((plan.rows, plan.seq, width), BF)
    return pl.pallas_call(
        functools.partial(gather_kernel, plan),
        out_shape=(
            rows,
            rows,
            jax.ShapeDtypeStruct((share,) + segment_ids.shape, jnp.int32),
            *[jax.ShapeDtypeStruct((n,) + b.shape, F32) for b in biases],
            *[jax.ShapeDtypeStruct((n,) + w.shape, BF) for w in weights],
        ),
        in_specs=[any_space] * 9,
        out_specs=[any_space] * 9,
        scratch_shapes=[
            dma((plan.groups, share, 2)), dma((2,)), dma((plan.groups, share, 2)), dma((2,)), dma((1,)), dma((1,)),
            dma((2,)), dma((2,)), *gatherer_sems(plan, 4),
        ],
        compiler_params=pltpu.CompilerParams(collective_id=0, has_side_effects=True),
        name="gather",
    )(tokens_in, cotangent, segment_ids, *biases, *weights)


class Reducer:
    def __init__(self, plan, at, grads, loc, sbl, yrc, slot, fin, grp, sems):
        self.plan, self.at, self.grads = plan, at, grads
        self.loc, self.sbl, self.yrc, self.slot, self.fin, self.grp = loc, sbl, yrc, slot, fin, grp
        (
            self.loc_sem, self.sib_send, self.sib_recv, self.y_send, self.y_recv, self.ring_send, self.ring_recv,
            self.grp_send, self.grp_recv, self.fin_send, self.fin_recv,
        ) = sems
        hops = plan.hops
        self.order = [(0, hops)] + [(way, dist) for dist in range(hops - 1, 0, -1) for way in range(2)] + [(0, 0)]

    def target(self, i):
        way, dist = self.order[i]
        return self.plan.ring_at(self.at.p + dist if way == 0 else self.at.p + self.plan.mp - dist)

    def load(self, w, yy, i):
        at, t = self.at, self.target(i)
        src = piece(self.grads[w].at[t], 2 * yy + at.core)
        return pltpu.make_async_copy(src, self.loc[w].at[yy, t], self.loc_sem.at[w, i, yy])

    def give(self, w, yy, i):
        at, t = self.at, self.target(i)
        src = piece(self.grads[w].at[t], 2 * yy + 1 - at.core)
        return remote(src, self.sbl[w].at[yy, t], self.sib_send.at[w], self.sib_recv.at[w, i, yy], dp=at.sib)

    def begin(self, w):
        for i in range(len(self.order)):
            for yy in range(2):
                self.load(w, yy, i).start()
                self.give(w, yy, i).start()
        if self.plan.hops > 0:
            for way in range(2):
                part = half_of(self.slot[w].at[way, 0], 1 - way)
                part[...] = jnp.zeros(part.shape, BF)

    def ready(self, w, yy, i):
        for v in range(2):

            @pl.when(yy == v)
            def _():
                self.load(w, v, i).wait()
                self.give(w, v, i).wait_recv()

    def add(self, w, yy, t, extra, put):
        rows, cols = self.loc[w].shape[2:]
        size = 32 if rows % 32 == 0 else rows

        def block(b):
            inner = pl.ds(pl.multiple_of(b * size, size), size)
            total = self.loc[w][yy, t, inner].astype(F32) + self.sbl[w][yy, t, inner].astype(F32)
            for ref in extra:
                total = total + ref[inner].astype(F32)
            put(inner, total)

        if rows == size:
            block(0)
        else:
            pl.loop(0, rows // size)(block)

    def cross(self, w, i):
        at, t = self.at, self.target(i)
        return remote(self.loc[w].at[1 - at.y, t], self.yrc[w].at[t], self.y_send.at[w], self.y_recv.at[w, i], dp=at.other)

    def first(self, w, i):
        at, t = self.at, self.target(i)
        self.ready(w, 1 - at.y, i)

        def put(inner, total):
            self.loc[w][1 - at.y, t, inner] = total.astype(BF)

        self.add(w, 1 - at.y, t, (), put)
        self.cross(w, i).start()

    def hop(self, w, way, s, t):
        src = self.loc[w].at[self.at.y, t]
        dst = self.slot[w].at[way, s]
        if s == 0:
            src, dst = half_of(src, way), half_of(dst, way)
        return remote(
            src, dst, self.ring_send.at[w, way], self.ring_recv.at[w, way, s], mp=self.at.neighbour[way]
        )

    def step(self, w, i):
        at, t = self.at, self.target(i)
        way, dist = self.order[i]
        s = self.plan.hops - dist
        self.ready(w, at.y, i)
        self.cross(w, i).wait_recv()
        extra = [self.yrc[w].at[t]]
        ways = (0, 1) if dist in (0, self.plan.hops) else (way,)
        if s > 0:
            for v in ways:
                self.hop(w, v, s - 1, t).wait_recv()
                extra.append(self.slot[w].at[v, s - 1])
        rows = self.loc[w].shape[2]
        if dist:

            def put(inner, total):
                self.loc[w][at.y, t, inner] = total.astype(BF)

            self.add(w, at.y, t, extra, put)
            for v in ways:
                self.hop(w, v, s, t).start()
        else:
            quads = self.plan.dp // 4
            mine = lax.div(at.d, 4)

            def put(inner, total):
                if quads > 1:
                    self.grp[w][mine, inner] = total.astype(BF)
                else:
                    to = pl.ds(pl.multiple_of(at.quarter * rows + inner.start, inner.size), inner.size)
                    self.fin[w][to] = total.astype(BF)

            self.add(w, at.y, t, extra, put)
            if quads > 1:
                for i in range(1, quads):
                    self.between(w, i, 0).start()

    def between(self, w, i, what):
        at, quads = self.at, self.plan.dp // 4
        to = lax.rem(at.d + 4 * i, self.plan.dp)
        block = self.grp[w].at[lax.div(at.d, 4)]
        return remote(block, block, self.grp_send.at[w], self.grp_recv.at[w], dp=to)

    def share_out(self, w, what):
        at = self.at
        quarter = at.quarter if what != 1 else 2 - 2 * at.y + at.core
        block = piece(self.fin[w], quarter)
        to = at.other if what == 2 else at.sib
        return remote(block, block, self.fin_send.at[w, what], self.fin_recv.at[w, what], dp=to)

    def last(self, w):
        quads = self.plan.dp // 4
        if quads > 1:
            rows = self.loc[w].shape[2]
            settle(self.grp[w].at[pl.ds(0, quads - 1)], self.grp_recv.at[w])
            total = self.grp[w][0].astype(F32)
            for i in range(1, quads):
                total = total + self.grp[w][i].astype(F32)
            self.fin[w][pl.ds(pl.multiple_of(self.at.quarter * rows, rows), rows)] = total.astype(BF)
        self.share_out(w, 2).start()
        self.share_out(w, 0).start()

    def spread(self, w):
        self.share_out(w, 2).wait_recv()
        self.share_out(w, 1).start()

    def arrived(self, w):
        self.share_out(w, 0).wait_recv()
        self.share_out(w, 1).wait_recv()

    def finish(self, w):
        hops = self.plan.hops
        quads = self.plan.dp // 4
        for what in range(3):
            self.share_out(w, what).wait_send()
        for i in range(1, quads):
            self.between(w, i, 0).wait_send()
        settle(self.loc[w].at[0], self.y_send.at[w])
        settle(self.sbl[w], self.sib_send.at[w])
        for way in range(2):
            settle(self.slot[w].at[way, pl.ds(0, hops - 1)], self.ring_send.at[w, way])
            settle(half_of(self.slot[w].at[way, 0], way), self.ring_send.at[w, way])


def reducer_scratch(plan, grads):
    n, quads = plan.mp, plan.dp // 4
    dma = pltpu.SemaphoreType.DMA
    count = len(grads)
    quarter = [(g.shape[1] // 4, g.shape[2]) for g in grads]
    scratch = [pltpu.VMEM((2, n) + q, BF) for q in quarter]
    scratch += [pltpu.VMEM((2, n) + q, BF) for q in quarter]
    scratch += [pltpu.VMEM((n,) + q, BF) for q in quarter]
    scratch += [pltpu.VMEM((2, plan.hops) + q, BF) for q in quarter]
    scratch += [pltpu.VMEM(g.shape[1:], BF) for g in grads]
    scratch += [pltpu.VMEM((quads,) + (q if quads > 1 else (8, 128)), BF) for q in quarter]
    scratch += [
        dma((count, n, 2)), dma((count,)), dma((count, n, 2)), dma((count,)), dma((count, n)), dma((count, 2)),
        dma((count, 2, plan.hops)), dma((count,)), dma((count,)), dma((count, 3)), dma((count, 3)),
    ]
    return scratch


class RowsOut:
    def __init__(self, plan, at, src, shared, dst, send, recv):
        self.plan, self.at, self.src, self.shared, self.dst, self.send, self.recv = plan, at, src, shared, dst, send, recv
        self.home = at.base + lax.div(at.m, plan.groups)
        self.first = lax.rem(at.m, plan.groups) * plan.group_rows

    def copies(self, what):
        plan, at = self.plan, self.at
        for q in range(plan.mp):
            here = jnp.logical_and(self.home == at.d, at.m == q)
            toks = pl.ds(q * plan.tok, plan.tok)
            if what == 0:
                yield q, here, True, self.src.at[pl.ds(0, plan.own), toks], self.dst.at[
                    pl.ds(self.first + plan.own * at.k, plan.own)
                ]
            else:
                holds = at.k == (q * plan.tok) // plan.part
                yield q, here, holds, self.shared.at[pl.ds((q * plan.tok) % plan.part, plan.tok)], self.dst.at[
                    self.first + plan.own * plan.share
                ]

    def start(self, what):
        for q, here, wanted, src, dst in self.copies(what):

            @pl.when(jnp.logical_and(here, wanted))
            def _():
                pltpu.make_async_copy(src, dst, self.recv.at[0]).start()

            @pl.when(jnp.logical_and(jnp.logical_not(here), wanted))
            def _():
                remote(src, dst, self.send.at[q, what], self.recv.at[0], dp=self.home, mp=q).start()

    def finish(self):
        settle(self.dst, self.recv.at[0])
        for what in range(2):
            for q, here, wanted, src, dst in self.copies(what):

                @pl.when(jnp.logical_and(jnp.logical_not(here), wanted))
                def _():
                    settle(src, self.send.at[q, what])


def reduce_kernel(plan, x0, x1, x2, x3, out3, tg3, vec, o0, o1, o2, o3, blk, tg, vout, *rest):
    share, own, part = plan.share, plan.own, plan.part
    grads, outs = (x0, x1, x2, x3), (o0, o1, o2, o3)
    groups = [rest[4 * i : 4 * i + 4] for i in range(6)]
    sems, rest = rest[24:35], rest[35:]
    fout, rest = rest[:4], rest[4:]
    (
        tgs, tgo, vrc, vsum, out_sem, blk_send, blk_recv, tg_send, tg_recv, tgs_send, tgs_recv, tgl_sem,
        v_send, v_recv,
    ) = rest
    at = Place(plan)
    red = Reducer(plan, at, grads, *groups, sems)
    blocks = RowsOut(plan, at, out3, out3.at[own], blk, blk_send, blk_recv)
    tokens = RowsOut(plan, at, tg3, tgo, tg, tg_send, tg_recv)
    greet(plan, at, True)
    me = at.d * plan.mp + at.m

    for w in range(4):
        red.begin(w)
    for i in range(share):
        src = tg3.at[own, pl.ds(i * part, part)]
        if i == 0:
            pltpu.make_async_copy(src, tgs.at[0], tgl_sem.at[0]).start()
        else:
            to = at.base + lax.rem(at.k + i, share)
            remote(src, tgs.at[share - i], tgs_send.at[i], tgs_recv.at[share - i], dp=to).start()

    def vector(phase, src_of, dst):
        def one(i, carry):
            to = lax.rem(me + i, plan.all)
            remote(
                src_of(to), dst.at[me], v_send.at[phase], v_recv.at[phase], dp=lax.div(to, plan.mp), mp=lax.rem(to, plan.mp)
            ).start()
            return carry

        lax.fori_loop(1, plan.all, one, 0)
        pltpu.make_async_copy(src_of(me), dst.at[me], v_recv.at[phase]).start()

    vector(0, lambda to: vec.at[to], vrc)
    blocks.start(0)
    blocks.start(1)
    tokens.start(0)
    for w in range(4):
        red.first(w, 0)
    settle(vrc, v_recv.at[0])
    vsum[...] = jnp.sum(vrc[...], axis=0)
    vector(1, lambda to: vsum, vout)
    for i in range(1, share):
        settle(tgs.at[i], tgs_recv.at[i])
    settle(tgs.at[0], tgl_sem.at[0])
    tgo[...] = sum(tgs[i].astype(F32) for i in range(share)).astype(BF)
    tokens.start(1)
    count = len(red.order)
    for i in range(count):
        for w in range(4):
            if i + 1 < count:
                red.first(w, i + 1)
            red.step(w, i)
    for w in range(4):
        red.last(w)
    for w in range(4):
        red.spread(w)
    for w in range(4):
        red.arrived(w)
        fout[w][...] = red.fin[w][...].astype(F32)
        pltpu.make_async_copy(fout[w], outs[w], out_sem.at[w]).start()
    for w in range(4):
        red.finish(w)
        settle(fout[w], out_sem.at[w])
    for i in range(1, share):
        settle(tgs.at[0], tgs_send.at[i])
    blocks.finish()
    tokens.finish()
    settle(vout, v_recv.at[1])
    for phase in range(2):
        settle(vout.at[pl.ds(0, plan.all - 1)], v_send.at[phase])


def reduce_out(plan, grads, out3, tg3, vec):
    n, share = plan.mp, plan.share
    width = out3.shape[2]
    any_space = pl.BlockSpec(memory_space=pl.ANY)
    dma = pltpu.SemaphoreType.DMA
    rows = jax.ShapeDtypeStruct((plan.rows_dev, plan.tok, width), BF)
    return pl.pallas_call(
        functools.partial(reduce_kernel, plan),
        out_shape=(
            *[jax.ShapeDtypeStruct(g.shape[1:], F32) for g in grads],
            rows,
            rows,
            jax.ShapeDtypeStruct(vec.shape, F32),
        ),
        in_specs=[any_space] * 7,
        out_specs=[any_space] * 7,
        scratch_shapes=[
            *reducer_scratch(plan, grads),
            *[pltpu.VMEM(g.shape[1:], F32) for g in grads],
            pltpu.VMEM((share, plan.part, width), BF),
            pltpu.VMEM((plan.part, width), BF),
            pltpu.VMEM(vec.shape, F32),
            pltpu.VMEM(vec.shape[1:], F32),
            dma((4,)), dma((n, 2)), dma((1,)), dma((n, 2)), dma((1,)), dma((share,)), dma((share,)), dma((1,)),
            dma((2,)), dma((2,)),
        ],
        compiler_params=pltpu.CompilerParams(
            collective_id=1, has_side_effects=True, vmem_limit_bytes=60 << 20
        ),
        name="reduce",
    )(*grads, out3, tg3, vec)


def scores_of(query, key, allowed):
    raw = lax.dot_general(query, key, (((1,), (1,)), ((), ())), preferred_element_type=F32)
    scores = jnp.where(allowed, raw * HEAD_DIM ** (-0.5), MASKED)
    raised = jnp.exp(scores - jnp.max(scores, axis=-1, keepdims=True))
    return raised / jnp.sum(raised, axis=-1, keepdims=True)


def attend_kernel(heads, proj, seg_col, seg_row, out):
    allowed = seg_col[0] == seg_row[0]
    for h in range(heads):
        at = h * 3 * HEAD_DIM
        query, key, value = (proj[0, :, at + i * HEAD_DIM : at + (i + 1) * HEAD_DIM] for i in range(3))
        probs = scores_of(query, key, allowed).astype(BF)
        mixed = jnp.dot(probs, value, preferred_element_type=F32)
        out[0, :, h * HEAD_DIM : (h + 1) * HEAD_DIM] = mixed.astype(BF)


def attend(proj, seg):
    rows, seq, width3 = proj.shape
    heads = width3 // (3 * HEAD_DIM)
    return pl.pallas_call(
        functools.partial(attend_kernel, heads),
        out_shape=jax.ShapeDtypeStruct((rows, seq, width3 // 3), BF),
        grid=(rows,),
        in_specs=[
            pl.BlockSpec((1, seq, width3), lambda r: (r, 0, 0)),
            pl.BlockSpec((1, seq, 1), lambda r: (r, 0, 0)),
            pl.BlockSpec((1, 1, seq), lambda r: (r, 0, 0)),
        ],
        out_specs=pl.BlockSpec((1, seq, width3 // 3), lambda r: (r, 0, 0)),
        name="attend",
    )(proj, seg[:, :, None], seg[:, None, :])


def attend_back_kernel(heads, proj, grad, seg_col, seg_row, out):
    allowed = seg_col[0] == seg_row[0]
    across = (((1,), (1,)), ((), ()))
    down = (((0,), (0,)), ((), ()))
    for h in range(heads):
        at = h * 3 * HEAD_DIM
        query, key, value = (proj[0, :, at + i * HEAD_DIM : at + (i + 1) * HEAD_DIM] for i in range(3))
        head_grad = grad[0, :, h * HEAD_DIM : (h + 1) * HEAD_DIM]
        full = scores_of(query, key, allowed)
        value_grad = lax.dot_general(full.astype(BF), head_grad, down, preferred_element_type=F32)
        probs_grad = lax.dot_general(head_grad, value, across, preferred_element_type=F32)
        delta = jnp.sum(probs_grad * full, axis=-1, keepdims=True)
        low = (jnp.where(allowed, full * (probs_grad - delta), 0.0) * HEAD_DIM ** (-0.5)).astype(BF)
        query_grad = jnp.dot(low, key, preferred_element_type=F32)
        key_grad = lax.dot_general(low, query, down, preferred_element_type=F32)
        for i, part in enumerate((query_grad, key_grad, value_grad)):
            out[0, :, at + i * HEAD_DIM : at + (i + 1) * HEAD_DIM] = part.astype(BF)


def attend_back(proj, grad, seg):
    rows, seq, width3 = proj.shape
    heads = width3 // (3 * HEAD_DIM)
    return pl.pallas_call(
        functools.partial(attend_back_kernel, heads),
        out_shape=jax.ShapeDtypeStruct((rows, seq, width3), BF),
        grid=(rows,),
        in_specs=[
            pl.BlockSpec((1, seq, width3), lambda r: (r, 0, 0)),
            pl.BlockSpec((1, seq, width3 // 3), lambda r: (r, 0, 0)),
            pl.BlockSpec((1, seq, 1), lambda r: (r, 0, 0)),
            pl.BlockSpec((1, 1, seq), lambda r: (r, 0, 0)),
        ],
        out_specs=pl.BlockSpec((1, seq, width3), lambda r: (r, 0, 0)),
        name="attend_back",
    )(proj, grad, seg[:, :, None], seg[:, None, :])


def norm(values, gain_vec, shift_vec):
    centred = values - jnp.mean(values, axis=-1, keepdims=True)
    scale = lax.rsqrt(jnp.mean(centred * centred, axis=-1, keepdims=True) + EPS)
    unit = centred * scale
    return unit, scale, unit * gain_vec + shift_vec


def norm_back(unit, scale, gain_vec, grad):
    pulled = grad * gain_vec
    inner = jnp.mean(pulled * unit, axis=-1, keepdims=True)
    return scale * (pulled - jnp.mean(pulled, axis=-1, keepdims=True) - unit * inner)


def per_device(
    plan, tokens_in, segment_ids, attn_gain, attn_shift, qkv_weight, qkv_bias, out_weight, out_bias, mlp_gain, mlp_shift,
    up_weight, up_bias, down_weight, down_bias, cotangent,
):
    n, own, seq, part = plan.mp, plan.own, plan.seq, plan.part
    width = tokens_in.shape[2]
    held = own * seq + part
    every = plan.rows * seq
    ff_local = up_weight.shape[1]
    tok3, cot3, seg_all, bias_q, bias_up, wq, wo, wu, wd = gather(
        plan, tokens_in, cotangent, segment_ids, (qkv_bias, up_bias.reshape(1, ff_local)),
        (qkv_weight, out_weight, up_weight, down_weight),
    )
    d, m = lax.axis_index("dp"), lax.axis_index("mp")
    k = lax.rem(d, plan.share)
    seg_flat = seg_all.reshape(plan.share * plan.rows_dev, seq)
    seg_own = lax.dynamic_slice(seg_flat, (m * plan.group_rows + own * k, 0), (own, seq))
    seg_last = lax.dynamic_slice(seg_flat, (m * plan.group_rows + own * plan.share, 0), (1, seq))
    seg_last = lax.dynamic_slice(jnp.concatenate([seg_last, seg_last], axis=1), (0, k * part), (1, seq))
    seg = jnp.concatenate([seg_own, seg_last], axis=0)

    heads_local = qkv_bias.shape[1] // HEAD_DIM
    bias_q = bias_q.reshape(n, 2, heads_local, HEAD_DIM)
    full_bias = jnp.stack([bias_q[:, 0], jnp.zeros_like(bias_q[:, 0]), bias_q[:, 1]], axis=2).reshape(n, -1)
    bias_up = bias_up.reshape(n, ff_local)

    tokens_f = tok3.reshape(every, width).astype(F32)
    unit_one, scale_one, normed = norm(tokens_f, attn_gain, attn_shift)
    normed_one = normed.astype(BF)
    projected = (
        (jnp.einsum("td,sdf->tsf", normed_one, wq, preferred_element_type=F32) + full_bias)
        .astype(BF)
        .reshape(plan.rows, seq, 3 * width)
    )
    attn_out = attend(projected, seg)
    attn_flat = attn_out.reshape(every, width)[:held]
    wo_full = wo.reshape(width, width)
    hidden = tokens_f[:held] + jnp.dot(attn_flat, wo_full, preferred_element_type=F32) + out_bias
    unit_two, scale_two, normed = norm(hidden, mlp_gain, mlp_shift)
    normed_two = normed.astype(BF)
    pre_act = jnp.einsum("td,sdf->tsf", normed_two, wu, preferred_element_type=F32) + bias_up
    act_low = jax.nn.gelu(pre_act, approximate=False).astype(BF)
    down_full = wd.reshape(n * ff_local, width)
    act_flat = act_low.reshape(held, n * ff_local)
    block = (hidden + jnp.dot(act_flat, down_full, preferred_element_type=F32) + down_bias).astype(BF)

    cot = cot3.reshape(every, width)[:held]
    cot_f = cot.astype(F32)
    act_grad = jnp.einsum("td,sfd->tsf", cot, wd, preferred_element_type=F32)
    down_grad = jnp.einsum("tsf,td->sfd", act_low, cot, preferred_element_type=F32).astype(BF)
    phi = 0.5 * (1.0 + lax.erf(pre_act * math.sqrt(0.5)))
    density = jnp.exp(-0.5 * pre_act * pre_act) * (1.0 / math.sqrt(2.0 * math.pi))
    pre_grad = (act_grad * (phi + pre_act * density)).astype(BF)
    up_bias_part = jnp.sum(pre_grad, axis=0, dtype=F32)
    up_grad = jnp.einsum("td,tsf->sdf", normed_two, pre_grad, preferred_element_type=F32).astype(BF)
    normed_two_grad = jnp.einsum("tsf,sdf->td", pre_grad, wu, preferred_element_type=F32)
    mlp_gain_part = jnp.sum(normed_two_grad * unit_two, axis=0)
    mlp_shift_part = jnp.sum(normed_two_grad, axis=0)
    hidden_grad = cot_f + norm_back(unit_two, scale_two, mlp_gain, normed_two_grad)
    branch_grad = hidden_grad.astype(BF)
    out_grad = jnp.einsum("th,td->hd", attn_flat, branch_grad, preferred_element_type=F32).astype(BF)
    out_grad = out_grad.reshape(n, width // n, width)
    attn_grad = jnp.einsum("td,hd->th", branch_grad, wo_full, preferred_element_type=F32).astype(BF)
    attn_grad = jnp.concatenate([attn_grad, jnp.zeros((every - held, width), BF)], axis=0)
    qkv_grads = attend_back(projected, attn_grad.reshape(plan.rows, seq, width), seg)
    qkv_flat = qkv_grads.reshape(every, n, -1)
    qkv_grad = jnp.einsum("td,tsf->sdf", normed_one, qkv_flat, preferred_element_type=F32).astype(BF)
    bias_sums = jnp.sum(qkv_flat, axis=0, dtype=F32).reshape(n, heads_local, 3, HEAD_DIM)
    qkv_bias_part = jnp.stack([bias_sums[:, :, 0], bias_sums[:, :, 2]], axis=1)
    normed_one_grad = jnp.einsum("tsf,sdf->td", qkv_flat, wq, preferred_element_type=F32)
    attn_gain_part = jnp.sum(normed_one_grad * unit_one, axis=0)
    attn_shift_part = jnp.sum(normed_one_grad, axis=0)
    token_part = norm_back(unit_one, scale_one, attn_gain, normed_one_grad)
    tokens_part = jnp.concatenate([token_part[:held] + hidden_grad, token_part[held:]], axis=0).astype(BF)

    block3 = jnp.concatenate([block, jnp.zeros((every - held, width), BF)], axis=0).reshape(plan.rows, seq, width)
    six = jnp.stack(
        [
            attn_gain_part, attn_shift_part, jnp.sum(hidden_grad, axis=0), mlp_gain_part, mlp_shift_part,
            jnp.sum(cot_f, axis=0),
        ]
    )
    six_size, up_size, qkv_size = 6 * width // plan.all, ff_local // plan.dp, 2 * width // plan.all
    up_rows = up_bias_part.reshape(n, plan.dp, up_size).swapaxes(0, 1).reshape(plan.all, up_size)
    qkv_rows = qkv_bias_part.reshape(n, plan.dp, qkv_size).swapaxes(0, 1).reshape(plan.all, qkv_size)
    vec = jnp.concatenate([six.reshape(plan.all, six_size), up_rows, qkv_rows], axis=1)
    size = vec.shape[1]
    padded = -(-size // 128) * 128
    vec = jnp.pad(vec, ((0, 0), (0, padded - size))).reshape(plan.all, padded // 128, 128)

    dq, do, du, dd, block_out, tokens_low, sums = reduce_out(
        plan, (qkv_grad, out_grad, up_grad, down_grad), block3, tokens_part.reshape(plan.rows, seq, width), vec
    )
    sums = sums.reshape(plan.all, padded)
    six = sums[:, :six_size].reshape(6, width)
    mine = lax.dynamic_index_in_dim(sums.reshape(plan.dp, n, padded), m, 1, keepdims=False)
    up_bias_grad = mine[:, six_size : six_size + up_size].reshape(ff_local)
    qkv_bias_grad = mine[:, six_size + up_size : size].reshape(2, width // n)
    tokens_grad = tokens_low.astype(F32)
    return (
        block_out, tokens_grad, six[0], six[1], dq, qkv_bias_grad, do, six[2], six[3], six[4], du, up_bias_grad, dd, six[5],
    )


def solution(mesh):
    dp, mp = mesh.shape["dp"], mesh.shape["mp"]
    rows_spec = P("dp", "mp", None)
    in_specs = (
        rows_spec, P("dp", None), P(), P(), P(None, "mp"), P(None, "mp"), P("mp", None), P(), P(), P(),
        P(None, "mp"), P("mp"), P("mp", None), P(), rows_spec,
    )
    out_specs = (
        rows_spec, rows_spec, P(), P(), P(None, "mp"), P(None, "mp"), P("mp", None), P(), P(), P(),
        P(None, "mp"), P("mp"), P("mp", None), P(),
    )

    def run(tokens_in, segment_ids, *rest):
        rows_all, seq_len, _ = tokens_in.shape
        plan = Plan(dp, mp, rows_all // dp, seq_len // mp, seq_len)
        return jax.shard_map(
            functools.partial(per_device, plan), mesh=mesh, in_specs=in_specs, out_specs=out_specs, check_vma=False
        )(tokens_in, segment_ids, *rest)

    return run
```

time: 723 us -> 595 us (0.82)
  blocking collectives: 84.8 us -> 0 us
  Pallas kernels: 445 us -> 411 us
    psum x1 -> x0, blocking collectives: 51.8 us -> none  [per_device(): sums = lax.psum(sums, ('dp', 'mp'))]
    all_gather x2 -> x0, blocking collectives: 33.1 us -> none  [the longest x1 21.9 us: per_device(): bias_up = lax.all_gather(up_bias, 'mp', axis=0)]
    pallas_call x1, Pallas kernels: 191 us -> 170 us  [gather(): pl.pallas_call(functools.partial(gather_kernel, plan), out_shape=(rows, r...]
    pallas_call x1, Pallas kernels: 204 us -> 191 us  [reduce_out(): pl.pallas_call(functools.partial(reduce_kernel, plan), out_shape=(*[jax.S...]
    unnamed x111 -> x107, local copies, waits for them, and re-layouts: 15.7 us -> 12.7 us
where the time goes in v2:
time: 595 us; the launch traced here: 588 us
  Pallas kernels  411 us (69%)
  matrix products  96 us (16%)
  other arithmetic  44.4 us (7%)
  local copies, waits for them, and re-layouts  34.4 us (6%)
    pallas_call x1, Pallas kernels, reduce_out(): pl.pallas_call(functools.partial(reduce_kernel, plan), out_shape=(*[jax.S...  191 us
    pallas_call x1, Pallas kernels, gather(): pl.pallas_call(functools.partial(gather_kernel, plan), out_shape=(rows, r...  170 us
    pallas_call x1, Pallas kernels, attend_back(): pl.pallas_call(functools.partial(attend_back_kernel, heads), out_shape=ja...  32.1 us
    convert_element_type x1, other arithmetic, per_device(): act_low = jax.nn.gelu(pre_act, approximate=False).astype(BF)  25.8 us
    pallas_call x1, Pallas kernels, attend(): pl.pallas_call(functools.partial(attend_kernel, heads), out_shape=jax.Sha...  18.5 us
    dot_general x1, matrix products, per_device(): act_grad = jnp.einsum('td,sfd->tsf', cot, wd, preferred_element_type=F32)  15.3 us
    unnamed x107, local copies, waits for them, and re-layouts  12.7 us
    dot_general x1, matrix products, per_device(): jnp.einsum('tsf,sdf->td', qkv_flat, wq, preferred_element_type=F32)  12.2 us

profile of v2, /device:TPU:11, one launch (start us, length us, event | category | flops | bytes accessed | tf_op | source)
XLA Modules:
  0.0 588.0 jit_solution(16994246754242366427)
XLA Ops:
  0.7 170.2 %gather.1 = (bf16[3,256,1024]{2,1,0:T(8,128)(2,1)}, bf16[3,256,1024]{2,1,0:T(8,128)(2,1)}, s32[2,20,256]{2,1,0:T(8,128)}, f32[8,2,128]{2,1,0:T(2,128)}, f32[8,1,...) custom-call(bf16[20,32,1024]{2,1,0:T(8,128)(2,1)} %tok.1, ...), custom_call_target="tpu_custom_call" | custom-call | tf_op jit(solution)/shard_map/gather/pallas_call | solution.py:264
  173.4 1.7 convert_reduce_fusion.3
  176.7 8.4 %add_convert_fusion = bf16[768,8,384]{2,0,1:T(8,128)(2,1)S(1)} fusion(f32[8,384]{1,0:T(8,128)S(1)} %add.128, bf16[8,1024,384]{2,1,0:T(8,128)(2,1)} %get-tuple-element.31, f32[1024]{0:T(1024)S(1)} %copy-done.34, f32[1024]{0:T(1024)S(1)} %copy-done.24, f32[768]{0:T(1024)S(1)} %rsqrt.21, f32[768]{0:T(1024)S(1)} %div.27, bf16[768,1024]{1,0:T(8,128)(2,1)S(1)} %bitcast.131), kind=kOutput, calls=%fused_computation.31 | convolution fusion | flops 4841275392 | bytes 12609536 | tf_op jit(solution)/shard_map/td,sdf->tsf/dot_general | solution.py:735
  185.1 5.0 copy.53
  190.1 8.3 %reshape.193.proj = bf16[3,256,3072]{2,1,0:T(8,128)(2,1)} reshape(bf16[768,8,384]{2,1,0:T(8,128)(2,1)} %copy.53) | data formatting | bytes 9437184 | tf_op jit(solution)/shard_map/reshape | solution.py:737
  198.4 18.5 %attend.1 = bf16[3,256,1024]{2,1,0:T(8,128)(2,1)} custom-call(bf16[3,256,3072]{2,1,0:T(8,128)(2,1)} %reshape.193.proj, s32[3,256,1]{2,1,0:T(8,128)} %copy.54.seg_col, s32[3,1,256]{2,1,0:T(1,128)} %broadcast_in_dim.5.seg_row), custom_call_target="tpu_custom_call" | custom-call | tf_op jit(solution)/shard_map/attend/pallas_call | solution.py:641
  219.1 1.7 fusion.55
  221.7 11.4 %fusion.29 = (u8[640,512]{1,0:T(8,128)(4,1)S(1)}, u8[640,512]{1,0:T(8,128)(4,1)}, f32[640,8,512]{2,0,1:T(8,128)}) fusion(f32[8,512]{1,0:T(8,128)S(1)} %bitcast.149, bf16[8,1024,512]{2,1,0:T(8,128)(2,1)S(1)} %bitcast.176, f32[640,1024]{1,0:T(8,128)S(1)} %get-tuple-element.72, f32[1024]{0:T(1024)S(1)} %copy-done.39, f32[1024]{0:T(1024)S(1)} %copy-done.32, ...), kind=kOutput, calls=%fused_computation.67 | convolution fusion | flops 5408030720 | bytes 22180864 | tf_op jit(solution)/shard_map/td,sdf->tsf/dot_general | solution.py:745
  233.1 15.3 %convert_reduce_fusion = (f32[8,512]{1,0:T(8,128)}, bf16[640,8,512]{2,0,1:T(8,128)(2,1)}) fusion(f32[640,8,512]{2,0,1:T(8,128)} %get-tuple-element.74, f32[8,512]{1,0:T(8,128)S(1)} %bitcast.150, bf16[8,512,1024]{2,1,0:T(8,128)(2,1)} %get-tuple-element.36, bf16[768,1024]{1,0:T(8,128)(2,1)S(1)} %bitcast.144), kind=kOutput, calls=%fused_computation.16 | convolution fusion | flops 5402783744 | bytes 25460736 | tf_op jit(solution)/shard_map/td,sfd->tsf/dot_general | solution.py:753
  248.4 10.3 %fusion.27 = (f32[1024]{0:T(1024)S(1)}, f32[640]{0:T(1024)S(1)}, f32[640]{0:T(1024)S(1)}, f32[1024]{0:T(1024)S(1)}, f32[640,1024,1]{1,0,2:T(8,128)S(1)}) fusion(f32[640,1024]{1,0:T(8,128)S(1)} %get-tuple-element.72, f32[640]{0:T(1024)S(1)} %add_rsqrt_fusion, f32[640]{0:T(1024)S(1)} %broadcast_multiply_fusion.4, f32[1024]{0:T(1024)S(1)} %copy-done.32, ...), kind=kOutput, calls=%fused_computation.62 | convolution fusion | flops 5374604288 | bytes 18896896 | tf_op jit(solution)/shard_map/tsf,sdf->td/dot_general | solution.py:760
  260.2 1.6 convolution_convert_fusion.2
  263.1 32.1 %attend_back.1 = bf16[3,256,3072]{2,1,0:T(8,128)(2,1)} custom-call(bf16[3,256,3072]{2,1,0:T(8,128)(2,1)} %reshape.193.proj, bf16[3,256,1024]{2,1,0:T(8,128)(2,1)} %bitcast.135, s32[3,256,1]{2,1,0:T(8,128)} %copy.54.seg_col, s32[3,1,256]{2,1,0:T(1,128)} %broadcast_in_dim.5.seg_row), custom_call_target="tpu_custom_call" | custom-call | tf_op jit(solution)/shard_map/attend_back/pallas_call | solution.py:677
  295.2 3.5 copy.73
  298.8 12.2 %fusion.21 = (f32[1024]{0:T(1024)S(1)}, f32[768]{0:T(1024)}, f32[768]{0:T(1024)}, f32[1024]{0:T(1024)S(1)}, f32[768,1024,1]{1,0,2:T(8,128)}) fusion(f32[768]{0:T(1024)S(1)} %rsqrt.21, f32[768]{0:T(1024)S(1)} %div.27, bf16[3,256,1024]{2,1,0:T(8,128)(2,1)S(1)} %copy-done, f32[1024]{0:T(1024)S(1)} %copy-done.24, bf16[8,1024,384]{2,1,0:T(8,128)(2,1)} %get-tuple-element.31, ...), kind=kOutput, calls=%fused_computation.44 | convolution fusion | flops 4839698432 | bytes 15753216 | tf_op jit(solution)/shard_map/tsf,sdf->td/dot_general | solution.py:774
  311.1 3.2 convert_reduce_fusion.1
  317.3 3.0 subtract_multiply_fusion
  322.8 25.8 %fusion.8 = bf16[640,8,512]{2,0,1:T(8,128)(2,1)S(1)} fusion(f32[640,8,512]{2,0,1:T(8,128)} %get-tuple-element.74, f32[8,512]{1,0:T(8,128)S(1)} %bitcast.151, u8[640,512]{1,0:T(8,128)(4,1)S(1)} %copy-done.14, u8[640,512]{1,0:T(8,128)(4,1)S(1)} %get-tuple-element.46), kind=kLoop, calls=%fused_computation.10 | loop fusion | flops 186122240 | bytes 16400384 | tf_op jit(solution)/shard_map/convert_element_type | solution.py:746
  348.6 5.6 fusion.26
  355.5 9.3 %convolution_convert_fusion.x3 = bf16[8,512,1024]{2,1,0:T(8,128)(2,1)} fusion(bf16[640,8,512]{2,0,1:T(8,128)(2,1)S(1)} %fusion.8, bf16[768,1024]{1,0:T(8,128)(2,1)S(1)} %bitcast.146), kind=kOutput, calls=%fused_computation.33 | convolution fusion | flops 5372903424 | bytes 14942208 | tf_op jit(solution)/shard_map/tsf,td->sfd/dot_general | solution.py:754
  364.9 9.9 %convert_bitcast_fusion.x2 = bf16[8,1024,512]{2,1,0:T(8,128)(2,1)} fusion(bf16[640,8,512]{2,0,1:T(8,128)(2,1)S(1)} %bitcast.180, f32[640,1024]{1,0:T(8,128)S(1)} %copy-done.4, f32[1024]{0:T(1024)S(1)} %copy-done.40, f32[1024]{0:T(1024)S(1)} %copy-done.33, f32[640]{0:T(1024)S(1)} %copy-done.28, f32[640]{0:T(1024)S(1)} %copy-done.21), kind=kOutput, calls=%fused_computation.32 | convolution fusion | flops 5376180224 | bytes 16266240 | tf_op jit(solution)/shard_map/td,tsf->sdf/dot_general | solution.py:759
  374.9 3.2 convolution_convert_fusion.1
  378.7 7.2 %convert_bitcast_fusion.1.x0 = bf16[8,1024,384]{2,1,0:T(8,128)(2,1)} fusion(bf16[768,1024,1]{1,0,2:T(8,128)(2,1)S(1)} %bitcast.141, bf16[768,8,384]{2,1,0:T(8,128)(2,1)S(1)} %bitcast.139), kind=kOutput, calls=%fused_computation.34 | convolution fusion | flops 4834983936 | bytes 12582912 | tf_op jit(solution)/shard_map/td,tsf->sdf/dot_general | solution.py:771
  385.9 190.6 %reduce.8 = (f32[1024,384]{1,0:T(8,128)}, f32[128,1024]{1,0:T(8,128)}, f32[1024,512]{1,0:T(8,128)}, f32[512,1024]{1,0:T(8,128)}, bf16[20,32,1024]{2,1,0:T(8,128)...) custom-call(bf16[8,1024,384]{2,1,0:T(8,128)(2,1)} %convert_bitcast_fusion.1.x0, ...), custom_call_target="tpu_custom_call" | custom-call | tf_op jit(solution)/shard_map/reduce/pallas_call | solution.py:594
  576.5 3.3 convert_element_type.97
  (157 shorter events, 25.1 us)
Async XLA Ops:
  170.9 5.8 copy-start.24
  175.1 10.0 %copy-start.18 = (f32[3,256]{1,0:T(4,128)}, f32[3,256]{1,0:T(4,128)S(1)}, u32[]{:S(2)}) copy-start(f32[3,256]{1,0:T(4,128)S(1)} %broadcast_multiply_fusion.5) | copy-start | bytes 9220
  176.3 122.4 %copy-start.26 = (f32[768]{0:T(1024)}, f32[768]{0:T(1024)S(1)}, u32[]{:S(2)}) copy-start(f32[768]{0:T(1024)S(1)} %rsqrt.21) | copy-start | bytes 9220
  176.7 122.1 %copy-start.29 = (f32[768]{0:T(1024)}, f32[768]{0:T(1024)S(1)}, u32[]{:S(2)}) copy-start(f32[768]{0:T(1024)S(1)} %div.27) | copy-start | bytes 9220
  220.7 38.0 %copy-start.3 = (f32[640,1024]{1,0:T(8,128)}, f32[640,1024]{1,0:T(8,128)S(1)}, u32[]{:S(2)}) copy-start(f32[640,1024]{1,0:T(8,128)S(1)} %get-tuple-element.72) | copy-start | bytes 7864324
  220.7 38.0 %copy-start.20 = (f32[640]{0:T(1024)}, f32[640]{0:T(1024)S(1)}, u32[]{:S(2)}) copy-start(f32[640]{0:T(1024)S(1)} %broadcast_multiply_fusion.4) | copy-start | bytes 7684
  221.2 37.6 %copy-start.27 = (f32[640]{0:T(1024)}, f32[640]{0:T(1024)S(1)}, u32[]{:S(2)}) copy-start(f32[640]{0:T(1024)S(1)} %add_rsqrt_fusion) | copy-start | bytes 7684
  221.2 11.9 %copy-start.16 = (f32[8,1,512]{2,0,1:T(8,128)}, f32[8,1,512]{2,0,1:T(8,128)S(1)}, u32[]{:S(2)}) copy-start(f32[8,1,512]{2,0,1:T(8,128)S(1)} %copy.87) | copy-start | bytes 49156
  221.7 11.4 %copy-start.11 = (bf16[3,256,1024]{2,1,0:T(8,128)(2,1)S(1)}, bf16[3,256,1024]{2,1,0:T(8,128)(2,1)}, u32[]{:S(2)}) copy-start(bf16[3,256,1024]{2,1,0:T(8,128)(2,1)} %get-tuple-element.33) | copy-start | bytes 4718596
  298.7 12.3 %copy-start.5 = (bf16[96,8,8,384]{3,2,1,0:T(8,128)(2,1)}, bf16[96,8,8,384]{3,2,1,0:T(8,128)(2,1)S(1)}, u32[]{:S(2)}) copy-start(bf16[96,8,8,384]{3,2,1,0:T(8,128)(2,1)S(1)} %copy.73) | copy-start | bytes 14155780
  320.2 28.3 %slice-start.2 = ((s8[8388608]{0:T(1024)(128)(4,1)}), s8[4194304]{0:T(1024)(128)(4,1)S(1)}, s32[]{:S(2)}) async-start(s8[8388608]{0:T(1024)(128)(4,1)} %bitcast.173), calls=%async_computation.2 | async-start | bytes 8388608
  322.8 25.8 %copy-start.4 = (f32[640,1024]{1,0:T(8,128)S(1)}, f32[640,1024]{1,0:T(8,128)}, u32[]{:S(2)}) copy-start(f32[640,1024]{1,0:T(8,128)} %copy-done.3) | copy-start | bytes 7864324
  322.8 25.8 %slice-start.3 = ((s8[8388608]{0:T(1024)(128)(4,1)}), s8[4194304]{0:T(1024)(128)(4,1)S(1)}, s32[]{:S(2)}) async-start(s8[8388608]{0:T(1024)(128)(4,1)} %bitcast.173), calls=%async_computation.3 | async-start | bytes 8388608
  322.8 25.8 %copy-start.38 = (f32[1024]{0:T(1024)S(1)}, f32[1024]{0:T(1024)}, u32[]{:S(2)}) copy-start(f32[1024]{0:T(1024)} %param.28) | copy-start | bytes 12292
  348.6 6.9 %copy-start.12 = (bf16[3,256,1024]{2,1,0:T(8,128)(2,1)S(1)}, bf16[3,256,1024]{2,1,0:T(8,128)(2,1)}, u32[]{:S(2)}) copy-start(bf16[3,256,1024]{2,1,0:T(8,128)(2,1)} %get-tuple-element.33) | copy-start | bytes 4718596
  354.2 10.7 %slice-start.6 = ((s8[5242880]{0:T(1024)(128)(4,1)}), s8[4194304]{0:T(1024)(128)(4,1)S(1)}, s32[]{:S(2)}) async-start(s8[5242880]{0:T(1024)(128)(4,1)} %bitcast.179), calls=%async_computation.6 | async-start | bytes 8388608
  355.5 9.3 %copy-start.21 = (f32[640]{0:T(1024)S(1)}, f32[640]{0:T(1024)}, u32[]{:S(2)}) copy-start(f32[640]{0:T(1024)} %copy-done.20) | copy-start | bytes 7684
  355.5 9.3 %copy-start.28 = (f32[640]{0:T(1024)S(1)}, f32[640]{0:T(1024)}, u32[]{:S(2)}) copy-start(f32[640]{0:T(1024)} %copy-done.27) | copy-start | bytes 7684
  355.5 9.3 %copy-start.33 = (f32[1024]{0:T(1024)S(1)}, f32[1024]{0:T(1024)}, u32[]{:S(2)}) copy-start(f32[1024]{0:T(1024)} %param.23) | copy-start | bytes 12292
  355.5 9.3 %copy-start.40 = (f32[1024]{0:T(1024)S(1)}, f32[1024]{0:T(1024)}, u32[]{:S(2)}) copy-start(f32[1024]{0:T(1024)} %param.24) | copy-start | bytes 12292
  355.5 9.3 %slice-start.7 = ((s8[5242880]{0:T(1024)(128)(4,1)}), s8[1048576]{0:T(1024)(128)(4,1)S(1)}, s32[]{:S(2)}) async-start(s8[5242880]{0:T(1024)(128)(4,1)} %bitcast.179), calls=%async_computation.7 | async-start | bytes 2097152
  355.5 23.2 %slice-start = ((s8[4718592]{0:T(1024)(128)(4,1)}), s8[524288]{0:T(1024)(128)(4,1)S(1)}, s32[]{:S(2)}) async-start(s8[4718592]{0:T(1024)(128)(4,1)} %bitcast.137), calls=%async_computation | async-start | bytes 1048576
  364.9 13.9 %slice-start.1 = ((s8[4718592]{0:T(1024)(128)(4,1)}), s8[4194304]{0:T(1024)(128)(4,1)S(1)}, s32[]{:S(2)}) async-start(s8[4718592]{0:T(1024)(128)(4,1)} %bitcast.137), calls=%async_computation.1 | async-start | bytes 8388608
  576.5 6.5 %copy-start.8 = (f32[1024,384]{1,0:T(8,128)S(1)}, f32[1024,384]{1,0:T(8,128)}, u32[]{:S(2)}) copy-start(f32[1024,384]{1,0:T(8,128)} %get-tuple-element.98) | copy-start | bytes 4718596
  (25 other events, 75.0 us)

commit v3 on v2

v3 whole, which is shorter than its diff:
```python
import functools
import math

import jax
import jax.numpy as jnp
from jax import lax
from jax.experimental import pallas as pl
from jax.experimental.pallas import tpu as pltpu
from jax.sharding import PartitionSpec as P

HEAD_DIM = 64
EPS = 1e-06
MASKED = -1000000000.0
MESH = pl.DeviceIdType.MESH
BF = jnp.bfloat16
F32 = jnp.float32


class Plan:
    def __init__(self, dp, mp, rows_dev, tok_local, seq_len):
        self.dp, self.mp, self.rows_dev, self.tok, self.seq = dp, mp, rows_dev, tok_local, seq_len
        self.share = mp // math.gcd(rows_dev, mp)
        self.group_rows = rows_dev * self.share // mp
        self.own = self.group_rows // self.share
        if self.share % 2 or dp % self.share or dp % 4 or self.group_rows != self.own * self.share + 1:
            raise ValueError("unsupported sizes")
        self.groups = mp // self.share
        self.part = seq_len // self.share
        self.rows = self.own + 1
        self.hops = mp // 2
        self.all = dp * mp

    def ring_at(self, p):
        p = lax.rem(p, self.mp)
        back = lax.div(p, self.mp // 2)
        return 2 * p * (1 - back) + (2 * self.mp - 1 - 2 * p) * back


class Place:
    def __init__(self, plan):
        d, m = lax.axis_index("dp"), lax.axis_index("mp")
        odd = lax.rem(m, 2)
        self.d, self.m = d, m
        self.p = lax.div(m, 2) * (1 - odd) + (plan.mp - 1 - lax.div(m, 2)) * odd
        self.core = lax.rem(d, 2)
        self.sib = d + 1 - 2 * self.core
        self.y = lax.rem(lax.div(d, 2), 2)
        self.other = d + 2 - 4 * self.y
        self.k = lax.rem(d, plan.share)
        self.base = d - self.k
        self.quarter = 2 * self.y + self.core
        self.neighbour = (plan.ring_at(self.p + 1), plan.ring_at(self.p + plan.mp - 1))

    def away(self, plan, way, s):
        return plan.ring_at(self.p + plan.mp - s if way == 0 else self.p + s)


def greet(plan, at, everyone):
    barrier = pltpu.get_barrier_semaphore()
    span = plan.dp if everyone else max(plan.share, 4)
    base = lax.div(at.d, span) * span

    def one(i, carry):
        e, q = base + lax.div(i, plan.mp), lax.rem(i, plan.mp)

        @pl.when(jnp.logical_or(e != at.d, q != at.m))
        def _():
            pl.semaphore_signal(barrier, inc=1, device_id={"dp": e, "mp": q}, device_id_type=MESH)

        return carry

    lax.fori_loop(0, span * plan.mp, one, 0)
    pl.semaphore_wait(barrier, span * plan.mp - 1)


def remote(src, dst, send, recv, **to):
    return pltpu.make_async_remote_copy(src, dst, send, recv, device_id=to, device_id_type=MESH)


def settle(ref, sem):
    pltpu.make_async_copy(ref, ref, sem).wait()


def piece(ref, quarter, half=None):
    rows, cols = ref.shape[0] // 4, ref.shape[1]
    first = quarter * rows
    if half is None:
        return ref.at[pl.ds(pl.multiple_of(first, rows), rows)]
    if cols % 256 == 0:
        return ref.at[pl.ds(pl.multiple_of(first, rows), rows), pl.ds(half * (cols // 2), cols // 2)]
    return ref.at[pl.ds(pl.multiple_of(first + half * (rows // 2), rows // 2), rows // 2)]


def half_of(ref, half):
    rows, cols = ref.shape
    if cols % 256 == 0:
        return ref.at[:, pl.ds(half * (cols // 2), cols // 2)]
    return ref.at[pl.ds(half * (rows // 2), rows // 2)]


class Gatherer:
    def __init__(self, plan, at, shards, full, sems):
        self.plan, self.at, self.shards, self.full = plan, at, shards, full
        self.own_sem, self.ring_send, self.ring_recv, self.y_send, self.y_recv, self.sib_send, self.sib_recv = sems

    def _half(self, way, s):
        return way if s == self.plan.hops - 1 else None

    def ring(self, w, way, s):
        at, origin = self.at, self.at.away(self.plan, way, s)
        half = self._half(way, s)
        dst = piece(self.full[w].at[origin], at.quarter, half)
        src = piece(self.shards[w], at.quarter, half) if s == 0 else dst
        return remote(src, dst, self.ring_send.at[w, way], self.ring_recv.at[w, way, s], mp=at.neighbour[way])

    def cross(self, w, way, s):
        at, origin = self.at, self.at.away(self.plan, way, s + 1)
        block = piece(self.full[w].at[origin], at.quarter, self._half(way, s))
        return remote(block, block, self.y_send.at[w], self.y_recv.at[w, way, s], dp=at.other)

    def give(self, w, way, s, mine):
        at, origin = self.at, self.at.away(self.plan, way, s + 1)
        quarter = at.quarter if mine else 2 - 2 * at.y + at.core
        block = piece(self.full[w].at[origin], quarter, self._half(way, s))
        return remote(block, block, self.sib_send.at[w], self.sib_recv.at[w], dp=at.sib)

    def begin(self, w):
        for way in range(2):
            self.ring(w, way, 0).start()
        pltpu.make_async_copy(self.shards[w], self.full[w].at[self.at.m], self.own_sem.at[w]).start()

    def step(self, w, s):
        for way in range(2):
            self.ring(w, way, s).wait_recv()
            if s < self.plan.hops - 1:
                self.ring(w, way, s + 1).start()
            self.cross(w, way, s).start()
            self.give(w, way, s, True).start()

    def follow(self, w, s):
        for way in range(2):
            self.cross(w, way, s).wait_recv()
            self.give(w, way, s, False).start()

    def arrived(self, w):
        n, rows = self.plan.mp, self.shards[w].shape[0]
        settle(self.full[w].at[pl.ds(0, n - 1), pl.ds(0, rows // 2)], self.sib_recv.at[w])
        settle(self.shards[w], self.own_sem.at[w])

    def finish(self, w):
        n, rows = self.plan.mp, self.shards[w].shape[0]
        settle(self.full[w].at[pl.ds(0, n - 1), pl.ds(0, rows // 2)], self.sib_send.at[w])
        settle(self.full[w].at[pl.ds(0, n - 1), pl.ds(0, rows // 4)], self.y_send.at[w])
        for way in range(2):
            settle(self.full[w].at[pl.ds(0, self.plan.hops - 1), pl.ds(0, rows // 4)], self.ring_send.at[w, way])
            settle(piece(self.full[w].at[0], 0, way), self.ring_send.at[w, way])


def gatherer_sems(plan, count):
    dma = pltpu.SemaphoreType.DMA
    return [
        dma((count,)), dma((count, 2)), dma((count, 2, plan.hops)), dma((count,)), dma((count, 2, plan.hops)),
        dma((count,)), dma((count,)),
    ]


class RowsIn:
    def __init__(self, plan, at, src, dst, send, recv, whole_shared):
        self.plan, self.at, self.src, self.dst, self.send, self.recv = plan, at, src, dst, send, recv
        self.whole_shared = whole_shared

    def copies(self):
        plan, at = self.plan, self.at
        mine = pl.ds(pl.multiple_of(at.m * plan.tok, plan.tok), plan.tok)
        for j in range(plan.groups):
            q = at.k * plan.groups + j
            first = j * plan.group_rows
            for e in range(plan.share):
                here = jnp.logical_and(at.k == e, at.m == q)
                holds = True if self.whole_shared else lax.div(at.m * plan.tok, plan.part) == e
                to = lax.rem(at.m * plan.tok + plan.seq - e * plan.part, plan.seq)
                to = pl.ds(pl.multiple_of(to, plan.tok), plan.tok)
                yield here, True, q, e, j, 0, self.src.at[pl.ds(first + plan.own * e, plan.own)], self.dst.at[
                    pl.ds(0, plan.own), mine
                ]
                yield here, holds, q, e, j, 1, self.src.at[first + plan.own * plan.share], self.dst.at[plan.own, to]

    def start(self, only=None):
        for here, wanted, q, e, j, what, src, dst in self.copies():
            if only is not None and only != j:
                continue

            @pl.when(jnp.logical_and(here, wanted))
            def _():
                pltpu.make_async_copy(src, dst, self.recv.at[what]).start()

            @pl.when(jnp.logical_and(jnp.logical_not(here), wanted))
            def _():
                remote(src, dst, self.send.at[j, e, what], self.recv.at[what], dp=self.at.base + e, mp=q).start()

    def arrived(self):
        plan = self.plan
        settle(self.dst.at[pl.ds(0, plan.own)], self.recv.at[0])
        extent = plan.seq if self.whole_shared else plan.part
        settle(self.dst.at[plan.own, pl.ds(0, extent)], self.recv.at[1])

    def finish(self):
        for here, wanted, q, e, j, what, src, dst in self.copies():

            @pl.when(jnp.logical_and(jnp.logical_not(here), wanted))
            def _():
                settle(src, self.send.at[j, e, what])


def run(count, body, table):
    def one(j, carry):
        for when, thunks in sorted(table.items()):

            @pl.when(j == when)
            def _():
                for thunk in thunks:
                    thunk()

        body(j)
        return carry

    lax.fori_loop(0, count, one, 0)


def spread_over(count, thunks, first=0):
    table = {}
    for i, thunk in enumerate(thunks):
        table.setdefault(first + i * (count - first) // len(thunks), []).append(thunk)
    return table


def norm_rows(values, gain_vec, shift_vec):
    unit, _, normed = norm(values, gain_vec, shift_vec)
    return normed


def forward_kernel(
    plan, heads, tok, cot, seg, bq, bu, w0, w1, w2, w3, gain_one, shift_one, out_bias, gain_two, shift_two,
    tok_o, cot3, seg_o, g0, g1, g2, g3, proj_o, attn_o, hid_o, two_o, act_o, der_o,
    tok_v, one_v, wq_v, proj_v, attn_v, wo_v, hid_v, two_v, wu_v, act_v, der_v, seg_v, bq_v, bu_v,
    tok_send, tok_recv, cot_send, cot_recv, seg_send, seg_recv, bias_send, bias_recv, load_sem, save_sem, act_sem, *sems,
):
    n, share, own, part, seq = plan.mp, plan.share, plan.own, plan.part, plan.seq
    held = own * seq + part
    at = Place(plan)
    gat = Gatherer(plan, at, (w0, w1, w2, w3), (g0, g1, g2, g3), sems)
    tokens = RowsIn(plan, at, tok, tok_v, tok_send, tok_recv, True)
    cots = RowsIn(plan, at, cot, cot3, cot_send, cot_recv, False)
    hops = plan.hops
    greet(plan, at, False)

    gat.begin(0)
    tokens.start()
    biases = ((bq, bq_v, 0), (bu, bu_v, 1))
    for src, dst, i in biases:
        pltpu.make_async_copy(src, dst.at[at.m], bias_recv.at[i]).start()
        for s in range(1, n):
            remote(src, dst.at[at.m], bias_send.at[i], bias_recv.at[i], mp=lax.rem(at.m + s, n)).start()
    pltpu.make_async_copy(seg, seg_v.at[at.k], seg_recv.at[0]).start()
    for e in range(1, share):
        remote(seg, seg_v.at[at.k], seg_send.at[0], seg_recv.at[0], dp=at.base + lax.rem(at.k + e, share)).start()
    part_of = functools.partial
    hop = [[part_of(gat.step, w, s) for s in range(hops)] for w in range(4)]
    after = [[part_of(gat.follow, w, s) for s in range(hops)] for w in range(4)]
    gat.begin(1)
    gat.begin(2)
    hop[0][0]()
    for s in range(1, hops):
        hop[0][s]()
        after[0][s - 1]()
        if s == 1:
            hop[2][0]()
        if s == 2:
            hop[1][0]()
            after[2][0]()
            gat.begin(3)
    after[1][0]()
    after[0][hops - 1]()
    tokens.arrived()
    save_tok = pltpu.make_async_copy(tok_v, tok_o, save_sem.at[0])
    save_tok.start()
    gain, shift = gain_one[...], shift_one[...]

    @pl.loop(0, plan.rows * share)
    def _(b):
        r, first = lax.div(b, share), pl.multiple_of(lax.rem(b, share) * part, part)
        values = tok_v[r, pl.ds(first, part)].astype(F32)
        one_v[pl.ds(pl.multiple_of(b * part, part), part)] = norm_rows(values, gain, shift).astype(BF)

    settle(seg_v, seg_recv.at[0])
    labels = []
    for r in range(plan.rows):
        row = at.m * plan.group_rows + (own * at.k + r if r < own else own * share)
        line = seg_v[lax.div(row, plan.rows_dev), pl.ds(lax.rem(row, plan.rows_dev), 1)]
        if r == own:
            turned = line
            for e in range(1, share):
                moved = jnp.concatenate([line[:, e * part :], line[:, : e * part]], axis=1)
                turned = jnp.where(at.k == e, moved, turned)
            line = turned
        seg_o[pl.ds(r, 1)] = line
    for src, dst, i in biases:
        settle(dst, bias_recv.at[i])

    gat.arrived(0)
    load_q = pltpu.make_async_copy(g0, wq_v, load_sem.at[0])
    load_q.start()
    load_q.wait()

    def attend_shard(s):
        @pl.loop(0, plan.rows)
        def _(r):
            rows = pl.ds(pl.multiple_of(r * seq, seq), seq)
            projected = jnp.dot(one_v[rows], wq_v[s], preferred_element_type=F32) + bq_v[s]
            proj_v[s, rows] = projected.astype(BF)

        def head(r, first, count, h):
            col = h * 3 * HEAD_DIM
            query = proj_v[s, pl.ds(first, count), col : col + HEAD_DIM]
            keys = pl.ds(pl.multiple_of(r * seq, seq), seq)
            key = proj_v[s, keys, col + HEAD_DIM : col + 2 * HEAD_DIM]
            value = proj_v[s, keys, col + 2 * HEAD_DIM : col + 3 * HEAD_DIM]
            line = seg_o[pl.ds(r, 1)].astype(F32)
            column = jnp.transpose(jnp.broadcast_to(line, (128, seq)))[:count, :1]
            probs = scores_of(query, key, column == line).astype(BF)
            mixed = jnp.dot(probs, value, preferred_element_type=F32)
            attn_v[s, pl.ds(first, count), h * HEAD_DIM : (h + 1) * HEAD_DIM] = mixed.astype(BF)

        @pl.loop(0, own)
        def _(r):
            for h in range(heads):
                head(r, pl.multiple_of(r * seq, seq), seq, h)

        for h in range(heads):
            head(own, own * seq, part, h)

    moves = []
    for s in range(1, hops):
        moves += [hop[2][s], hop[1][s], part_of(cots.start, s - 1)]
        moves += [hop[3][s - 1], after[2][s], after[1][s]]
        moves += [after[3][s - 2]] if s > 1 else []
    for j in range(hops - 1, plan.groups):
        moves.append(part_of(cots.start, j))
    comm = spread_over(n, moves)
    run(n, attend_shard, comm)
    save_proj = pltpu.make_async_copy(proj_v, proj_o, save_sem.at[1])
    save_proj.start()
    save_attn = pltpu.make_async_copy(attn_v, attn_o, save_sem.at[2])
    save_attn.start()

    gat.arrived(1)
    load_o = pltpu.make_async_copy(g1, wo_v, load_sem.at[0])
    load_o.start()
    load_o.wait()
    bias, gain, shift = out_bias[...], gain_two[...], shift_two[...]

    @pl.loop(0, own * share + 1)
    def _(b):
        r, first = lax.div(b, share), pl.multiple_of(lax.rem(b, share) * part, part)
        rows = pl.ds(pl.multiple_of(b * part, part), part)
        total = tok_v[r, pl.ds(first, part)].astype(F32) + bias
        for s in range(n):
            total = total + jnp.dot(attn_v[s, rows], wo_v[s], preferred_element_type=F32)
        hid_v[rows] = total
        two_v[rows] = norm_rows(total, gain, shift).astype(BF)

    save_hid = pltpu.make_async_copy(hid_v, hid_o, save_sem.at[3])
    save_hid.start()
    save_two = pltpu.make_async_copy(two_v, two_o, save_sem.at[4])
    save_two.start()
    after[3][hops - 2]()
    hop[3][hops - 1]()
    gat.arrived(2)
    load_u = pltpu.make_async_copy(g2, wu_v, load_sem.at[0])
    load_u.start()
    load_u.wait()

    def feed_shard(s):
        @pl.loop(0, own * share + 1)
        def _(b):
            rows = pl.ds(pl.multiple_of(b * part, part), part)
            pre = jnp.dot(two_v[rows], wu_v[s], preferred_element_type=F32) + bu_v[s]
            below = 0.5 * (1.0 + lax.erf(pre * math.sqrt(0.5)))
            density = jnp.exp(-0.5 * pre * pre) * (1.0 / math.sqrt(2.0 * math.pi))
            act_v[s, rows] = (pre * below).astype(BF)
            der_v[s, rows] = below + pre * density

        pltpu.make_async_copy(act_v.at[s], act_o.at[s], act_sem.at[0]).start()
        pltpu.make_async_copy(der_v.at[s], der_o.at[s], act_sem.at[1]).start()

    run(n, feed_shard, {})
    after[3][hops - 1]()
    gat.arrived(3)
    for w in range(4):
        gat.finish(w)
    tokens.finish()
    cots.arrived()
    cots.finish()
    for src, dst, i in biases:
        settle(dst.at[pl.ds(0, n - 1)], bias_send.at[i])
    settle(seg_v.at[pl.ds(0, share - 1)], seg_send.at[0])
    for save in (save_tok, save_proj, save_attn, save_hid, save_two):
        save.wait()
    settle(act_v, act_sem.at[0])
    settle(der_v, act_sem.at[1])


def forward(plan, tokens_in, cotangent, segment_ids, biases, weights, vectors):
    n, share = plan.mp, plan.share
    width = tokens_in.shape[2]
    held, every = plan.own * plan.seq + plan.part, plan.rows * plan.seq
    any_space = pl.BlockSpec(memory_space=pl.ANY)
    in_vmem = pl.BlockSpec(memory_space=pltpu.VMEM)
    dma = pltpu.SemaphoreType.DMA
    rows = ((plan.rows, plan.seq, width), BF)
    heads = weights[1].shape[0] // HEAD_DIM
    local, three, ff = weights[1].shape[0], weights[0].shape[1], weights[2].shape[1]
    full = [((n,) + w.shape, BF) for w in weights]
    proj, attn = ((n, every, three), BF), ((n, held, local), BF)
    hid, two = ((held, width), F32), ((held, width), BF)
    act, der = ((n, held, ff), BF), ((n, held, ff), F32)
    outs = [rows, rows, ((plan.rows, plan.seq), jnp.int32), *full, proj, attn, hid, two, act, der]
    return pl.pallas_call(
        functools.partial(forward_kernel, plan, heads),
        out_shape=[jax.ShapeDtypeStruct(*o) for o in outs],
        in_specs=[any_space] * 9 + [in_vmem] * 5,
        out_specs=[any_space] * 2 + [in_vmem] + [any_space] * 10,
        scratch_shapes=[
            pltpu.VMEM(*rows), pltpu.VMEM((every, width), BF), pltpu.VMEM(*full[0]), pltpu.VMEM(*proj),
            pltpu.VMEM(*attn), pltpu.VMEM(*full[1]), pltpu.VMEM(*hid), pltpu.VMEM(*two), pltpu.VMEM(*full[2]),
            pltpu.VMEM(*act), pltpu.VMEM(*der), pltpu.VMEM((share,) + segment_ids.shape, jnp.int32),
            *[pltpu.VMEM((n,) + b.shape, F32) for b in biases],
            dma((plan.groups, share, 2)), dma((2,)), dma((plan.groups, share, 2)), dma((2,)), dma((1,)), dma((1,)),
            dma((2,)), dma((2,)), dma((1,)), dma((5,)), dma((2,)), *gatherer_sems(plan, 4),
        ],
        compiler_params=pltpu.CompilerParams(
            collective_id=0, has_side_effects=True, vmem_limit_bytes=58 << 20
        ),
        name="forward",
    )(tokens_in, cotangent, segment_ids, *biases, *weights, *vectors)


class Reducer:
    def __init__(self, plan, at, stage, loc, sbl, yrc, slot, fin, grp, out, sems):
        self.plan, self.at, self.stage = plan, at, stage
        self.loc, self.sbl, self.yrc, self.slot, self.fin, self.grp, self.out = loc, sbl, yrc, slot, fin, grp, out
        (
            self.sib_send, self.sib_recv, self.y_send, self.y_recv, self.ring_send, self.ring_recv,
            self.grp_send, self.grp_recv, self.fin_send, self.fin_recv, self.out_sem, self.credit,
        ) = sems
        hops = plan.hops
        self.order = [(0, hops)] + [(way, dist) for dist in range(hops - 1, 0, -1) for way in range(2)] + [(0, 0)]

    def target(self, i):
        n, hops = self.plan.mp, self.plan.hops
        dist = hops - lax.div(i + 1, 2)
        up = jnp.where(i == 0, 1, lax.rem(i, 2))
        return self.plan.ring_at(self.at.p + dist * up + (n - dist) * (1 - up))

    def give(self, u, yy, i):
        at, t = self.at, self.target(i)
        src = self.stage[u].at[2 * yy + 1 - at.core]
        return remote(src, self.sbl[u].at[yy, t], self.sib_send.at[u], self.sib_recv.at[u, i, yy], dp=at.sib)

    def begin(self, u, i):
        at, t = self.at, self.target(i)
        rows = self.stage[u].shape[1]
        for yy in range(2):
            self.give(u, yy, i).start()
        size = 32 if rows % 32 == 0 else rows
        for yy in range(2):

            @pl.loop(0, rows // size)
            def _(b):
                inner = pl.ds(pl.multiple_of(b * size, size), size)
                self.loc[u][yy, t, inner] = self.stage[u][2 * yy + at.core, inner]

    def given(self, u):
        settle(self.stage[u].at[pl.ds(0, 2)], self.sib_send.at[u])

    def clear(self, u):
        for way in range(2):
            part = half_of(self.slot[u].at[way, 0], 1 - way)
            part[...] = jnp.zeros(part.shape, BF)

    def add(self, u, yy, t, extra, put):
        rows = self.loc[u].shape[2]
        size = 32 if rows % 32 == 0 else rows

        def block(b):
            inner = pl.ds(pl.multiple_of(b * size, size), size)
            total = self.loc[u][yy, t, inner].astype(F32) + self.sbl[u][yy, t, inner].astype(F32)
            for ref in extra:
                total = total + ref[inner].astype(F32)
            put(inner, total)

        pl.loop(0, rows // size)(block)

    def cross(self, u, i):
        at, t = self.at, self.target(i)
        return remote(self.loc[u].at[1 - at.y, t], self.yrc[u].at[t], self.y_send.at[u], self.y_recv.at[u, i], dp=at.other)

    def first(self, u, i):
        at, t = self.at, self.target(i)
        self.give(u, 1 - at.y, i).wait_recv()

        def put(inner, total):
            self.loc[u][1 - at.y, t, inner] = total.astype(BF)

        self.add(u, 1 - at.y, t, (), put)
        self.cross(u, i).start()

    def hop(self, u, way, s, t):
        src = self.loc[u].at[self.at.y, t]
        dst = self.slot[u].at[way, s]
        if s == 0:
            src, dst = half_of(src, way), half_of(dst, way)
        return remote(
            src, dst, self.ring_send.at[u, way], self.ring_recv.at[u, way, s], mp=self.at.neighbour[way]
        )

    def step(self, u, i):
        at, t = self.at, self.target(i)
        way, dist = self.order[i]
        s = self.plan.hops - dist
        self.give(u, at.y, i).wait_recv()
        self.cross(u, i).wait_recv()
        extra = [self.yrc[u].at[t]]
        ways = (0, 1) if dist in (0, self.plan.hops) else (way,)
        if s > 0:
            for v in ways:
                self.hop(u, v, s - 1, t).wait_recv()
                extra.append(self.slot[u].at[v, s - 1])
        rows = self.loc[u].shape[2]
        quads = self.plan.dp // 4

        def put(inner, total):
            if dist:
                self.loc[u][at.y, t, inner] = total.astype(BF)
            elif quads > 1:
                self.grp[u][lax.div(at.d, 4), inner] = total.astype(BF)
            else:
                to = pl.ds(pl.multiple_of(at.quarter * rows + inner.start, inner.size), inner.size)
                self.fin[u][to] = total.astype(BF)

        self.add(u, at.y, t, extra, put)
        if dist:
            for v in ways:
                self.hop(u, v, s, t).start()
        else:
            for other in range(1, quads):
                self.between(u, other).start()

    def between(self, u, other):
        at = self.at
        to = lax.rem(at.d + 4 * other, self.plan.dp)
        block = self.grp[u].at[lax.div(at.d, 4)]
        return remote(block, block, self.grp_send.at[u], self.grp_recv.at[u], dp=to)

    def share_out(self, u, what):
        at = self.at
        quarter = at.quarter if what != 1 else 2 - 2 * at.y + at.core
        block = piece(self.fin[u], quarter)
        to = at.other if what == 2 else at.sib
        return remote(block, block, self.fin_send.at[u, what], self.fin_recv.at[u, what], dp=to)

    def last(self, u):
        quads = self.plan.dp // 4
        if quads > 1:
            rows = self.loc[u].shape[2]
            settle(self.grp[u].at[pl.ds(0, quads - 1)], self.grp_recv.at[u])
            total = self.grp[u][0].astype(F32)
            for other in range(1, quads):
                total = total + self.grp[u][other].astype(F32)
            self.fin[u][pl.ds(pl.multiple_of(self.at.quarter * rows, rows), rows)] = total.astype(BF)
        self.share_out(u, 2).start()
        self.share_out(u, 0).start()

    def spread(self, u):
        self.share_out(u, 2).wait_recv()
        self.share_out(u, 1).start()

    def write(self, u, dst):
        self.share_out(u, 0).wait_recv()
        self.share_out(u, 1).wait_recv()
        rows = self.loc[u].shape[2]

        @pl.loop(0, 4)
        def _(q):
            at = pl.ds(pl.multiple_of(q * rows, rows), rows)
            slot = lax.rem(q, 2)

            @pl.when(q > 1)
            def _():
                settle(self.out.at[slot], self.out_sem.at[slot])

            self.out[slot] = self.fin[u][at].astype(F32)
            pltpu.make_async_copy(self.out.at[slot], dst.at[at], self.out_sem.at[slot]).start()

        for slot in range(2):
            settle(self.out.at[slot], self.out_sem.at[slot])

    def sent(self, u):
        hops = self.plan.hops
        settle(self.loc[u].at[0], self.y_send.at[u])
        for way in range(2):
            settle(self.slot[u].at[way, pl.ds(0, hops - 1)], self.ring_send.at[u, way])
            settle(half_of(self.slot[u].at[way, 0], way), self.ring_send.at[u, way])

    def release(self, u):
        at = self.at
        self.sent(u)
        for to in ({"dp": at.sib}, {"dp": at.other}, {"mp": at.neighbour[0]}, {"mp": at.neighbour[1]}):
            pl.semaphore_signal(self.credit, inc=1, device_id=to, device_id_type=MESH)

    def claim(self):
        pl.semaphore_wait(self.credit, 4)

    def finish(self, u):
        for what in range(3):
            self.share_out(u, what).wait_send()
        for other in range(1, self.plan.dp // 4):
            self.between(u, other).wait_send()


class RowsOut:
    def __init__(self, plan, at, src, shared, dst, send, recv):
        self.plan, self.at, self.src, self.shared, self.dst, self.send, self.recv = plan, at, src, shared, dst, send, recv
        self.home = at.base + lax.div(at.m, plan.groups)
        self.first = lax.rem(at.m, plan.groups) * plan.group_rows

    def copies(self, what):
        plan, at = self.plan, self.at
        for q in range(plan.mp):
            here = jnp.logical_and(self.home == at.d, at.m == q)
            toks = pl.ds(q * plan.tok, plan.tok)
            if what == 0:
                yield q, here, True, self.src.at[pl.ds(0, plan.own), toks], self.dst.at[
                    pl.ds(self.first + plan.own * at.k, plan.own)
                ]
            else:
                holds = at.k == (q * plan.tok) // plan.part
                yield q, here, holds, self.shared.at[pl.ds((q * plan.tok) % plan.part, plan.tok)], self.dst.at[
                    self.first + plan.own * plan.share
                ]

    def start(self, what):
        for q, here, wanted, src, dst in self.copies(what):

            @pl.when(jnp.logical_and(here, wanted))
            def _():
                pltpu.make_async_copy(src, dst, self.recv.at[0]).start()

            @pl.when(jnp.logical_and(jnp.logical_not(here), wanted))
            def _():
                remote(src, dst, self.send.at[q, what], self.recv.at[0], dp=self.home, mp=q).start()

    def finish(self):
        settle(self.dst, self.recv.at[0])
        for what in range(2):
            for q, here, wanted, src, dst in self.copies(what):

                @pl.when(jnp.logical_and(jnp.logical_not(here), wanted))
                def _():
                    settle(src, self.send.at[q, what])


ACROSS = (((1,), (1,)), ((), ()))
DOWN = (((0,), (0,)), ((), ()))


def backward_kernel(
    plan, heads, g0, g1, g2, g3, tok, cot, seg, proj, attn, hid, two, act, der, gain_one, shift_one, gain_two, down_bias,
    blk, tg, o0, o1, o2, vout, *rest,
):
    n, share, own, part, seq = plan.mp, plan.share, plan.own, plan.part, plan.seq
    hops = plan.hops
    held, every = own * seq + part, plan.rows * seq
    width, ff, three, local = hid.shape[1], act.shape[2], proj.shape[2], attn.shape[2]
    (
        stage_a, stage_b, loc_a, loc_b, sbl_a, sbl_b, yrc_a, yrc_b, slot_a, slot_b, fin_a, fin_b, fin_c,
        grp_a, grp_b, grp_c, out_v,
    ) = rest[:17]
    sems, rest = rest[17:29], rest[29:]
    (
        grad_v, low_v, block_v, tgs, tgo, sums, ups, qbs, msg, vrc, vsum,
        load_sem, wgt_sem, blk_send, blk_recv, tg_send, tg_recv, tgs_send, tgs_recv, tgl_sem, v_send, v_recv,
    ) = rest
    at = Place(plan)
    red = Reducer(
        plan, at, (stage_a, stage_b, stage_a), (loc_a, loc_b, loc_a), (sbl_a, sbl_b, sbl_a), (yrc_a, yrc_b, yrc_a),
        (slot_a, slot_b, slot_a), (fin_a, fin_b, fin_c), (grp_a, grp_b, grp_c), out_v, sems,
    )
    blocks = RowsOut(plan, at, block_v, block_v.at[own], blk, blk_send, blk_recv)
    greet(plan, at, True)
    part_of = functools.partial
    count = len(red.order)
    first = [[part_of(red.first, u, i) for i in range(count)] for u in range(3)]
    step = [[part_of(red.step, u, i) for i in range(count)] for u in range(3)]
    red.clear(0)
    red.clear(1)
    sums[...] = jnp.zeros(sums.shape, F32)
    blocks_held = own * share + 1

    def stream(loads, i):
        def copies(j, slot):
            t = red.target(j)
            for what, (src, dst) in enumerate(loads):
                yield pltpu.make_async_copy(src.at[t], dst.at[slot], wgt_sem.at[what, slot])

        if isinstance(i, int):
            for copy in copies(i, i % 2):
                copy.start()
            return

        @pl.when(i + 1 < n)
        def _():
            for copy in copies(i + 1, lax.rem(i + 1, 2)):
                copy.start()

        for copy in copies(i, lax.rem(i, 2)):
            copy.wait()

    def feed_forward(wd_v, wu_v, act_v, der_v, low_pre, two_v, cot_v, hid_v, sum_v):
        loads = ((g3, wd_v), (g2, wu_v), (act, act_v), (der, der_v))
        stream(loads, 0)
        small = [pltpu.make_async_copy(two, two_v, load_sem.at[0]), pltpu.make_async_copy(hid, hid_v, load_sem.at[1])]
        for r in range(plan.rows):
            extent = seq if r < own else part
            small.append(
                pltpu.make_async_copy(
                    cot.at[r, pl.ds(0, extent)], cot_v.at[pl.ds(r * seq, extent)], load_sem.at[2 + r]
                )
            )
        for copy in small:
            copy.start()
        for copy in small:
            copy.wait()

        @pl.loop(0, blocks_held)
        def _(b):
            rows = pl.ds(pl.multiple_of(b * part, part), part)
            sum_v[rows] = hid_v[rows] + down_bias[...]
            grad_v[rows] = jnp.zeros((part, width), F32)

        def body(i):
            stream(loads, i)
            slot = lax.rem(i, 2)
            rows = ff // 4

            @pl.when(i > 0)
            def _():
                red.given(0)
                red.given(1)

            for q in range(4):
                lhs = act_v[slot, :, q * rows : (q + 1) * rows]
                stage_a[q] = lax.dot_general(lhs, cot_v[...], DOWN, preferred_element_type=F32).astype(BF)
            red.begin(0, i)

            def block(b, total):
                at_rows = pl.ds(pl.multiple_of(b * part, part), part)
                act_grad = lax.dot_general(cot_v[at_rows], wd_v[slot], ACROSS, preferred_element_type=F32)
                low = (act_grad * der_v[slot, at_rows]).astype(BF)
                low_pre[at_rows] = low
                grad_v[at_rows] += lax.dot_general(low, wu_v[slot], ACROSS, preferred_element_type=F32)
                sum_v[at_rows] += jnp.dot(act_v[slot, at_rows], wd_v[slot], preferred_element_type=F32)
                return total + jnp.sum(low.astype(F32), axis=0, keepdims=True)

            total = lax.fori_loop(0, blocks_held, block, jnp.zeros((1, ff), F32))
            ups[red.target(i)] = total
            for q in range(4):
                lhs = low_pre[:, q * rows : (q + 1) * rows]
                stage_b[q] = lax.dot_general(lhs, two_v[...], DOWN, preferred_element_type=F32).astype(BF)
            red.begin(1, i)

        table = {}
        for i in range(count - 1):
            table.setdefault(i + 1, []).append(first[0][i])
        for i in range(count - 2):
            table.setdefault(i + 2, []).append(step[0][i])
        run(n, body, table)
        red.given(0)
        red.given(1)
        first[0][count - 1]()
        first[1][0]()
        step[0][count - 2]()
        first[1][1]()

        @pl.loop(0, blocks_held)
        def _(b):
            r, start = lax.div(b, share), pl.multiple_of(lax.rem(b, share) * part, part)
            rows = pl.ds(pl.multiple_of(b * part, part), part)
            block_v[r, pl.ds(start, part)] = sum_v[rows].astype(BF)
            hidden, grad, cot_f = hid_v[rows], grad_v[rows], cot_v[rows].astype(F32)
            unit, scale, _ = norm(hidden, gain_two[...], 0.0)
            hidden_grad = cot_f + norm_back(unit, scale, gain_two[...], grad)
            grad_v[rows] = hidden_grad
            low_v[rows] = hidden_grad.astype(BF)
            for line, value in ((2, hidden_grad), (3, grad * unit), (4, grad), (5, cot_f)):
                sums[pl.ds(line, 1)] += jnp.sum(value, axis=0, keepdims=True)

        blocks.start(0)
        blocks.start(1)

    pl.run_scoped(
        feed_forward,
        pltpu.VMEM((2,) + g3.shape[1:], BF), pltpu.VMEM((2,) + g2.shape[1:], BF), pltpu.VMEM((2, held, ff), BF),
        pltpu.VMEM((2, held, ff), F32), pltpu.VMEM((held, ff), BF), pltpu.VMEM((held, width), BF),
        pltpu.VMEM((held, width), BF), pltpu.VMEM((held, width), F32), pltpu.VMEM((held, width), F32),
    )

    def attention(wq_v, wo_v, proj_v, attn_v, head_v, three_v, tok_v, one_v, back_v, out3):
        loads = ((g0, wq_v), (g1, wo_v), (proj, proj_v), (attn, attn_v))
        stream(loads, 0)
        load = pltpu.make_async_copy(tok, tok_v, load_sem.at[0])
        load.start()
        step[0][count - 1]()
        red.last(0)
        for i in range(2, count):
            first[1][i]()
        red.spread(0)
        red.release(0)
        load.wait()

        @pl.loop(0, plan.rows * share)
        def _(b):
            r, start = lax.div(b, share), pl.multiple_of(lax.rem(b, share) * part, part)
            rows = pl.ds(pl.multiple_of(b * part, part), part)
            values = tok_v[r, pl.ds(start, part)].astype(F32)
            one_v[rows] = norm_rows(values, gain_one[...], shift_one[...]).astype(BF)
            back_v[rows] = jnp.zeros((part, width), F32)

        three_v[...] = jnp.zeros(three_v.shape, BF)
        red.claim()

        def body(i):
            stream(loads, i)
            slot = lax.rem(i, 2)

            @pl.loop(0, blocks_held)
            def _(b):
                rows = pl.ds(pl.multiple_of(b * part, part), part)
                grad = lax.dot_general(low_v[rows], wo_v[slot], ACROSS, preferred_element_type=F32)
                head_v[rows] = grad.astype(BF)

            def head(r, queries, amount, h):
                col = h * 3 * HEAD_DIM
                keys = pl.ds(pl.multiple_of(r * seq, seq), seq)
                query = proj_v[slot, pl.ds(queries, amount), col : col + HEAD_DIM]
                key = proj_v[slot, keys, col + HEAD_DIM : col + 2 * HEAD_DIM]
                value = proj_v[slot, keys, col + 2 * HEAD_DIM : col + 3 * HEAD_DIM]
                head_grad = head_v[pl.ds(queries, amount), h * HEAD_DIM : (h + 1) * HEAD_DIM]
                line = seg[pl.ds(r, 1)].astype(F32)
                column = jnp.transpose(jnp.broadcast_to(line, (128, seq)))[:amount, :1]
                allowed = column == line
                full = scores_of(query, key, allowed)
                value_grad = lax.dot_general(full.astype(BF), head_grad, DOWN, preferred_element_type=F32)
                probs_grad = lax.dot_general(head_grad, value, ACROSS, preferred_element_type=F32)
                delta = jnp.sum(probs_grad * full, axis=-1, keepdims=True)
                low = (jnp.where(allowed, full * (probs_grad - delta), 0.0) * HEAD_DIM ** (-0.5)).astype(BF)
                query_grad = jnp.dot(low, key, preferred_element_type=F32)
                key_grad = lax.dot_general(low, query, DOWN, preferred_element_type=F32)
                three_v[pl.ds(queries, amount), col : col + HEAD_DIM] = query_grad.astype(BF)
                three_v[keys, col + HEAD_DIM : col + 2 * HEAD_DIM] = key_grad.astype(BF)
                three_v[keys, col + 2 * HEAD_DIM : col + 3 * HEAD_DIM] = value_grad.astype(BF)

            @pl.loop(0, own)
            def _(r):
                for h in range(heads):
                    head(r, pl.multiple_of(r * seq, seq), seq, h)

            for h in range(heads):
                head(own, own * seq, part, h)

            @pl.when(i > 0)
            def _():
                red.given(2)

            wide, narrow = three // 4, local // 4
            weight = lax.dot_general(three_v[...], one_v[...], DOWN, preferred_element_type=F32).astype(BF)
            out_weight = lax.dot_general(attn_v[slot], low_v[...], DOWN, preferred_element_type=F32).astype(BF)
            for q in range(4):
                stage_a[q, :wide] = weight[q * wide : (q + 1) * wide]
                stage_a[q, wide:] = out_weight[q * narrow : (q + 1) * narrow]
            red.begin(2, i)

            def block(b, total):
                rows = pl.ds(pl.multiple_of(b * part, part), part)
                low = three_v[rows]
                back_v[rows] += lax.dot_general(low, wq_v[slot], ACROSS, preferred_element_type=F32)
                return total + jnp.sum(low.astype(F32), axis=0, keepdims=True)

            qbs[red.target(i)] = lax.fori_loop(0, plan.rows * share, block, jnp.zeros((1, three), F32))

        table = {}
        for i in range(count):
            table.setdefault(i, []).append(step[1][i])
            if i + 1 < count:
                table.setdefault(i + 1, []).append(first[2][i])
        run(n, body, table)
        red.last(1)
        red.given(2)
        first[2][count - 1]()

        @pl.loop(0, plan.rows * share)
        def _(b):
            r, start = lax.div(b, share), pl.multiple_of(lax.rem(b, share) * part, part)
            rows = pl.ds(pl.multiple_of(b * part, part), part)
            unit, scale, _ = norm(tok_v[r, pl.ds(start, part)].astype(F32), gain_one[...], 0.0)
            grad = back_v[rows]
            for line, value in ((0, grad * unit), (1, grad)):
                sums[pl.ds(line, 1)] += jnp.sum(value, axis=0, keepdims=True)
            grad = norm_back(unit, scale, gain_one[...], grad)

            @pl.when(b < blocks_held)
            def _():
                mine = pl.ds(pl.multiple_of(jnp.minimum(b, blocks_held - 1) * part, part), part)
                out3[r, pl.ds(start, part)] = (grad + grad_v[mine]).astype(BF)

            @pl.when(b >= blocks_held)
            def _():
                out3[r, pl.ds(start, part)] = grad.astype(BF)

        tokens = RowsOut(plan, at, out3, tgo, tg, tg_send, tg_recv)
        for e in range(share):
            src = out3.at[own, pl.ds(e * part, part)]
            if e == 0:
                pltpu.make_async_copy(src, tgs.at[0], tgl_sem.at[0]).start()
            else:
                to = at.base + lax.rem(at.k + e, share)
                remote(src, tgs.at[share - e], tgs_send.at[e], tgs_recv.at[share - e], dp=to).start()
        tokens.start(0)

        lines = [-(-size // 128) for size in (ff, three)]
        msg[...] = jnp.zeros(msg.shape, F32)
        for q in range(n):
            msg[q, :8, : width // n] = sums[:, q * (width // n) : (q + 1) * (width // n)]
            line = 8
            for ref, size in ((ups, ff), (qbs, three)):
                for first_col in range(0, size, 128):
                    cols = min(128, size - first_col)
                    msg[q, line : line + 1, :cols] = ref[q, :, first_col : first_col + cols]
                    line += 1
        me = at.d * n + at.m

        def one(i, carry):
            to = lax.rem(me + i, plan.all)
            e, q = lax.div(to, n), lax.rem(to, n)
            remote(msg.at[q], vrc.at[me], v_send.at[0], v_recv.at[0], dp=e, mp=q).start()
            return carry

        lax.fori_loop(1, plan.all, one, 0)
        pltpu.make_async_copy(msg.at[at.m], vrc.at[me], v_recv.at[0]).start()
        step[2][0]()
        for e in range(1, share):
            settle(tgs.at[e], tgs_recv.at[e])
        settle(tgs.at[0], tgl_sem.at[0])
        tgo[...] = sum(tgs[e].astype(F32) for e in range(share)).astype(BF)
        tokens.start(1)
        step[2][1]()
        red.spread(1)
        settle(vrc, v_recv.at[0])
        vsum[...] = jnp.sum(vrc[...], axis=0)
        for e in range(1, n):
            remote(vsum, vout.at[at.m], v_send.at[1], v_recv.at[1], mp=lax.rem(at.m + e, n)).start()
        pltpu.make_async_copy(vsum, vout.at[at.m], v_recv.at[1]).start()
        red.write(0, o0)
        for i in range(2, count):
            step[2][i]()
            if i == 3:
                red.write(1, o1)
        red.last(2)
        red.spread(2)
        red.write(2, o2)
        for u in range(3):
            red.finish(u)
        red.sent(1)
        red.sent(2)
        for e in range(1, share):
            settle(tgs.at[0], tgs_send.at[e])
        blocks.finish()
        tokens.finish()
        settle(vout, v_recv.at[1])
        settle(vrc.at[pl.ds(0, plan.all - 1)], v_send.at[0])
        settle(vout.at[pl.ds(0, n - 1)], v_send.at[1])

    pl.run_scoped(
        attention,
        pltpu.VMEM((2,) + g0.shape[1:], BF), pltpu.VMEM((2,) + g1.shape[1:], BF), pltpu.VMEM((2, every, three), BF),
        pltpu.VMEM((2, held, local), BF), pltpu.VMEM((held, local), BF), pltpu.VMEM((every, three), BF),
        pltpu.VMEM((plan.rows, seq, width), BF), pltpu.VMEM((every, width), BF), pltpu.VMEM((every, width), F32),
        pltpu.VMEM((plan.rows, seq, width), BF),
    )


def backward(plan, weights, tok3, cot3, seg, proj, attn, hid, two, act, der, vectors):
    n, share = plan.mp, plan.share
    held, width = hid.shape
    ff, three, local = act.shape[2], proj.shape[2], attn.shape[2]
    heads = local // HEAD_DIM
    quads, quarter = plan.dp // 4, ff // 4
    if local + three != ff:
        raise ValueError("unsupported sizes")
    any_space = pl.BlockSpec(memory_space=pl.ANY)
    in_vmem = pl.BlockSpec(memory_space=pltpu.VMEM)
    dma = pltpu.SemaphoreType.DMA
    rows = jax.ShapeDtypeStruct((plan.rows_dev, plan.tok, width), BF)
    shard = jax.ShapeDtypeStruct((ff, width), F32)
    size = 8 + -(-ff // 128) + -(-three // 128)
    size = -(-size // 8) * 8
    vec = (size, 128)
    return pl.pallas_call(
        functools.partial(backward_kernel, plan, heads),
        out_shape=[rows, rows, shard, shard, shard, jax.ShapeDtypeStruct((n,) + vec, F32)],
        in_specs=[any_space] * 6 + [in_vmem] + [any_space] * 6 + [in_vmem] * 4,
        out_specs=[any_space] * 6,
        scratch_shapes=[
            *[pltpu.VMEM((4, quarter, width), BF)] * 2,
            *[pltpu.VMEM((2, n, quarter, width), BF)] * 4,
            *[pltpu.VMEM((n, quarter, width), BF)] * 2,
            *[pltpu.VMEM((2, plan.hops, quarter, width), BF)] * 2,
            *[pltpu.VMEM((ff, width), BF)] * 3,
            *[pltpu.VMEM((quads,) + ((quarter, width) if quads > 1 else (8, 128)), BF)] * 3,
            pltpu.VMEM((2, quarter, width), F32),
            dma((3,)), dma((3, n, 2)), dma((3,)), dma((3, n)), dma((3, 2)), dma((3, 2, plan.hops)), dma((3,)), dma((3,)),
            dma((3, 3)), dma((3, 3)), dma((2,)), pltpu.SemaphoreType.REGULAR,
            pltpu.VMEM((held, width), F32), pltpu.VMEM((held, width), BF), pltpu.VMEM((plan.rows, plan.seq, width), BF),
            pltpu.VMEM((share, plan.part, width), BF), pltpu.VMEM((plan.part, width), BF), pltpu.VMEM((8, width), F32),
            pltpu.VMEM((n, 1, ff), F32), pltpu.VMEM((n, 1, three), F32), pltpu.VMEM((n,) + vec, F32),
            pltpu.VMEM((plan.all,) + vec, F32), pltpu.VMEM(vec, F32),
            dma((2 + plan.rows,)), dma((4, 2)), dma((n, 2)), dma((1,)), dma((n, 2)), dma((1,)), dma((share,)),
            dma((share,)), dma((1,)), dma((2,)), dma((2,)),
        ],
        compiler_params=pltpu.CompilerParams(
            collective_id=1, has_side_effects=True, vmem_limit_bytes=61 << 20
        ),
        name="backward",
    )(*weights, tok3, cot3, seg, proj, attn, hid, two, act, der, *vectors)


def scores_of(query, key, allowed):
    raw = lax.dot_general(query, key, (((1,), (1,)), ((), ())), preferred_element_type=F32)
    scores = jnp.where(allowed, raw * HEAD_DIM ** (-0.5), MASKED)
    raised = jnp.exp(scores - jnp.max(scores, axis=-1, keepdims=True))
    return raised / jnp.sum(raised, axis=-1, keepdims=True)


def norm(values, gain_vec, shift_vec):
    centred = values - jnp.mean(values, axis=-1, keepdims=True)
    scale = lax.rsqrt(jnp.mean(centred * centred, axis=-1, keepdims=True) + EPS)
    unit = centred * scale
    return unit, scale, unit * gain_vec + shift_vec


def norm_back(unit, scale, gain_vec, grad):
    pulled = grad * gain_vec
    inner = jnp.mean(pulled * unit, axis=-1, keepdims=True)
    return scale * (pulled - jnp.mean(pulled, axis=-1, keepdims=True) - unit * inner)


def per_device(
    plan, tokens_in, segment_ids, attn_gain, attn_shift, qkv_weight, qkv_bias, out_weight, out_bias, mlp_gain, mlp_shift,
    up_weight, up_bias, down_weight, down_bias, cotangent,
):
    n, width = plan.mp, tokens_in.shape[2]
    ff_local = up_weight.shape[1]
    heads_local = qkv_bias.shape[1] // HEAD_DIM
    parts = qkv_bias.reshape(2, heads_local, HEAD_DIM)
    bias_three = jnp.stack([parts[0], jnp.zeros_like(parts[0]), parts[1]], axis=1).reshape(1, -1)
    vectors = [v.reshape(1, width) for v in (attn_gain, attn_shift, out_bias, mlp_gain, mlp_shift)]
    tok3, cot3, seg, wq, wo, wu, wd, proj, attn, hidden, normed_two, act_low, gelu_slope = forward(
        plan, tokens_in, cotangent, segment_ids, (bias_three, up_bias.reshape(1, ff_local)),
        (qkv_weight, out_weight, up_weight, down_weight), vectors,
    )
    block_out, tokens_low, down_grad, up_grad, rest_grad, sums = backward(
        plan, (wq, wo, wu, wd), tok3, cot3, seg, proj, attn, hidden, normed_two, act_low, gelu_slope,
        [v.reshape(1, width) for v in (attn_gain, attn_shift, mlp_gain, down_bias)],
    )
    local, three = out_weight.shape[0], qkv_weight.shape[1]
    rest_grad = rest_grad.reshape(4, (local + three) // 4, width)
    qkv_grad = rest_grad[:, : three // 4].reshape(three, width).T
    out_grad = rest_grad[:, three // 4 :].reshape(local, width)
    six = jnp.swapaxes(sums[:, :6, : width // n], 0, 1).reshape(6, width)
    mine = lax.dynamic_index_in_dim(sums, lax.axis_index("mp"), 0, keepdims=False)
    lines = [-(-size // 128) for size in (ff_local, three)]
    up_bias_grad = mine[8 : 8 + lines[0]].reshape(-1)[:ff_local]
    bias_sums = mine[8 + lines[0] : 8 + sum(lines)].reshape(-1)[:three].reshape(heads_local, 3, HEAD_DIM)
    qkv_bias_grad = jnp.stack([bias_sums[:, 0], bias_sums[:, 2]]).reshape(2, local)
    return (
        block_out, tokens_low.astype(F32), six[0], six[1], qkv_grad, qkv_bias_grad, out_grad, six[2], six[3], six[4],
        up_grad.T, up_bias_grad, down_grad, six[5],
    )


def solution(mesh):
    dp, mp = mesh.shape["dp"], mesh.shape["mp"]
    rows_spec = P("dp", "mp", None)
    in_specs = (
        rows_spec, P("dp", None), P(), P(), P(None, "mp"), P(None, "mp"), P("mp", None), P(), P(), P(),
        P(None, "mp"), P("mp"), P("mp", None), P(), rows_spec,
    )
    out_specs = (
        rows_spec, rows_spec, P(), P(), P(None, "mp"), P(None, "mp"), P("mp", None), P(), P(), P(),
        P(None, "mp"), P("mp"), P("mp", None), P(),
    )

    def run(tokens_in, segment_ids, *rest):
        rows_all, seq_len, _ = tokens_in.shape
        plan = Plan(dp, mp, rows_all // dp, seq_len // mp, seq_len)
        return jax.shard_map(
            functools.partial(per_device, plan), mesh=mesh, in_specs=in_specs, out_specs=out_specs, check_vma=False
        )(tokens_in, segment_ids, *rest)

    return run
```

time: 595 us -> 468 us (0.79)
  matrix products: 96 us -> 0 us
  other arithmetic: 44.4 us -> 2.46 us
  Pallas kernels: 411 us -> 447 us
  local copies, waits for them, and re-layouts: 34.4 us -> 13.7 us
    dot_general x12 -> x0, matrix products: 96 us -> none  [the longest x1 15.3 us: per_device(): act_grad = jnp.einsum('td,sfd->tsf', cot, wd, preferred_element_type=F32)]
    pallas_call x4 -> x2, Pallas kernels: 411 us -> 447 us  [the longest x1 257 us: backward(): pl.pallas_call(functools.partial(backward_kernel, plan, heads), out_shape...]
    convert_element_type x4 -> x1, other arithmetic: 30.1 us -> 1.82 us  [per_device(): tokens_low.astype(F32)]
    reshape x9 -> x2, local copies, waits for them, and re-layouts: 11.5 us -> 1.22 us  [the longest x1 0.65 us: per_device(): jnp.stack([parts[0], jnp.zeros_like(parts[0]), parts[1]], axis=1)]
    reduce_sum x5 -> x0, other arithmetic: 7.19 us -> none  [the longest x1 3.16 us: per_device(): jnp.sum(qkv_flat, axis=0, dtype=F32).reshape(n, heads_local, 3, HEAD_DIM)]
    unnamed x107 -> x14, local copies, waits for them, and re-layouts: 12.7 us -> 6.29 us
where the time goes in v3:
time: 468 us; the launch traced here: 463 us
  Pallas kernels  447 us (96%)
  local copies, waits for them, and re-layouts  13.7 us (3%)
    pallas_call x1, Pallas kernels, backward(): pl.pallas_call(functools.partial(backward_kernel, plan, heads), out_shape...  257 us
    pallas_call x1, Pallas kernels, forward(): pl.pallas_call(functools.partial(forward_kernel, plan, heads), out_shape=...  190 us

profile of v3, /device:TPU:11, one launch (start us, length us, event | category | flops | bytes accessed | tf_op | source)
XLA Modules:
  0.0 463.5 jit_solution(13355350618216259215)
XLA Ops:
  0.6 0.8 slice_reduce_fusion.3
  1.4 0.1 stack_squeeze.8
  1.5 0.1 stack_squeeze.9
  1.6 0.1 pad.3.clone
  1.7 0.1 pad_maximum_fusion
  1.7 0.6 reshape.94.bq
  2.4 189.7 %forward.1 = (bf16[3,256,1024]{2,1,0:T(8,128)(2,1)}, bf16[3,256,1024]{2,1,0:T(8,128)(2,1)}, s32[3,256]{1,0:T(4,128)}, bf16[8,1024,384]{2,1,0:T(8,128)(2,1)}, bf1...) custom-call(bf16[20,32,1024]{2,1,0:T(8,128)(2,1)} %tok.1, ...), custom_call_target="tpu_custom_call" | custom-call | tf_op jit(solution)/shard_map/forward/pallas_call | solution.py:428
  192.1 256.9 %backward.1 = (bf16[20,32,1024]{2,1,0:T(8,128)(2,1)}, bf16[20,32,1024]{2,1,0:T(8,128)(2,1)}, f32[512,1024]{1,0:T(8,128)}, f32[512,1024]{1,0:T(8,128)}, f32[512,1024]{1,0:T(8,128)}, /*index=5*/f32[8,16,128]{2,1,0:T(8,128)}) custom-call(bf16[8,1024,384]{2,1,0:T(8,128)(2,1)} %get-tuple-element.33.g0, bf16[8,128,1024]{2,1,0:T(8,128)(2,1)} %get-tuple-element.34.g1, ...), custom_call_target="tpu_custom_call" | custom-call | tf_op jit(solution)/shard_map/backward/pallas_call | solution.py:1018
  449.1 0.7 constant_dynamic-slice_fusion
  449.8 0.1 reshape_reshape.3
  449.9 0.1 stack.11
  449.9 0.1 stack.12
  450.0 0.6 pad_maximum_fusion.1
  450.6 1.5 slice.72
  452.1 1.6 copy.35
  453.7 0.0 copy-done.3
  453.7 1.8 convert_element_type.3
  455.6 0.5 copy-done.1
  456.0 1.8 copy.36
  457.8 2.0 slice.75
  459.9 0.6 fusion
  460.5 0.6 dynamic-slice_bitcast_fusion
  461.1 1.1 copy.39
  462.2 1.3 copy.40
  (11 shorter events, 0.0 us)
Async XLA Ops:
  452.1 1.6 copy-start.3
  453.7 2.3 copy-start.1
  456.0 3.8 copy-start.4
  456.0 5.1 %copy-start.2 = (bf16[20,32,1024]{2,1,0:T(8,128)(2,1)S(1)}, bf16[20,32,1024]{2,1,0:T(8,128)(2,1)}, u32[]{:S(2)}) copy-start(bf16[20,32,1024]{2,1,0:T(8,128)(2,1)} %get-tuple-element.104) | copy-start | bytes 3932164
  457.8 4.3 copy-start

commit v4 on v3

--- a/solution.py
+++ b/solution.py
@@ -14,6 +14,8 @@
 MESH = pl.DeviceIdType.MESH
 BF = jnp.bfloat16
 F32 = jnp.float32
+ACROSS = (((1,), (1,)), ((), ()))
+DOWN = (((0,), (0,)), ((), ()))
 
 
 class Plan:
@@ -242,7 +244,7 @@
 def forward_kernel(
     plan, heads, tok, cot, seg, bq, bu, w0, w1, w2, w3, gain_one, shift_one, out_bias, gain_two, shift_two,
     tok_o, cot3, seg_o, g0, g1, g2, g3, proj_o, attn_o, hid_o, two_o, act_o, der_o,
-    tok_v, one_v, wq_v, proj_v, attn_v, wo_v, hid_v, two_v, wu_v, act_v, der_v, seg_v, bq_v, bu_v,
+    tok_v, one_v, wq_v, proj_v, attn_v, wo_v, hid_v, two_v, wu_v, act_v, der_v, seg_v, columns, bq_v, bu_v,
     tok_send, tok_recv, cot_send, cot_recv, seg_send, seg_recv, bias_send, bias_recv, load_sem, save_sem, act_sem, *sems,
 ):
     n, share, own, part, seq = plan.mp, plan.share, plan.own, plan.part, plan.seq
@@ -304,6 +306,7 @@
                 turned = jnp.where(at.k == e, moved, turned)
             line = turned
         seg_o[pl.ds(r, 1)] = line
+    label_columns(seg_o, plan.rows, columns)
     for src, dst, i in biases:
         settle(dst, bias_recv.at[i])
 
@@ -313,31 +316,26 @@
     load_q.wait()
 
     def attend_shard(s):
-        @pl.loop(0, plan.rows)
-        def _(r):
-            rows = pl.ds(pl.multiple_of(r * seq, seq), seq)
-            projected = jnp.dot(one_v[rows], wq_v[s], preferred_element_type=F32) + bq_v[s]
-            proj_v[s, rows] = projected.astype(BF)
-
-        def head(r, first, count, h):
-            col = h * 3 * HEAD_DIM
-            query = proj_v[s, pl.ds(first, count), col : col + HEAD_DIM]
+        projected = jnp.dot(one_v[...], wq_v[s], preferred_element_type=F32) + bq_v[s]
+        proj_v[s] = projected.astype(BF)
+
+        def attend(r, first, amount):
+            allowed = same_image(seg_o, columns, r, amount)
             keys = pl.ds(pl.multiple_of(r * seq, seq), seq)
-            key = proj_v[s, keys, col + HEAD_DIM : col + 2 * HEAD_DIM]
-            value = proj_v[s, keys, col + 2 * HEAD_DIM : col + 3 * HEAD_DIM]
-            line = seg_o[pl.ds(r, 1)].astype(F32)
-            column = jnp.transpose(jnp.broadcast_to(line, (128, seq)))[:count, :1]
-            probs = scores_of(query, key, column == line).astype(BF)
-            mixed = jnp.dot(probs, value, preferred_element_type=F32)
-            attn_v[s, pl.ds(first, count), h * HEAD_DIM : (h + 1) * HEAD_DIM] = mixed.astype(BF)
+            for h in range(heads):
+                col = h * 3 * HEAD_DIM
+                query = proj_v[s, pl.ds(first, amount), col : col + HEAD_DIM]
+                key = proj_v[s, keys, col + HEAD_DIM : col + 2 * HEAD_DIM]
+                value = proj_v[s, keys, col + 2 * HEAD_DIM : col + 3 * HEAD_DIM]
+                probs = probs_of(key, query, allowed).astype(BF)
+                mixed = lax.dot_general(probs, value, DOWN, preferred_element_type=F32)
+                attn_v[s, pl.ds(first, amount), h * HEAD_DIM : (h + 1) * HEAD_DIM] = mixed.astype(BF)
 
         @pl.loop(0, own)
         def _(r):
-            for h in range(heads):
-                head(r, pl.multiple_of(r * seq, seq), seq, h)
-
-        for h in range(heads):
-            head(own, own * seq, part, h)
+            attend(r, pl.multiple_of(r * seq, seq), seq)
+
+        attend(own, own * seq, part)
 
     moves = []
     for s in range(1, hops):
@@ -359,15 +357,19 @@
     load_o.wait()
     bias, gain, shift = out_bias[...], gain_two[...], shift_two[...]
 
-    @pl.loop(0, own * share + 1)
-    def _(b):
-        r, first = lax.div(b, share), pl.multiple_of(lax.rem(b, share) * part, part)
-        rows = pl.ds(pl.multiple_of(b * part, part), part)
-        total = tok_v[r, pl.ds(first, part)].astype(F32) + bias
+    def branch(first, amount, values):
+        rows = pl.ds(first, amount)
+        total = values.astype(F32) + bias
         for s in range(n):
             total = total + jnp.dot(attn_v[s, rows], wo_v[s], preferred_element_type=F32)
         hid_v[rows] = total
         two_v[rows] = norm_rows(total, gain, shift).astype(BF)
+
+    @pl.loop(0, own)
+    def _(r):
+        branch(pl.multiple_of(r * seq, seq), seq, tok_v[r])
+
+    branch(own * seq, part, tok_v[own, :part])
 
     save_hid = pltpu.make_async_copy(hid_v, hid_o, save_sem.at[3])
     save_hid.start()
@@ -381,14 +383,11 @@
     load_u.wait()
 
     def feed_shard(s):
-        @pl.loop(0, own * share + 1)
-        def _(b):
-            rows = pl.ds(pl.multiple_of(b * part, part), part)
-            pre = jnp.dot(two_v[rows], wu_v[s], preferred_element_type=F32) + bu_v[s]
-            below = 0.5 * (1.0 + lax.erf(pre * math.sqrt(0.5)))
-            density = jnp.exp(-0.5 * pre * pre) * (1.0 / math.sqrt(2.0 * math.pi))
-            act_v[s, rows] = (pre * below).astype(BF)
-            der_v[s, rows] = below + pre * density
+        pre = jnp.dot(two_v[...], wu_v[s], preferred_element_type=F32) + bu_v[s]
+        below = 0.5 * (1.0 + lax.erf(pre * math.sqrt(0.5)))
+        density = jnp.exp(-0.5 * pre * pre) * (1.0 / math.sqrt(2.0 * math.pi))
+        act_v[s] = (pre * below).astype(BF)
+        der_v[s] = below + pre * density
 
         pltpu.make_async_copy(act_v.at[s], act_o.at[s], act_sem.at[0]).start()
         pltpu.make_async_copy(der_v.at[s], der_o.at[s], act_sem.at[1]).start()
@@ -434,6 +433,7 @@
             pltpu.VMEM(*rows), pltpu.VMEM((every, width), BF), pltpu.VMEM(*full[0]), pltpu.VMEM(*proj),
             pltpu.VMEM(*attn), pltpu.VMEM(*full[1]), pltpu.VMEM(*hid), pltpu.VMEM(*two), pltpu.VMEM(*full[2]),
             pltpu.VMEM(*act), pltpu.VMEM(*der), pltpu.VMEM((share,) + segment_ids.shape, jnp.int32),
+            pltpu.VMEM((plan.rows, plan.seq, 128), F32),
             *[pltpu.VMEM((n,) + b.shape, F32) for b in biases],
             dma((plan.groups, share, 2)), dma((2,)), dma((plan.groups, share, 2)), dma((2,)), dma((1,)), dma((1,)),
             dma((2,)), dma((2,)), dma((1,)), dma((5,)), dma((2,)), *gatherer_sems(plan, 4),
@@ -446,8 +446,8 @@
 
 
 class Reducer:
-    def __init__(self, plan, at, stage, loc, sbl, yrc, slot, fin, grp, out, sems):
-        self.plan, self.at, self.stage = plan, at, stage
+    def __init__(self, plan, at, stage, loc, sbl, yrc, slot, wide, fin, grp, out, sems):
+        self.plan, self.at, self.stage, self.wide = plan, at, stage, wide
         self.loc, self.sbl, self.yrc, self.slot, self.fin, self.grp, self.out = loc, sbl, yrc, slot, fin, grp, out
         (
             self.sib_send, self.sib_recv, self.y_send, self.y_recv, self.ring_send, self.ring_recv,
@@ -487,6 +487,9 @@
         for way in range(2):
             part = half_of(self.slot[u].at[way, 0], 1 - way)
             part[...] = jnp.zeros(part.shape, BF)
+            for yy in range(2):
+                part = half_of(self.wide.at[way, 0, yy], 1 - way)
+                part[...] = jnp.zeros(part.shape, BF)
 
     def add(self, u, yy, t, extra, put):
         rows = self.loc[u].shape[2]
@@ -556,6 +559,81 @@
             for other in range(1, quads):
                 self.between(u, other).start()
 
+    def wide_hop(self, u, way, s, t):
+        src, dst = self.loc[u].at[:, t], self.wide.at[way, s]
+        if s == 0:
+            half = self.wide.shape[-1] // 2
+            src, dst = (ref.at[:, :, pl.ds(way * half, half)] for ref in (src, dst))
+        return remote(
+            src, dst, self.ring_send.at[u, way], self.ring_recv.at[u, way, s], mp=self.at.neighbour[way]
+        )
+
+    def wide_cross(self, u):
+        mine, theirs = self.yrc[u].at[pl.ds(2, 2)], self.yrc[u].at[pl.ds(0, 2)]
+        return remote(mine, theirs, self.y_send.at[u], self.y_recv.at[u, 0], dp=self.at.other)
+
+    def wide_step(self, u, i):
+        at, t = self.at, self.target(i)
+        way, dist = self.order[i]
+        s = self.plan.hops - dist
+        ways = (0, 1) if dist in (0, self.plan.hops) else (way,)
+        for yy in range(2):
+            self.give(u, yy, i).wait_recv()
+        if s > 0:
+            for v in ways:
+                self.wide_hop(u, v, s - 1, t).wait_recv()
+        for yy in range(2):
+            extra = [self.wide.at[v, s - 1, yy] for v in ways] if s > 0 else []
+
+            def put(inner, total):
+                if dist:
+                    self.loc[u][yy, t, inner] = total.astype(BF)
+                else:
+                    self.yrc[u][2 + yy, inner] = total.astype(BF)
+
+            self.add(u, yy, t, extra, put)
+        if dist:
+            for v in ways:
+                self.wide_hop(u, v, s, t).start()
+        else:
+            self.wide_cross(u).start()
+
+    def wide_last(self, u):
+        at, quads = self.at, self.plan.dp // 4
+        rows = self.loc[u].shape[2]
+        self.wide_cross(u).wait_recv()
+        for yy in range(2):
+            to = pl.ds(pl.multiple_of((2 * yy + at.core) * rows, rows), rows)
+            total = self.yrc[u][yy].astype(F32) + self.yrc[u][2 + yy].astype(F32)
+            if quads > 1:
+                self.grp[u][lax.div(at.d, 4), yy] = total.astype(BF)
+            else:
+                self.fin[u][to] = total.astype(BF)
+        if quads > 1:
+            for other in range(1, quads):
+                self.between(u, other).start()
+            settle(self.grp[u].at[pl.ds(0, quads - 1)], self.grp_recv.at[u])
+            for yy in range(2):
+                to = pl.ds(pl.multiple_of((2 * yy + at.core) * rows, rows), rows)
+                total = self.grp[u][0, yy].astype(F32)
+                for other in range(1, quads):
+                    total = total + self.grp[u][other, yy].astype(F32)
+                self.fin[u][to] = total.astype(BF)
+        for what in range(2):
+            self.wide_out(u, what).start()
+
+    def wide_out(self, u, what):
+        block = piece(self.fin[u], 2 * what + self.at.core)
+        return remote(block, block, self.fin_send.at[u, what], self.fin_recv.at[u, what], dp=self.at.sib)
+
+    def wide_sent(self, u):
+        hops = self.plan.hops
+        settle(self.yrc[u].at[pl.ds(0, 2)], self.y_send.at[u])
+        for way in range(2):
+            settle(self.wide.at[way, pl.ds(0, hops - 1)], self.ring_send.at[u, way])
+            half = self.wide.shape[-1] // 2
+            settle(self.wide.at[way, 0, :, :, pl.ds(0, half)], self.ring_send.at[u, way])
+
     def between(self, u, other):
         at = self.at
         to = lax.rem(at.d + 4 * other, self.plan.dp)
@@ -585,9 +663,9 @@
         self.share_out(u, 2).wait_recv()
         self.share_out(u, 1).start()
 
-    def write(self, u, dst):
-        self.share_out(u, 0).wait_recv()
-        self.share_out(u, 1).wait_recv()
+    def write(self, u, dst, wide=False):
+        for what in range(2):
+            (self.wide_out if wide else self.share_out)(u, what).wait_recv()
         rows = self.loc[u].shape[2]
 
         @pl.loop(0, 4)
@@ -614,16 +692,16 @@
 
     def release(self, u):
         at = self.at
-        self.sent(u)
+        self.wide_sent(u)
         for to in ({"dp": at.sib}, {"dp": at.other}, {"mp": at.neighbour[0]}, {"mp": at.neighbour[1]}):
             pl.semaphore_signal(self.credit, inc=1, device_id=to, device_id_type=MESH)
 
     def claim(self):
         pl.semaphore_wait(self.credit, 4)
 
-    def finish(self, u):
-        for what in range(3):
-            self.share_out(u, what).wait_send()
+    def finish(self, u, wide=False):
+        for what in range(2 if wide else 3):
+            (self.wide_out if wide else self.share_out)(u, what).wait_send()
         for other in range(1, self.plan.dp // 4):
             self.between(u, other).wait_send()
 
@@ -670,10 +748,6 @@
                     settle(src, self.send.at[q, what])
 
 
-ACROSS = (((1,), (1,)), ((), ()))
-DOWN = (((0,), (0,)), ((), ()))
-
-
 def backward_kernel(
     plan, heads, g0, g1, g2, g3, tok, cot, seg, proj, attn, hid, two, act, der, gain_one, shift_one, gain_two, down_bias,
     blk, tg, o0, o1, o2, vout, *rest,
@@ -683,10 +757,10 @@
     held, every = own * seq + part, plan.rows * seq
     width, ff, three, local = hid.shape[1], act.shape[2], proj.shape[2], attn.shape[2]
     (
-        stage_a, stage_b, loc_a, loc_b, sbl_a, sbl_b, yrc_a, yrc_b, slot_a, slot_b, fin_a, fin_b, fin_c,
+        stage_a, stage_b, loc_a, loc_b, sbl_a, sbl_b, yrc_a, yrc_b, slot_a, slot_b, wide_v, fin_a, fin_b, fin_c,
         grp_a, grp_b, grp_c, out_v,
-    ) = rest[:17]
-    sems, rest = rest[17:29], rest[29:]
+    ) = rest[:18]
+    sems, rest = rest[18:30], rest[30:]
     (
         grad_v, low_v, block_v, tgs, tgo, sums, ups, qbs, msg, vrc, vsum,
         load_sem, wgt_sem, blk_send, blk_recv, tg_send, tg_recv, tgs_send, tgs_recv, tgl_sem, v_send, v_recv,
@@ -694,7 +768,7 @@
     at = Place(plan)
     red = Reducer(
         plan, at, (stage_a, stage_b, stage_a), (loc_a, loc_b, loc_a), (sbl_a, sbl_b, sbl_a), (yrc_a, yrc_b, yrc_a),
-        (slot_a, slot_b, slot_a), (fin_a, fin_b, fin_c), (grp_a, grp_b, grp_c), out_v, sems,
+        (slot_a, slot_b, slot_a), wide_v, (fin_a, fin_b, fin_c), (grp_a, grp_b, grp_c), out_v, sems,
     )
     blocks = RowsOut(plan, at, block_v, block_v.at[own], blk, blk_send, blk_recv)
     greet(plan, at, True)
@@ -702,6 +776,7 @@
     count = len(red.order)
     first = [[part_of(red.first, u, i) for i in range(count)] for u in range(3)]
     step = [[part_of(red.step, u, i) for i in range(count)] for u in range(3)]
+    wide = [part_of(red.wide_step, 0, i) for i in range(count)]
     red.clear(0)
     red.clear(1)
     sums[...] = jnp.zeros(sums.shape, F32)
@@ -763,34 +838,28 @@
                 stage_a[q] = lax.dot_general(lhs, cot_v[...], DOWN, preferred_element_type=F32).astype(BF)
             red.begin(0, i)
 
-            def block(b, total):
-                at_rows = pl.ds(pl.multiple_of(b * part, part), part)
-                act_grad = lax.dot_general(cot_v[at_rows], wd_v[slot], ACROSS, preferred_element_type=F32)
-                low = (act_grad * der_v[slot, at_rows]).astype(BF)
-                low_pre[at_rows] = low
-                grad_v[at_rows] += lax.dot_general(low, wu_v[slot], ACROSS, preferred_element_type=F32)
-                sum_v[at_rows] += jnp.dot(act_v[slot, at_rows], wd_v[slot], preferred_element_type=F32)
-                return total + jnp.sum(low.astype(F32), axis=0, keepdims=True)
-
-            total = lax.fori_loop(0, blocks_held, block, jnp.zeros((1, ff), F32))
-            ups[red.target(i)] = total
+            act_grad = lax.dot_general(cot_v[...], wd_v[slot], ACROSS, preferred_element_type=F32)
+            low = (act_grad * der_v[slot]).astype(BF)
+            low_pre[...] = low
+            ups[red.target(i)] = jnp.sum(low.astype(F32), axis=0, keepdims=True)
             for q in range(4):
                 lhs = low_pre[:, q * rows : (q + 1) * rows]
                 stage_b[q] = lax.dot_general(lhs, two_v[...], DOWN, preferred_element_type=F32).astype(BF)
             red.begin(1, i)
+            grad_v[...] += lax.dot_general(low_pre[...], wu_v[slot], ACROSS, preferred_element_type=F32)
+            sum_v[...] += jnp.dot(act_v[slot], wd_v[slot], preferred_element_type=F32)
 
         table = {}
         for i in range(count - 1):
-            table.setdefault(i + 1, []).append(first[0][i])
+            table.setdefault(i + 1, []).extend([first[1][i], wide[i]])
         for i in range(count - 2):
-            table.setdefault(i + 2, []).append(step[0][i])
+            table.setdefault(i + 2, []).append(step[1][i])
         run(n, body, table)
         red.given(0)
         red.given(1)
-        first[0][count - 1]()
-        first[1][0]()
-        step[0][count - 2]()
-        first[1][1]()
+        first[1][count - 1]()
+        wide[count - 1]()
+        step[1][count - 2]()
 
         @pl.loop(0, blocks_held)
         def _(b):
@@ -815,16 +884,14 @@
         pltpu.VMEM((held, width), BF), pltpu.VMEM((held, width), F32), pltpu.VMEM((held, width), F32),
     )
 
-    def attention(wq_v, wo_v, proj_v, attn_v, head_v, three_v, tok_v, one_v, back_v, out3):
+    def attention(wq_v, wo_v, proj_v, attn_v, head_v, three_v, tok_v, one_v, back_v, out3, columns):
         loads = ((g0, wq_v), (g1, wo_v), (proj, proj_v), (attn, attn_v))
         stream(loads, 0)
         load = pltpu.make_async_copy(tok, tok_v, load_sem.at[0])
         load.start()
-        step[0][count - 1]()
-        red.last(0)
-        for i in range(2, count):
-            first[1][i]()
-        red.spread(0)
+        step[1][count - 1]()
+        red.last(1)
+        red.wide_last(0)
         red.release(0)
         load.wait()
 
@@ -837,46 +904,41 @@
             back_v[rows] = jnp.zeros((part, width), F32)
 
         three_v[...] = jnp.zeros(three_v.shape, BF)
+        label_columns(seg, plan.rows, columns)
+        red.spread(1)
         red.claim()
 
         def body(i):
             stream(loads, i)
             slot = lax.rem(i, 2)
 
-            @pl.loop(0, blocks_held)
-            def _(b):
-                rows = pl.ds(pl.multiple_of(b * part, part), part)
-                grad = lax.dot_general(low_v[rows], wo_v[slot], ACROSS, preferred_element_type=F32)
-                head_v[rows] = grad.astype(BF)
-
-            def head(r, queries, amount, h):
-                col = h * 3 * HEAD_DIM
-                keys = pl.ds(pl.multiple_of(r * seq, seq), seq)
-                query = proj_v[slot, pl.ds(queries, amount), col : col + HEAD_DIM]
-                key = proj_v[slot, keys, col + HEAD_DIM : col + 2 * HEAD_DIM]
-                value = proj_v[slot, keys, col + 2 * HEAD_DIM : col + 3 * HEAD_DIM]
-                head_grad = head_v[pl.ds(queries, amount), h * HEAD_DIM : (h + 1) * HEAD_DIM]
-                line = seg[pl.ds(r, 1)].astype(F32)
-                column = jnp.transpose(jnp.broadcast_to(line, (128, seq)))[:amount, :1]
-                allowed = column == line
-                full = scores_of(query, key, allowed)
-                value_grad = lax.dot_general(full.astype(BF), head_grad, DOWN, preferred_element_type=F32)
-                probs_grad = lax.dot_general(head_grad, value, ACROSS, preferred_element_type=F32)
-                delta = jnp.sum(probs_grad * full, axis=-1, keepdims=True)
-                low = (jnp.where(allowed, full * (probs_grad - delta), 0.0) * HEAD_DIM ** (-0.5)).astype(BF)
-                query_grad = jnp.dot(low, key, preferred_element_type=F32)
-                key_grad = lax.dot_general(low, query, DOWN, preferred_element_type=F32)
-                three_v[pl.ds(queries, amount), col : col + HEAD_DIM] = query_grad.astype(BF)
-                three_v[keys, col + HEAD_DIM : col + 2 * HEAD_DIM] = key_grad.astype(BF)
-                three_v[keys, col + 2 * HEAD_DIM : col + 3 * HEAD_DIM] = value_grad.astype(BF)
+            head_v[...] = lax.dot_general(low_v[...], wo_v[slot], ACROSS, preferred_element_type=F32).astype(BF)
+
+            def attend(r, first, amount):
+                allowed = same_image(seg, columns, r, amount)
+                keys, queries = pl.ds(pl.multiple_of(r * seq, seq), seq), pl.ds(first, amount)
+                for h in range(heads):
+                    col = h * 3 * HEAD_DIM
+                    query = proj_v[slot, queries, col : col + HEAD_DIM]
+                    key = proj_v[slot, keys, col + HEAD_DIM : col + 2 * HEAD_DIM]
+                    value = proj_v[slot, keys, col + 2 * HEAD_DIM : col + 3 * HEAD_DIM]
+                    head_grad = head_v[queries, h * HEAD_DIM : (h + 1) * HEAD_DIM]
+                    full = probs_of(key, query, allowed)
+                    value_grad = jnp.dot(full.astype(BF), head_grad, preferred_element_type=F32)
+                    probs_grad = lax.dot_general(value, head_grad, ACROSS, preferred_element_type=F32)
+                    delta = jnp.sum(probs_grad * full, axis=0, keepdims=True)
+                    low = (jnp.where(allowed, full * (probs_grad - delta), 0.0) * HEAD_DIM ** (-0.5)).astype(BF)
+                    query_grad = lax.dot_general(low, key, DOWN, preferred_element_type=F32)
+                    key_grad = jnp.dot(low, query, preferred_element_type=F32)
+                    three_v[queries, col : col + HEAD_DIM] = query_grad.astype(BF)
+                    three_v[keys, col + HEAD_DIM : col + 2 * HEAD_DIM] = key_grad.astype(BF)
+                    three_v[keys, col + 2 * HEAD_DIM : col + 3 * HEAD_DIM] = value_grad.astype(BF)
 
             @pl.loop(0, own)
             def _(r):
-                for h in range(heads):
-                    head(r, pl.multiple_of(r * seq, seq), seq, h)
-
-            for h in range(heads):
-                head(own, own * seq, part, h)
+                attend(r, pl.multiple_of(r * seq, seq), seq)
+
+            attend(own, own * seq, part)
 
             @pl.when(i > 0)
             def _():
@@ -890,23 +952,18 @@
                 stage_a[q, wide:] = out_weight[q * narrow : (q + 1) * narrow]
             red.begin(2, i)
 
-            def block(b, total):
-                rows = pl.ds(pl.multiple_of(b * part, part), part)
-                low = three_v[rows]
-                back_v[rows] += lax.dot_general(low, wq_v[slot], ACROSS, preferred_element_type=F32)
-                return total + jnp.sum(low.astype(F32), axis=0, keepdims=True)
-
-            qbs[red.target(i)] = lax.fori_loop(0, plan.rows * share, block, jnp.zeros((1, three), F32))
-
-        table = {}
-        for i in range(count):
-            table.setdefault(i, []).append(step[1][i])
-            if i + 1 < count:
-                table.setdefault(i + 1, []).append(first[2][i])
+            back_v[...] += lax.dot_general(three_v[...], wq_v[slot], ACROSS, preferred_element_type=F32)
+            qbs[red.target(i)] = jnp.sum(three_v[...].astype(F32), axis=0, keepdims=True)
+
+        table = {2: [part_of(red.write, 0, o0, True)], 3: [part_of(red.write, 1, o1)]}
+        for i in range(count - 1):
+            table.setdefault(i + 1, []).append(first[2][i])
+        for i in range(count - 2):
+            table.setdefault(i + 2, []).append(step[2][i])
         run(n, body, table)
-        red.last(1)
         red.given(2)
         first[2][count - 1]()
+        step[2][count - 2]()
 
         @pl.loop(0, plan.rows * share)
         def _(b):
@@ -957,29 +1014,22 @@
 
         lax.fori_loop(1, plan.all, one, 0)
         pltpu.make_async_copy(msg.at[at.m], vrc.at[me], v_recv.at[0]).start()
-        step[2][0]()
         for e in range(1, share):
             settle(tgs.at[e], tgs_recv.at[e])
         settle(tgs.at[0], tgl_sem.at[0])
         tgo[...] = sum(tgs[e].astype(F32) for e in range(share)).astype(BF)
         tokens.start(1)
-        step[2][1]()
-        red.spread(1)
+        step[2][count - 1]()
+        red.last(2)
         settle(vrc, v_recv.at[0])
         vsum[...] = jnp.sum(vrc[...], axis=0)
         for e in range(1, n):
             remote(vsum, vout.at[at.m], v_send.at[1], v_recv.at[1], mp=lax.rem(at.m + e, n)).start()
         pltpu.make_async_copy(vsum, vout.at[at.m], v_recv.at[1]).start()
-        red.write(0, o0)
-        for i in range(2, count):
-            step[2][i]()
-            if i == 3:
-                red.write(1, o1)
-        red.last(2)
         red.spread(2)
         red.write(2, o2)
         for u in range(3):
-            red.finish(u)
+            red.finish(u, u == 0)
         red.sent(1)
         red.sent(2)
         for e in range(1, share):
@@ -995,7 +1045,7 @@
         pltpu.VMEM((2,) + g0.shape[1:], BF), pltpu.VMEM((2,) + g1.shape[1:], BF), pltpu.VMEM((2, every, three), BF),
         pltpu.VMEM((2, held, local), BF), pltpu.VMEM((held, local), BF), pltpu.VMEM((every, three), BF),
         pltpu.VMEM((plan.rows, seq, width), BF), pltpu.VMEM((every, width), BF), pltpu.VMEM((every, width), F32),
-        pltpu.VMEM((plan.rows, seq, width), BF),
+        pltpu.VMEM((plan.rows, seq, width), BF), pltpu.VMEM((plan.rows, seq, 128), F32),
     )
 
 
@@ -1025,8 +1075,10 @@
             *[pltpu.VMEM((2, n, quarter, width), BF)] * 4,
             *[pltpu.VMEM((n, quarter, width), BF)] * 2,
             *[pltpu.VMEM((2, plan.hops, quarter, width), BF)] * 2,
+            pltpu.VMEM((2, plan.hops, 2, quarter, width), BF),
             *[pltpu.VMEM((ff, width), BF)] * 3,
-            *[pltpu.VMEM((quads,) + ((quarter, width) if quads > 1 else (8, 128)), BF)] * 3,
+            pltpu.VMEM((quads, 2) + ((quarter, width) if quads > 1 else (8, 128)), BF),
+            *[pltpu.VMEM((quads,) + ((quarter, width) if quads > 1 else (8, 128)), BF)] * 2,
             pltpu.VMEM((2, quarter, width), F32),
             dma((3,)), dma((3, n, 2)), dma((3,)), dma((3, n)), dma((3, 2)), dma((3, 2, plan.hops)), dma((3,)), dma((3,)),
             dma((3, 3)), dma((3, 3)), dma((2,)), pltpu.SemaphoreType.REGULAR,
@@ -1044,11 +1096,25 @@
     )(*weights, tok3, cot3, seg, proj, attn, hid, two, act, der, *vectors)
 
 
-def scores_of(query, key, allowed):
-    raw = lax.dot_general(query, key, (((1,), (1,)), ((), ())), preferred_element_type=F32)
+def probs_of(key, query, allowed):
+    raw = lax.dot_general(key, query, ACROSS, preferred_element_type=F32)
     scores = jnp.where(allowed, raw * HEAD_DIM ** (-0.5), MASKED)
-    raised = jnp.exp(scores - jnp.max(scores, axis=-1, keepdims=True))
-    return raised / jnp.sum(raised, axis=-1, keepdims=True)
+    raised = jnp.exp(scores - jnp.max(scores, axis=0, keepdims=True))
+    return raised * (1.0 / jnp.sum(raised, axis=0, keepdims=True))
+
+
+def label_columns(labels, rows, columns):
+    for r in range(rows):
+        line = labels[pl.ds(r, 1)].astype(F32)
+        columns[r] = jnp.transpose(jnp.broadcast_to(line, (128, line.shape[1])))
+
+
+def same_image(labels, columns, r, amount):
+    line = labels[pl.ds(r, 1)].astype(F32)[:, :amount]
+    down = columns[r]
+    if amount < 128:
+        return down[:, :amount] == line
+    return jnp.concatenate([down] * (amount // 128), axis=1) == line
 
 
 def norm(values, gain_vec, shift_vec):

time: 468 us -> 412 us (0.88)
  Pallas kernels: 447 us -> 392 us
    pallas_call x1, Pallas kernels: 257 us -> 210 us  [backward(): pl.pallas_call(functools.partial(backward_kernel, plan, heads), out_shape...]
    pallas_call x1, Pallas kernels: 190 us -> 182 us  [forward(): pl.pallas_call(functools.partial(forward_kernel, plan, heads), out_shape=...]
where the time goes in v4:
time: 412 us; the launch traced here: 408 us
  Pallas kernels  392 us (95%)
  local copies, waits for them, and re-layouts  13.7 us (3%)
    pallas_call x1, Pallas kernels, backward(): pl.pallas_call(functools.partial(backward_kernel, plan, heads), out_shape...  210 us
    pallas_call x1, Pallas kernels, forward(): pl.pallas_call(functools.partial(forward_kernel, plan, heads), out_shape=...  182 us

profile of v4, /device:TPU:11, one launch (start us, length us, event | category | flops | bytes accessed | tf_op | source)
XLA Modules:
  0.0 408.5 jit_solution(8233960192804172756)
XLA Ops:
  0.6 0.8 slice_reduce_fusion.3
  1.4 0.1 stack_squeeze.8
  1.5 0.1 stack_squeeze.9
  1.6 0.1 pad.3.clone
  1.7 0.1 pad_maximum_fusion
  1.7 0.6 reshape.94.bq
  2.4 181.7 %forward.1 = (bf16[3,256,1024]{2,1,0:T(8,128)(2,1)}, bf16[3,256,1024]{2,1,0:T(8,128)(2,1)}, s32[3,256]{1,0:T(4,128)}, bf16[8,1024,384]{2,1,0:T(8,128)(2,1)}, bf1...) custom-call(bf16[20,32,1024]{2,1,0:T(8,128)(2,1)} %tok.1, ...), custom_call_target="tpu_custom_call" | custom-call | tf_op jit(solution)/shard_map/forward/pallas_call | solution.py:427
  184.1 210.0 %backward.1 = (bf16[20,32,1024]{2,1,0:T(8,128)(2,1)}, bf16[20,32,1024]{2,1,0:T(8,128)(2,1)}, f32[512,1024]{1,0:T(8,128)}, f32[512,1024]{1,0:T(8,128)}, f32[512,1024]{1,0:T(8,128)}, /*index=5*/f32[8,16,128]{2,1,0:T(8,128)}) custom-call(bf16[8,1024,384]{2,1,0:T(8,128)(2,1)} %get-tuple-element.33.g0, bf16[8,128,1024]{2,1,0:T(8,128)(2,1)} %get-tuple-element.34.g1, ...), custom_call_target="tpu_custom_call" | custom-call | tf_op jit(solution)/shard_map/backward/pallas_call | solution.py:1068
  394.0 0.7 constant_dynamic-slice_fusion
  394.7 0.1 reshape_reshape.3
  394.8 0.1 stack.11
  394.9 0.1 stack.12
  395.0 0.6 pad_maximum_fusion.1
  395.6 1.5 slice.72
  397.1 1.6 copy.35
  398.7 0.0 copy-done.3
  398.7 1.8 convert_element_type.3
  400.5 0.5 copy-done.1
  401.0 1.8 copy.36
  402.8 2.0 slice.75
  404.9 0.6 fusion
  405.5 0.6 dynamic-slice_bitcast_fusion
  406.1 1.1 copy.39
  407.1 1.3 copy.40
  (11 shorter events, 0.0 us)
Async XLA Ops:
  397.1 1.6 copy-start.3
  398.7 2.3 copy-start.1
  401.0 3.8 copy-start.4
  401.0 5.1 %copy-start.2 = (bf16[20,32,1024]{2,1,0:T(8,128)(2,1)S(1)}, bf16[20,32,1024]{2,1,0:T(8,128)(2,1)}, u32[]{:S(2)}) copy-start(bf16[20,32,1024]{2,1,0:T(8,128)(2,1)} %get-tuple-element.104) | copy-start | bytes 3932164
  402.8 4.3 %copy-start = (f32[512,1024]{1,0:T(8,128)S(1)}, f32[512,1024]{1,0:T(8,128)}, u32[]{:S(2)}) copy-start(f32[512,1024]{1,0:T(8,128)} %get-tuple-element.116) | copy-start | bytes 6291460

commit v5 on v4

--- a/solution.py
+++ b/solution.py
@@ -1,4 +1,5 @@
 import functools
+import itertools
 import math
 
 import jax
@@ -16,6 +17,10 @@
 F32 = jnp.float32
 ACROSS = (((1,), (1,)), ((), ()))
 DOWN = (((0,), (0,)), ((), ()))
+
+
+WIDE_FIRST, WIDE_PACE = 1, 4
+BLOCKS_MID, BLOCKS_OVER = 8, 4
 
 
 class Plan:
@@ -214,16 +219,17 @@
                 settle(src, self.send.at[j, e, what])
 
 
-def run(count, body, table):
+def run(count, body, *tables):
     def one(j, carry):
-        for when, thunks in sorted(table.items()):
-
-            @pl.when(j == when)
-            def _():
-                for thunk in thunks:
-                    thunk()
-
-        body(j)
+        def take(k):
+            for when, thunks in sorted(tables[k].items()):
+
+                @pl.when(j == when)
+                def _():
+                    for thunk in thunks:
+                        thunk()
+
+        body(j, take)
         return carry
 
     lax.fori_loop(0, count, one, 0)
@@ -257,7 +263,8 @@
     greet(plan, at, False)
 
     gat.begin(0)
-    tokens.start()
+    gat.begin(2)
+    tokens.start(0)
     biases = ((bq, bq_v, 0), (bu, bu_v, 1))
     for src, dst, i in biases:
         pltpu.make_async_copy(src, dst.at[at.m], bias_recv.at[i]).start()
@@ -269,19 +276,16 @@
     part_of = functools.partial
     hop = [[part_of(gat.step, w, s) for s in range(hops)] for w in range(4)]
     after = [[part_of(gat.follow, w, s) for s in range(hops)] for w in range(4)]
-    gat.begin(1)
-    gat.begin(2)
-    hop[0][0]()
-    for s in range(1, hops):
+    begin = [part_of(gat.begin, w) for w in range(4)]
+    token = [part_of(tokens.start, j) for j in range(plan.groups)]
+    between = {0: [begin[3], hop[2][0]] + token[1:2], 1: token[2:3] + [hop[2][1], after[2][0]], 2: token[3:] + [hop[3][0]]}
+    between[hops - 1] = between.get(hops - 1, []) + [hop[2][2], after[2][1], begin[1]]
+    for s in range(hops):
         hop[0][s]()
-        after[0][s - 1]()
-        if s == 1:
-            hop[2][0]()
-        if s == 2:
-            hop[1][0]()
-            after[2][0]()
-            gat.begin(3)
-    after[1][0]()
+        if s:
+            after[0][s - 1]()
+        for thunk in between.get(s, []):
+            thunk()
     after[0][hops - 1]()
     tokens.arrived()
     save_tok = pltpu.make_async_copy(tok_v, tok_o, save_sem.at[0])
@@ -315,7 +319,8 @@
     load_q.start()
     load_q.wait()
 
-    def attend_shard(s):
+    def attend_shard(s, take):
+        take(0)
         projected = jnp.dot(one_v[...], wq_v[s], preferred_element_type=F32) + bq_v[s]
         proj_v[s] = projected.astype(BF)
 
@@ -335,17 +340,21 @@
         def _(r):
             attend(r, pl.multiple_of(r * seq, seq), seq)
 
+        take(1)
         attend(own, own * seq, part)
 
+    rest = []
+    for w, done in ((2, 3), (3, 1), (1, 0)):
+        steps = [hop[w][s : s + 1] + (after[w][s - 1 : s] if s else []) for s in range(done, hops)]
+        rest.append(steps + [after[w][hops - 1 :]])
+    rest.append([[part_of(cots.start, j)] for j in range(plan.groups)])
     moves = []
-    for s in range(1, hops):
-        moves += [hop[2][s], hop[1][s], part_of(cots.start, s - 1)]
-        moves += [hop[3][s - 1], after[2][s], after[1][s]]
-        moves += [after[3][s - 2]] if s > 1 else []
-    for j in range(hops - 1, plan.groups):
-        moves.append(part_of(cots.start, j))
-    comm = spread_over(n, moves)
-    run(n, attend_shard, comm)
+    for at_once in itertools.zip_longest(*rest):
+        moves += [thunks for thunks in at_once if thunks]
+    tables = ({}, {})
+    for j, thunks in spread_over(2 * n, moves).items():
+        tables[j % 2][j // 2] = [thunk for some in thunks for thunk in some]
+    run(n, attend_shard, *tables)
     save_proj = pltpu.make_async_copy(proj_v, proj_o, save_sem.at[1])
     save_proj.start()
     save_attn = pltpu.make_async_copy(attn_v, attn_o, save_sem.at[2])
@@ -375,14 +384,12 @@
     save_hid.start()
     save_two = pltpu.make_async_copy(two_v, two_o, save_sem.at[4])
     save_two.start()
-    after[3][hops - 2]()
-    hop[3][hops - 1]()
     gat.arrived(2)
     load_u = pltpu.make_async_copy(g2, wu_v, load_sem.at[0])
     load_u.start()
     load_u.wait()
 
-    def feed_shard(s):
+    def feed_shard(s, take):
         pre = jnp.dot(two_v[...], wu_v[s], preferred_element_type=F32) + bu_v[s]
         below = 0.5 * (1.0 + lax.erf(pre * math.sqrt(0.5)))
         density = jnp.exp(-0.5 * pre * pre) * (1.0 / math.sqrt(2.0 * math.pi))
@@ -392,8 +399,7 @@
         pltpu.make_async_copy(act_v.at[s], act_o.at[s], act_sem.at[0]).start()
         pltpu.make_async_copy(der_v.at[s], der_o.at[s], act_sem.at[1]).start()
 
-    run(n, feed_shard, {})
-    after[3][hops - 1]()
+    run(n, feed_shard)
     gat.arrived(3)
     for w in range(4):
         gat.finish(w)
@@ -487,6 +493,9 @@
         for way in range(2):
             part = half_of(self.slot[u].at[way, 0], 1 - way)
             part[...] = jnp.zeros(part.shape, BF)
+
+    def wide_clear(self):
+        for way in range(2):
             for yy in range(2):
                 part = half_of(self.wide.at[way, 0, yy], 1 - way)
                 part[...] = jnp.zeros(part.shape, BF)
@@ -678,7 +687,15 @@
                 settle(self.out.at[slot], self.out_sem.at[slot])
 
             self.out[slot] = self.fin[u][at].astype(F32)
-            pltpu.make_async_copy(self.out.at[slot], dst.at[at], self.out_sem.at[slot]).start()
+            begun = 0
+            for ref in dst:
+                size = ref.shape[0] // 4
+                pltpu.make_async_copy(
+                    self.out.at[slot, pl.ds(begun, size)],
+                    ref.at[pl.ds(pl.multiple_of(q * size, size), size)],
+                    self.out_sem.at[slot],
+                ).start()
+                begun += size
 
         for slot in range(2):
             settle(self.out.at[slot], self.out_sem.at[slot])
@@ -692,7 +709,7 @@
 
     def release(self, u):
         at = self.at
-        self.wide_sent(u)
+        self.sent(u)
         for to in ({"dp": at.sib}, {"dp": at.other}, {"mp": at.neighbour[0]}, {"mp": at.neighbour[1]}):
             pl.semaphore_signal(self.credit, inc=1, device_id=to, device_id_type=MESH)
 
@@ -727,8 +744,10 @@
                     self.first + plan.own * plan.share
                 ]
 
-    def start(self, what):
+    def start(self, what, only=None):
         for q, here, wanted, src, dst in self.copies(what):
+            if only is not None and only != q:
+                continue
 
             @pl.when(jnp.logical_and(here, wanted))
             def _():
@@ -750,25 +769,25 @@
 
 def backward_kernel(
     plan, heads, g0, g1, g2, g3, tok, cot, seg, proj, attn, hid, two, act, der, gain_one, shift_one, gain_two, down_bias,
-    blk, tg, o0, o1, o2, vout, *rest,
+    blk, tg, o0, o1, o2, o3, vout, *rest,
 ):
     n, share, own, part, seq = plan.mp, plan.share, plan.own, plan.part, plan.seq
     hops = plan.hops
     held, every = own * seq + part, plan.rows * seq
     width, ff, three, local = hid.shape[1], act.shape[2], proj.shape[2], attn.shape[2]
     (
-        stage_a, stage_b, loc_a, loc_b, sbl_a, sbl_b, yrc_a, yrc_b, slot_a, slot_b, wide_v, fin_a, fin_b, fin_c,
+        stage_a, stage_b, loc_a, loc_b, sbl_a, sbl_b, yrc_a, yrc_b, slot_b, wide_v, fin_a, fin_b, fin_c,
         grp_a, grp_b, grp_c, out_v,
-    ) = rest[:18]
-    sems, rest = rest[18:30], rest[30:]
+    ) = rest[:17]
+    sems, rest = rest[17:29], rest[29:]
     (
         grad_v, low_v, block_v, tgs, tgo, sums, ups, qbs, msg, vrc, vsum,
         load_sem, wgt_sem, blk_send, blk_recv, tg_send, tg_recv, tgs_send, tgs_recv, tgl_sem, v_send, v_recv,
     ) = rest
     at = Place(plan)
     red = Reducer(
-        plan, at, (stage_a, stage_b, stage_a), (loc_a, loc_b, loc_a), (sbl_a, sbl_b, sbl_a), (yrc_a, yrc_b, yrc_a),
-        (slot_a, slot_b, slot_a), wide_v, (fin_a, fin_b, fin_c), (grp_a, grp_b, grp_c), out_v, sems,
+        plan, at, (stage_a, stage_b, stage_b), (loc_a, loc_b, loc_b), (sbl_a, sbl_b, sbl_b), (yrc_a, yrc_b, yrc_b),
+        (None, slot_b, slot_b), wide_v, (fin_a, fin_b, fin_c), (grp_a, grp_b, grp_c), out_v, sems,
     )
     blocks = RowsOut(plan, at, block_v, block_v.at[own], blk, blk_send, blk_recv)
     greet(plan, at, True)
@@ -777,7 +796,8 @@
     first = [[part_of(red.first, u, i) for i in range(count)] for u in range(3)]
     step = [[part_of(red.step, u, i) for i in range(count)] for u in range(3)]
     wide = [part_of(red.wide_step, 0, i) for i in range(count)]
-    red.clear(0)
+    when_wide = [WIDE_FIRST + i * WIDE_PACE // 4 for i in range(count)]
+    red.wide_clear()
     red.clear(1)
     sums[...] = jnp.zeros(sums.shape, F32)
     blocks_held = own * share + 1
@@ -823,7 +843,8 @@
             sum_v[rows] = hid_v[rows] + down_bias[...]
             grad_v[rows] = jnp.zeros((part, width), F32)
 
-        def body(i):
+        def body(i, take):
+            take(0)
             stream(loads, i)
             slot = lax.rem(i, 2)
             rows = ff // 4
@@ -837,6 +858,7 @@
                 lhs = act_v[slot, :, q * rows : (q + 1) * rows]
                 stage_a[q] = lax.dot_general(lhs, cot_v[...], DOWN, preferred_element_type=F32).astype(BF)
             red.begin(0, i)
+            take(1)
 
             act_grad = lax.dot_general(cot_v[...], wd_v[slot], ACROSS, preferred_element_type=F32)
             low = (act_grad * der_v[slot]).astype(BF)
@@ -849,16 +871,18 @@
             grad_v[...] += lax.dot_general(low_pre[...], wu_v[slot], ACROSS, preferred_element_type=F32)
             sum_v[...] += jnp.dot(act_v[slot], wd_v[slot], preferred_element_type=F32)
 
-        table = {}
+        table, middle = {}, {}
         for i in range(count - 1):
-            table.setdefault(i + 1, []).extend([first[1][i], wide[i]])
+            table.setdefault(i + 1, []).append(first[1][i])
+        for i in range(count):
+            if when_wide[i] < n:
+                middle.setdefault(when_wide[i], []).append(wide[i])
         for i in range(count - 2):
             table.setdefault(i + 2, []).append(step[1][i])
-        run(n, body, table)
+        run(n, body, table, middle)
         red.given(0)
         red.given(1)
         first[1][count - 1]()
-        wide[count - 1]()
         step[1][count - 2]()
 
         @pl.loop(0, blocks_held)
@@ -874,8 +898,10 @@
             for line, value in ((2, hidden_grad), (3, grad * unit), (4, grad), (5, cot_f)):
                 sums[pl.ds(line, 1)] += jnp.sum(value, axis=0, keepdims=True)
 
-        blocks.start(0)
-        blocks.start(1)
+        for q in range(n):
+            if q < BLOCKS_MID:
+                blocks.start(0, q)
+                blocks.start(1, q)
 
     pl.run_scoped(
         feed_forward,
@@ -891,8 +917,7 @@
         load.start()
         step[1][count - 1]()
         red.last(1)
-        red.wide_last(0)
-        red.release(0)
+        red.release(1)
         load.wait()
 
         @pl.loop(0, plan.rows * share)
@@ -906,9 +931,9 @@
         three_v[...] = jnp.zeros(three_v.shape, BF)
         label_columns(seg, plan.rows, columns)
         red.spread(1)
-        red.claim()
-
-        def body(i):
+
+        def body(i, take):
+            take(0)
             stream(loads, i)
             slot = lax.rem(i, 2)
 
@@ -938,29 +963,42 @@
             def _(r):
                 attend(r, pl.multiple_of(r * seq, seq), seq)
 
+            take(1)
             attend(own, own * seq, part)
 
             @pl.when(i > 0)
             def _():
                 red.given(2)
+
+            @pl.when(i == 0)
+            def _():
+                red.claim()
 
             wide, narrow = three // 4, local // 4
             weight = lax.dot_general(three_v[...], one_v[...], DOWN, preferred_element_type=F32).astype(BF)
             out_weight = lax.dot_general(attn_v[slot], low_v[...], DOWN, preferred_element_type=F32).astype(BF)
             for q in range(4):
-                stage_a[q, :wide] = weight[q * wide : (q + 1) * wide]
-                stage_a[q, wide:] = out_weight[q * narrow : (q + 1) * narrow]
+                stage_b[q, :wide] = weight[q * wide : (q + 1) * wide]
+                stage_b[q, wide:] = out_weight[q * narrow : (q + 1) * narrow]
             red.begin(2, i)
 
             back_v[...] += lax.dot_general(three_v[...], wq_v[slot], ACROSS, preferred_element_type=F32)
             qbs[red.target(i)] = jnp.sum(three_v[...].astype(F32), axis=0, keepdims=True)
 
-        table = {2: [part_of(red.write, 0, o0, True)], 3: [part_of(red.write, 1, o1)]}
+        late = max(when_wide[-1] - n + 1, 1)
+        table = {3: [part_of(red.write, 1, (o1,))]}
+        table.setdefault(late, []).append(part_of(red.wide_last, 0))
+        table.setdefault(min(late + 2, n - 1), []).append(part_of(red.write, 0, (o0,), True))
+        for i in range(count):
+            if when_wide[i] >= n:
+                table.setdefault(when_wide[i] - n, []).insert(0, wide[i])
         for i in range(count - 1):
-            table.setdefault(i + 1, []).append(first[2][i])
-        for i in range(count - 2):
-            table.setdefault(i + 2, []).append(step[2][i])
-        run(n, body, table)
+            table.setdefault(i + 1, []).insert(0, first[2][i])
+        middle = {i + 2: [step[2][i]] for i in range(count - 2)}
+        for q in range(BLOCKS_MID, n):
+            for what in range(2):
+                table.setdefault((q - BLOCKS_MID) * BLOCKS_OVER // n, []).append(part_of(blocks.start, what, q))
+        run(n, body, table, middle)
         red.given(2)
         first[2][count - 1]()
         step[2][count - 2]()
@@ -992,8 +1030,6 @@
             else:
                 to = at.base + lax.rem(at.k + e, share)
                 remote(src, tgs.at[share - e], tgs_send.at[e], tgs_recv.at[share - e], dp=to).start()
-        tokens.start(0)
-
         lines = [-(-size // 128) for size in (ff, three)]
         msg[...] = jnp.zeros(msg.shape, F32)
         for q in range(n):
@@ -1014,6 +1050,7 @@
 
         lax.fori_loop(1, plan.all, one, 0)
         pltpu.make_async_copy(msg.at[at.m], vrc.at[me], v_recv.at[0]).start()
+        tokens.start(0)
         for e in range(1, share):
             settle(tgs.at[e], tgs_recv.at[e])
         settle(tgs.at[0], tgl_sem.at[0])
@@ -1027,10 +1064,10 @@
             remote(vsum, vout.at[at.m], v_send.at[1], v_recv.at[1], mp=lax.rem(at.m + e, n)).start()
         pltpu.make_async_copy(vsum, vout.at[at.m], v_recv.at[1]).start()
         red.spread(2)
-        red.write(2, o2)
+        red.write(2, (o2, o3))
         for u in range(3):
             red.finish(u, u == 0)
-        red.sent(1)
+        red.wide_sent(0)
         red.sent(2)
         for e in range(1, share):
             settle(tgs.at[0], tgs_send.at[e])
@@ -1067,14 +1104,18 @@
     vec = (size, 128)
     return pl.pallas_call(
         functools.partial(backward_kernel, plan, heads),
-        out_shape=[rows, rows, shard, shard, shard, jax.ShapeDtypeStruct((n,) + vec, F32)],
+        out_shape=[
+            rows, rows, shard, shard, jax.ShapeDtypeStruct((three, width), F32), jax.ShapeDtypeStruct((local, width), F32),
+            jax.ShapeDtypeStruct((n,) + vec, F32),
+        ],
         in_specs=[any_space] * 6 + [in_vmem] + [any_space] * 6 + [in_vmem] * 4,
-        out_specs=[any_space] * 6,
+        out_specs=[any_space] * 7,
         scratch_shapes=[
             *[pltpu.VMEM((4, quarter, width), BF)] * 2,
             *[pltpu.VMEM((2, n, quarter, width), BF)] * 4,
-            *[pltpu.VMEM((n, quarter, width), BF)] * 2,
-            *[pltpu.VMEM((2, plan.hops, quarter, width), BF)] * 2,
+            pltpu.VMEM((4, quarter, width), BF),
+            pltpu.VMEM((n, quarter, width), BF),
+            pltpu.VMEM((2, plan.hops, quarter, width), BF),
             pltpu.VMEM((2, plan.hops, 2, quarter, width), BF),
             *[pltpu.VMEM((ff, width), BF)] * 3,
             pltpu.VMEM((quads, 2) + ((quarter, width) if quads > 1 else (8, 128)), BF),
@@ -1144,14 +1185,11 @@
         plan, tokens_in, cotangent, segment_ids, (bias_three, up_bias.reshape(1, ff_local)),
         (qkv_weight, out_weight, up_weight, down_weight), vectors,
     )
-    block_out, tokens_low, down_grad, up_grad, rest_grad, sums = backward(
+    block_out, tokens_low, down_grad, up_grad, qkv_grad, out_grad, sums = backward(
         plan, (wq, wo, wu, wd), tok3, cot3, seg, proj, attn, hidden, normed_two, act_low, gelu_slope,
         [v.reshape(1, width) for v in (attn_gain, attn_shift, mlp_gain, down_bias)],
     )
     local, three = out_weight.shape[0], qkv_weight.shape[1]
-    rest_grad = rest_grad.reshape(4, (local + three) // 4, width)
-    qkv_grad = rest_grad[:, : three // 4].reshape(three, width).T
-    out_grad = rest_grad[:, three // 4 :].reshape(local, width)
     six = jnp.swapaxes(sums[:, :6, : width // n], 0, 1).reshape(6, width)
     mine = lax.dynamic_index_in_dim(sums, lax.axis_index("mp"), 0, keepdims=False)
     lines = [-(-size // 128) for size in (ff_local, three)]
@@ -1159,7 +1197,7 @@
     bias_sums = mine[8 + lines[0] : 8 + sum(lines)].reshape(-1)[:three].reshape(heads_local, 3, HEAD_DIM)
     qkv_bias_grad = jnp.stack([bias_sums[:, 0], bias_sums[:, 2]]).reshape(2, local)
     return (
-        block_out, tokens_low.astype(F32), six[0], six[1], qkv_grad, qkv_bias_grad, out_grad, six[2], six[3], six[4],
+        block_out, tokens_low.astype(F32), six[0], six[1], qkv_grad.T, qkv_bias_grad, out_grad, six[2], six[3], six[4],
         up_grad.T, up_bias_grad, down_grad, six[5],
     )
 

time: 412 us -> 394 us (0.956)
  Pallas kernels: 392 us -> 375 us
    pallas_call x1, Pallas kernels: 182 us -> 166 us  [forward(): pl.pallas_call(functools.partial(forward_kernel, plan, heads), out_shape=...]
where the time goes in v5:
time: 394 us; the launch traced here: 392 us
  Pallas kernels  375 us (95%)
  local copies, waits for them, and re-layouts  12.1 us (3%)
    pallas_call x1, Pallas kernels, backward(): pl.pallas_call(functools.partial(backward_kernel, plan, heads), out_shape...  210 us
    pallas_call x1, Pallas kernels, forward(): pl.pallas_call(functools.partial(forward_kernel, plan, heads), out_shape=...  166 us
    unnamed x15, local copies, waits for them, and re-layouts  8.12 us

profile of v5, /device:TPU:11, one launch (start us, length us, event | category | flops | bytes accessed | tf_op | source)
XLA Modules:
  0.0 391.7 jit_solution(17265354390075414639)
XLA Ops:
  0.6 0.8 slice_reduce_fusion.3
  1.4 0.1 stack_squeeze.8
  1.5 0.1 stack_squeeze.9
  1.6 0.1 pad.3.clone
  1.7 0.1 pad_maximum_fusion
  1.7 0.6 reshape.85.bq
  2.4 165.6 %forward.1 = (bf16[3,256,1024]{2,1,0:T(8,128)(2,1)}, bf16[3,256,1024]{2,1,0:T(8,128)(2,1)}, s32[3,256]{1,0:T(4,128)}, bf16[8,1024,384]{2,1,0:T(8,128)(2,1)}, bf1...) custom-call(bf16[20,32,1024]{2,1,0:T(8,128)(2,1)} %tok.1, ...), custom_call_target="tpu_custom_call" | custom-call | tf_op jit(solution)/shard_map/forward/pallas_call | solution.py:433
  168.0 209.5 %backward.1 = (bf16[20,32,1024]{2,1,0:T(8,128)(2,1)}, bf16[20,32,1024]{2,1,0:T(8,128)(2,1)}, f32[512,1024]{1,0:T(8,128)}, f32[512,1024]{1,0:T(8,128)}, f32[384,1...) custom-call(bf16[8,1024,384]{2,1,0:T(8,128)(2,1)} %get-tuple-element.34.g0, ...), custom_call_target="tpu_custom_call" | custom-call | tf_op jit(solution)/shard_map/backward/pallas_call | solution.py:1105
  377.5 0.0 copy-start.1
  377.5 0.8 constant_dynamic-slice_fusion
  378.4 0.1 reshape_reshape.3
  378.5 0.1 stack.11
  378.6 0.1 stack.12
  378.6 0.6 pad_maximum_fusion.1
  379.2 3.1 convert_element_type.3
  382.4 0.0 copy-done.1
  382.4 1.8 copy.36
  384.2 3.1 copy.35
  387.3 0.0 copy-done.4
  387.3 0.6 fusion
  387.9 0.6 dynamic-slice_bitcast_fusion
  388.5 1.1 copy.40
  389.6 0.8 copy.41
  390.4 1.3 copy.42
  (10 shorter events, 0.0 us)
Async XLA Ops:
  377.5 4.8 %copy-start.1 = (f32[512,1024]{1,0:T(8,128)S(1)}, f32[512,1024]{1,0:T(8,128)}, u32[]{:S(2)}) copy-start(f32[512,1024]{1,0:T(8,128)} %get-tuple-element.52) | copy-start | bytes 6291460
  384.2 3.1 copy-start.4
  384.2 4.4 %copy-start.2 = (bf16[20,32,1024]{2,1,0:T(8,128)(2,1)S(1)}, bf16[20,32,1024]{2,1,0:T(8,128)(2,1)}, u32[]{:S(2)}) copy-start(bf16[20,32,1024]{2,1,0:T(8,128)(2,1)} %get-tuple-element.106) | copy-start | bytes 3932164
  387.3 3.1 copy-start
  387.9 1.6 copy-start.3

commit v6 on v5

--- a/solution.py
+++ b/solution.py
@@ -77,7 +77,11 @@
         return carry
 
     lax.fori_loop(0, span * plan.mp, one, 0)
-    pl.semaphore_wait(barrier, span * plan.mp - 1)
+
+
+def meet(plan, everyone):
+    span = plan.dp if everyone else max(plan.share, 4)
+    pl.semaphore_wait(pltpu.get_barrier_semaphore(), span * plan.mp - 1)
 
 
 def remote(src, dst, send, recv, **to):
@@ -172,9 +176,8 @@
 
 
 class RowsIn:
-    def __init__(self, plan, at, src, dst, send, recv, whole_shared):
+    def __init__(self, plan, at, src, dst, send, recv):
         self.plan, self.at, self.src, self.dst, self.send, self.recv = plan, at, src, dst, send, recv
-        self.whole_shared = whole_shared
 
     def copies(self):
         plan, at = self.plan, self.at
@@ -184,7 +187,7 @@
             first = j * plan.group_rows
             for e in range(plan.share):
                 here = jnp.logical_and(at.k == e, at.m == q)
-                holds = True if self.whole_shared else lax.div(at.m * plan.tok, plan.part) == e
+                holds = lax.div(at.m * plan.tok, plan.part) == e
                 to = lax.rem(at.m * plan.tok + plan.seq - e * plan.part, plan.seq)
                 to = pl.ds(pl.multiple_of(to, plan.tok), plan.tok)
                 yield here, True, q, e, j, 0, self.src.at[pl.ds(first + plan.own * e, plan.own)], self.dst.at[
@@ -208,8 +211,7 @@
     def arrived(self):
         plan = self.plan
         settle(self.dst.at[pl.ds(0, plan.own)], self.recv.at[0])
-        extent = plan.seq if self.whole_shared else plan.part
-        settle(self.dst.at[plan.own, pl.ds(0, extent)], self.recv.at[1])
+        settle(self.dst.at[plan.own, pl.ds(0, plan.part)], self.recv.at[1])
 
     def finish(self):
         for here, wanted, q, e, j, what, src, dst in self.copies():
@@ -251,16 +253,17 @@
     plan, heads, tok, cot, seg, bq, bu, w0, w1, w2, w3, gain_one, shift_one, out_bias, gain_two, shift_two,
     tok_o, cot3, seg_o, g0, g1, g2, g3, proj_o, attn_o, hid_o, two_o, act_o, der_o,
     tok_v, one_v, wq_v, proj_v, attn_v, wo_v, hid_v, two_v, wu_v, act_v, der_v, seg_v, columns, bq_v, bu_v,
-    tok_send, tok_recv, cot_send, cot_recv, seg_send, seg_recv, bias_send, bias_recv, load_sem, save_sem, act_sem, *sems,
+    tok_send, tok_recv, cot_send, cot_recv, seg_send, seg_recv, bias_send, bias_recv, part_send, part_recv, load_sem, save_sem, act_sem, *sems,
 ):
     n, share, own, part, seq = plan.mp, plan.share, plan.own, plan.part, plan.seq
     held = own * seq + part
     at = Place(plan)
     gat = Gatherer(plan, at, (w0, w1, w2, w3), (g0, g1, g2, g3), sems)
-    tokens = RowsIn(plan, at, tok, tok_v, tok_send, tok_recv, True)
-    cots = RowsIn(plan, at, cot, cot3, cot_send, cot_recv, False)
+    tokens = RowsIn(plan, at, tok, tok_v, tok_send, tok_recv)
+    cots = RowsIn(plan, at, cot, cot3, cot_send, cot_recv)
     hops = plan.hops
     greet(plan, at, False)
+    meet(plan, False)
 
     gat.begin(0)
     gat.begin(2)
@@ -288,6 +291,14 @@
             thunk()
     after[0][hops - 1]()
     tokens.arrived()
+    mine = tok_v.at[own, pl.ds(0, part)]
+    for e in range(1, share):
+        remote(
+            mine, tok_v.at[own, pl.ds((share - e) * part, part)], part_send.at[0], part_recv.at[0],
+            dp=at.base + lax.rem(at.k + e, share),
+        ).start()
+    others = tok_v.at[own, pl.ds(part, (share - 1) * part)]
+    settle(others, part_recv.at[0])
     save_tok = pltpu.make_async_copy(tok_v, tok_o, save_sem.at[0])
     save_tok.start()
     gain, shift = gain_one[...], shift_one[...]
@@ -323,6 +334,7 @@
         take(0)
         projected = jnp.dot(one_v[...], wq_v[s], preferred_element_type=F32) + bq_v[s]
         proj_v[s] = projected.astype(BF)
+        take(1)
 
         def attend(r, first, amount):
             allowed = same_image(seg_o, columns, r, amount)
@@ -336,11 +348,9 @@
                 mixed = lax.dot_general(probs, value, DOWN, preferred_element_type=F32)
                 attn_v[s, pl.ds(first, amount), h * HEAD_DIM : (h + 1) * HEAD_DIM] = mixed.astype(BF)
 
-        @pl.loop(0, own)
-        def _(r):
-            attend(r, pl.multiple_of(r * seq, seq), seq)
-
-        take(1)
+        for r in range(own):
+            attend(r, r * seq, seq)
+            take(2 + r)
         attend(own, own * seq, part)
 
     rest = []
@@ -351,9 +361,10 @@
     moves = []
     for at_once in itertools.zip_longest(*rest):
         moves += [thunks for thunks in at_once if thunks]
-    tables = ({}, {})
-    for j, thunks in spread_over(2 * n, moves).items():
-        tables[j % 2][j // 2] = [thunk for some in thunks for thunk in some]
+    points = 2 + own
+    tables = [{} for _ in range(points)]
+    for j, thunks in spread_over(points * n, moves).items():
+        tables[j % points][j // points] = [thunk for some in thunks for thunk in some]
     run(n, attend_shard, *tables)
     save_proj = pltpu.make_async_copy(proj_v, proj_o, save_sem.at[1])
     save_proj.start()
@@ -404,6 +415,7 @@
     for w in range(4):
         gat.finish(w)
     tokens.finish()
+    settle(others, part_send.at[0])
     cots.arrived()
     cots.finish()
     for src, dst, i in biases:
@@ -442,7 +454,7 @@
             pltpu.VMEM((plan.rows, plan.seq, 128), F32),
             *[pltpu.VMEM((n,) + b.shape, F32) for b in biases],
             dma((plan.groups, share, 2)), dma((2,)), dma((plan.groups, share, 2)), dma((2,)), dma((1,)), dma((1,)),
-            dma((2,)), dma((2,)), dma((1,)), dma((5,)), dma((2,)), *gatherer_sems(plan, 4),
+            dma((2,)), dma((2,)), dma((1,)), dma((1,)), dma((1,)), dma((5,)), dma((2,)), *gatherer_sems(plan, 4),
         ],
         compiler_params=pltpu.CompilerParams(
             collective_id=0, has_side_effects=True, vmem_limit_bytes=58 << 20
@@ -843,6 +855,8 @@
             sum_v[rows] = hid_v[rows] + down_bias[...]
             grad_v[rows] = jnp.zeros((part, width), F32)
 
+        meet(plan, True)
+
         def body(i, take):
             take(0)
             stream(loads, i)
@@ -959,11 +973,9 @@
                     three_v[keys, col + HEAD_DIM : col + 2 * HEAD_DIM] = key_grad.astype(BF)
                     three_v[keys, col + 2 * HEAD_DIM : col + 3 * HEAD_DIM] = value_grad.astype(BF)
 
-            @pl.loop(0, own)
-            def _(r):
-                attend(r, pl.multiple_of(r * seq, seq), seq)
-
-            take(1)
+            for r in range(own):
+                attend(r, r * seq, seq)
+                take(1 + r)
             attend(own, own * seq, part)
 
             @pl.when(i > 0)
@@ -998,13 +1010,12 @@
         for q in range(BLOCKS_MID, n):
             for what in range(2):
                 table.setdefault((q - BLOCKS_MID) * BLOCKS_OVER // n, []).append(part_of(blocks.start, what, q))
-        run(n, body, table, middle)
+        run(n, body, table, *[{}] * (own - 1), middle)
         red.given(2)
         first[2][count - 1]()
         step[2][count - 2]()
 
-        @pl.loop(0, plan.rows * share)
-        def _(b):
+        def norm_block(b):
             r, start = lax.div(b, share), pl.multiple_of(lax.rem(b, share) * part, part)
             rows = pl.ds(pl.multiple_of(b * part, part), part)
             unit, scale, _ = norm(tok_v[r, pl.ds(start, part)].astype(F32), gain_one[...], 0.0)
@@ -1021,6 +1032,8 @@
             @pl.when(b >= blocks_held)
             def _():
                 out3[r, pl.ds(start, part)] = grad.astype(BF)
+
+        pl.loop(own * share, plan.rows * share)(norm_block)
 
         tokens = RowsOut(plan, at, out3, tgo, tg, tg_send, tg_recv)
         for e in range(share):
@@ -1030,6 +1043,9 @@
             else:
                 to = at.base + lax.rem(at.k + e, share)
                 remote(src, tgs.at[share - e], tgs_send.at[e], tgs_recv.at[share - e], dp=to).start()
+
+        pl.loop(0, own * share)(norm_block)
+
         lines = [-(-size // 128) for size in (ff, three)]
         msg[...] = jnp.zeros(msg.shape, F32)
         for q in range(n):

time: 394 us -> 379 us (0.962)
  Pallas kernels: 375 us -> 360 us
    pallas_call x1, Pallas kernels: 210 us -> 199 us  [backward(): pl.pallas_call(functools.partial(backward_kernel, plan, heads), out_shape...]
    pallas_call x1, Pallas kernels: 166 us -> 161 us  [forward(): pl.pallas_call(functools.partial(forward_kernel, plan, heads), out_shape=...]
where the time goes in v6:
time: 379 us; the launch traced here: 376 us
  Pallas kernels  360 us (95%)
  local copies, waits for them, and re-layouts  12.1 us (3%)
    pallas_call x1, Pallas kernels, backward(): pl.pallas_call(functools.partial(backward_kernel, plan, heads), out_shape...  199 us
    pallas_call x1, Pallas kernels, forward(): pl.pallas_call(functools.partial(forward_kernel, plan, heads), out_shape=...  161 us
    unnamed x15, local copies, waits for them, and re-layouts  8.12 us

profile of v6, /device:TPU:11, one launch (start us, length us, event | category | flops | bytes accessed | tf_op | source)
XLA Modules:
  0.0 376.2 jit_solution(4996054006494121652)
XLA Ops:
  0.6 0.8 slice_reduce_fusion.3
  1.4 0.1 stack_squeeze.8
  1.5 0.1 stack_squeeze.9
  1.6 0.1 pad.3.clone
  1.7 0.1 pad_maximum_fusion
  1.7 0.6 reshape.85.bq
  2.4 160.9 %forward.1 = (bf16[3,256,1024]{2,1,0:T(8,128)(2,1)}, bf16[3,256,1024]{2,1,0:T(8,128)(2,1)}, s32[3,256]{1,0:T(4,128)}, bf16[8,1024,384]{2,1,0:T(8,128)(2,1)}, bf1...) custom-call(bf16[20,32,1024]{2,1,0:T(8,128)(2,1)} %tok.1, ...), custom_call_target="tpu_custom_call" | custom-call | tf_op jit(solution)/shard_map/forward/pallas_call | solution.py:445
  163.3 198.7 %backward.1 = (bf16[20,32,1024]{2,1,0:T(8,128)(2,1)}, bf16[20,32,1024]{2,1,0:T(8,128)(2,1)}, f32[512,1024]{1,0:T(8,128)}, f32[512,1024]{1,0:T(8,128)}, f32[384,1...) custom-call(bf16[8,1024,384]{2,1,0:T(8,128)(2,1)} %get-tuple-element.34.g0, ...), custom_call_target="tpu_custom_call" | custom-call | tf_op jit(solution)/shard_map/backward/pallas_call | solution.py:1121
  362.0 0.0 copy-start.1
  362.1 0.8 constant_dynamic-slice_fusion
  362.9 0.1 reshape_reshape.3
  363.0 0.1 stack.11
  363.1 0.1 stack.12
  363.2 0.6 pad_maximum_fusion.1
  363.7 3.1 convert_element_type.3
  366.9 0.0 copy-done.1
  366.9 1.8 copy.36
  368.7 3.1 copy.35
  371.8 0.6 fusion
  372.4 0.6 dynamic-slice_bitcast_fusion
  373.0 0.0 copy-done.2
  373.0 1.1 copy.40
  374.1 0.8 copy.41
  374.9 1.3 copy.42
  (10 shorter events, 0.0 us)
Async XLA Ops:
  362.0 4.8 %copy-start.1 = (f32[512,1024]{1,0:T(8,128)S(1)}, f32[512,1024]{1,0:T(8,128)}, u32[]{:S(2)}) copy-start(f32[512,1024]{1,0:T(8,128)} %get-tuple-element.52) | copy-start | bytes 6291460
  368.7 3.1 copy-start.4
  368.7 4.4 %copy-start.2 = (bf16[20,32,1024]{2,1,0:T(8,128)(2,1)S(1)}, bf16[20,32,1024]{2,1,0:T(8,128)(2,1)}, u32[]{:S(2)}) copy-start(bf16[20,32,1024]{2,1,0:T(8,128)(2,1)} %get-tuple-element.106) | copy-start | bytes 3932164
  371.8 3.1 copy-start
  372.4 1.6 copy-start.3

commit v7 on v6

--- a/solution.py
+++ b/solution.py
@@ -899,11 +899,17 @@
         first[1][count - 1]()
         step[1][count - 2]()
 
+        for r in range(plan.rows):
+            extent = seq if r < own else part
+            block_v[r, pl.ds(0, extent)] = sum_v[pl.ds(r * seq, extent)].astype(BF)
+        for q in range(n):
+            if q < BLOCKS_MID:
+                blocks.start(0, q)
+                blocks.start(1, q)
+
         @pl.loop(0, blocks_held)
         def _(b):
-            r, start = lax.div(b, share), pl.multiple_of(lax.rem(b, share) * part, part)
             rows = pl.ds(pl.multiple_of(b * part, part), part)
-            block_v[r, pl.ds(start, part)] = sum_v[rows].astype(BF)
             hidden, grad, cot_f = hid_v[rows], grad_v[rows], cot_v[rows].astype(F32)
             unit, scale, _ = norm(hidden, gain_two[...], 0.0)
             hidden_grad = cot_f + norm_back(unit, scale, gain_two[...], grad)
@@ -912,10 +918,6 @@
             for line, value in ((2, hidden_grad), (3, grad * unit), (4, grad), (5, cot_f)):
                 sums[pl.ds(line, 1)] += jnp.sum(value, axis=0, keepdims=True)
 
-        for q in range(n):
-            if q < BLOCKS_MID:
-                blocks.start(0, q)
-                blocks.start(1, q)
 
     pl.run_scoped(
         feed_forward,

time: 379 us -> 379 us (level)
  no operation moved by 1% of the time
where the time goes in v7:
time: 379 us; the launch traced here: 376 us
  Pallas kernels  360 us (95%)
  local copies, waits for them, and re-layouts  12.1 us (3%)
    pallas_call x1, Pallas kernels, backward(): pl.pallas_call(functools.partial(backward_kernel, plan, heads), out_shape...  199 us
    pallas_call x1, Pallas kernels, forward(): pl.pallas_call(functools.partial(forward_kernel, plan, heads), out_shape=...  161 us
    unnamed x15, local copies, waits for them, and re-layouts  8.12 us

profile of v7, /device:TPU:11, one launch (start us, length us, event | category | flops | bytes accessed | tf_op | source)
XLA Modules:
  0.0 376.2 jit_solution(9073862320701417464)
XLA Ops:
  0.6 0.8 slice_reduce_fusion.3
  1.4 0.1 stack_squeeze.8
  1.5 0.1 stack_squeeze.9
  1.6 0.1 pad.3.clone
  1.7 0.1 pad_maximum_fusion
  1.7 0.6 reshape.85.bq
  2.4 160.9 %forward.1 = (bf16[3,256,1024]{2,1,0:T(8,128)(2,1)}, bf16[3,256,1024]{2,1,0:T(8,128)(2,1)}, s32[3,256]{1,0:T(4,128)}, bf16[8,1024,384]{2,1,0:T(8,128)(2,1)}, bf1...) custom-call(bf16[20,32,1024]{2,1,0:T(8,128)(2,1)} %tok.1, ...), custom_call_target="tpu_custom_call" | custom-call | tf_op jit(solution)/shard_map/forward/pallas_call | solution.py:445
  163.3 198.7 %backward.1 = (bf16[20,32,1024]{2,1,0:T(8,128)(2,1)}, bf16[20,32,1024]{2,1,0:T(8,128)(2,1)}, f32[512,1024]{1,0:T(8,128)}, f32[512,1024]{1,0:T(8,128)}, f32[384,1...) custom-call(bf16[8,1024,384]{2,1,0:T(8,128)(2,1)} %get-tuple-element.34.g0, ...), custom_call_target="tpu_custom_call" | custom-call | tf_op jit(solution)/shard_map/backward/pallas_call | solution.py:1123
  362.0 0.0 copy-start.1
  362.1 0.8 constant_dynamic-slice_fusion
  362.9 0.1 reshape_reshape.3
  363.0 0.1 stack.11
  363.1 0.1 stack.12
  363.2 0.6 pad_maximum_fusion.1
  363.7 3.1 convert_element_type.3
  366.9 0.0 copy-done.1
  366.9 1.8 copy.36
  368.7 3.1 copy.35
  371.8 0.0 copy-done.4
  371.8 0.6 fusion
  372.4 0.6 dynamic-slice_bitcast_fusion
  373.0 1.1 copy.40
  374.1 0.8 copy.41
  374.9 1.3 copy.42
  (10 shorter events, 0.0 us)
Async XLA Ops:
  362.0 4.8 %copy-start.1 = (f32[512,1024]{1,0:T(8,128)S(1)}, f32[512,1024]{1,0:T(8,128)}, u32[]{:S(2)}) copy-start(f32[512,1024]{1,0:T(8,128)} %get-tuple-element.52) | copy-start | bytes 6291460
  368.7 3.1 copy-start.4
  368.7 4.4 %copy-start.2 = (bf16[20,32,1024]{2,1,0:T(8,128)(2,1)S(1)}, bf16[20,32,1024]{2,1,0:T(8,128)(2,1)}, u32[]{:S(2)}) copy-start(bf16[20,32,1024]{2,1,0:T(8,128)(2,1)} %get-tuple-element.106) | copy-start | bytes 3932164
  371.8 3.1 copy-start
  372.4 1.6 copy-start.3
